TPU v7x, 32 devices: a whole 2x2x4 slice. The times are simulated.
32 devices in a mesh: ctx: 8 (over y, x, core), head: 4 (over z).
Axes of the slice: x: 2, y: 2, z: 4, core: 2. Of those that a mesh axis runs over, the one named last changes fastest.
Arguments:
- query_noisy: bfloat16 [4096, 2048], P(('ctx', 'head')), may hold values from -7 to 7
- key_noisy: bfloat16 [4096, 2048], P(('ctx', 'head')), may hold values from -7 to 7
- value_noisy: bfloat16 [4096, 2048], P(('ctx', 'head')), may hold values from -48 to 48
- key_clean: bfloat16 [4096, 2048], P(('ctx', 'head')), may hold values from -6 to 6
- value_clean: bfloat16 [4096, 2048], P(('ctx', 'head')), may hold values from -48 to 48
- grad_output: bfloat16 [4096, 2048], P(('ctx', 'head')), may hold values from -192 to 192
- block_list: int32 [16, 4], replicated, may hold values from -1 to 14, as said below
Outputs:
- attended: bfloat16 [4096, 2048], P(('ctx', 'head'))
- query_grad: bfloat16 [4096, 2048], P(('ctx', 'head'))
- noisykey_grad: bfloat16 [4096, 2048], P(('ctx', 'head'))
- noisyvalue_grad: bfloat16 [4096, 2048], P(('ctx', 'head'))
- cleankey_grad: bfloat16 [4096, 2048], P(('ctx', 'head'))
- cleanvalue_grad: bfloat16 [4096, 2048], P(('ctx', 'head'))
Inputs may be any that keep to these rules, and one draw needn't show every extreme that they name: `block_list`: each entry of row b is -1 or a block before b. The 8 entries in the rows of one index of ctx name blocks of any one index of ctx at most 1 times, and that most is reached in every draw. The first entry of the first row of every index of ctx after the first names a block of index 0. The last entry of each index's last row names that index's block 0.
All inputs are finite; a program needn't handle non-finite values.
Results may differ from a plain program's by a relative error of at most 0.03.
Values may be sent and summed in bfloat16 or wider, within the bound.
No kernel may reach another device: no remote copies, remote signals or barrier semaphores. Data moves between devices by JAX's collectives and lax.ppermute only.
A program may use at most 128 MiB of HBM per device.

v0:
```python
import functools
import math

import jax
import jax.numpy as jnp
from jax import lax
from jax.experimental import pallas as pl
from jax.experimental.pallas import tpu as pltpu
from jax.sharding import PartitionSpec as P

HD = 128
BLK = 256
SEL = 4
CHUNKS = 2

MASKED = -1e30
BF = jnp.bfloat16
F32 = jnp.float32


HBM = pl.BlockSpec(memory_space=pl.ANY)
SMEM = pl.BlockSpec(memory_space=pltpu.SMEM)


def cost(nbytes, flops=0, trans=0):
    return pl.CostEstimate(flops=flops, bytes_accessed=nbytes, transcendentals=trans)


def swap(x, axis, mask):
    count = lax.axis_size(axis)
    return lax.ppermute(x, axis, [(i, i ^ mask) for i in range(count)])


class Plan:
    def __init__(self, rows, features, blocks, chunks):
        self.ctx = lax.axis_size("ctx")
        self.n = lax.axis_size("head")
        self.rows = rows
        self.features = features
        self.bh = blocks // self.ctx
        self.per = self.n // self.bh
        self.group = features // self.n
        self.heads = self.group // HD
        self.chunks = min(chunks, self.heads)
        self.width = self.group // self.chunks
        self.tile = (2, self.per, rows, self.width)
        self.tile_bytes = 2 * BLK * self.width * 2

    def cols(self, z, mask, chunk):
        start = (z ^ mask) * self.group + chunk * self.width
        return pl.ds(pl.multiple_of(start, HD), self.width)


def run_all(copies):
    for c in copies:
        c.start()
    return copies


def wait_all(copies):
    for c in copies:
        c.wait()


def pack(plan, arrays, chunk):
    k, n = len(arrays), plan.n

    def body(*refs):
        ins, outs = refs[:k], refs[k : k + n - 1]
        buf, sem_in, sem_out = refs[k + n - 1 :]
        z = lax.axis_index("head")
        loads = [
            run_all(
                [
                    pltpu.make_async_copy(
                        ins[i].at[:, plan.cols(z, m, chunk)],
                        buf.at[m - 1, i],
                        sem_in.at[m - 1, i],
                    )
                    for i in range(k)
                ]
            )
            for m in range(1, n)
        ]
        stores = []
        for m in range(1, n):
            wait_all(loads[m - 1])
            stores += run_all(
                [pltpu.make_async_copy(buf.at[m - 1], outs[m - 1], sem_out.at[m - 1])]
            )
        wait_all(stores)

    shape = (k, plan.rows, plan.width)
    return pl.pallas_call(
        body,
        out_shape=[jax.ShapeDtypeStruct(shape, BF)] * (n - 1),
        in_specs=[HBM] * k,
        out_specs=[HBM] * (n - 1),
        scratch_shapes=[
            pltpu.VMEM((n - 1,) + shape, BF),
            pltpu.SemaphoreType.DMA((n - 1, k)),
            pltpu.SemaphoreType.DMA((n - 1,)),
        ],
        cost_estimate=cost(2 * k * (n - 1) * plan.rows * plan.width * 2),
        name="pack",
    )(*arrays)


def unpack(plan, pieces, k):
    n, chunks = plan.n, plan.chunks
    flat = [p for chunk in pieces for p in chunk]

    def body(*refs):
        ins, outs = refs[: n * chunks], refs[n * chunks : n * chunks + k]
        buf, sem_in, sem_out = refs[n * chunks + k :]
        z = lax.axis_index("head")
        loads = []
        for c in range(chunks):
            for m in range(n):
                at = c * n + m
                loads.append(
                    pltpu.make_async_copy(
                        ins[at], buf.at[:, :, plan.cols(z, m, c)], sem_in.at[at]
                    )
                )
        run_all(loads)
        wait_all(loads)
        wait_all(
            run_all([pltpu.make_async_copy(buf.at[i], outs[i], sem_out.at[i]) for i in range(k)])
        )

    shape = (plan.rows, plan.features)
    return pl.pallas_call(
        body,
        out_shape=[jax.ShapeDtypeStruct(shape, BF)] * k,
        in_specs=[HBM] * len(flat),
        out_specs=[HBM] * k,
        scratch_shapes=[
            pltpu.VMEM((k,) + shape, BF),
            pltpu.SemaphoreType.DMA((len(flat),)),
            pltpu.SemaphoreType.DMA((k,)),
        ],
        cost_estimate=cost(2 * k * plan.rows * plan.features * 2),
        name="unpack",
    )(*flat)


def wanted(plan, lists, reader, owner, z):
    live, which = jnp.int32(0), jnp.int32(0)
    for e in range(plan.bh * SEL):
        entry = lists[reader * plan.bh + e // SEL, e % SEL]
        hit = (entry >= 0) & (lax.div(entry, jnp.int32(plan.bh)) == owner)
        local = lax.rem(entry, jnp.int32(plan.bh)) ^ lax.div(z, jnp.int32(plan.per))
        live = jnp.where(hit, 1, live)
        which = jnp.where(hit, local, which)
    return live, which


def select(plan, kclean, vclean, got, lists, chunk):
    n, per, slots = plan.n, plan.per, plan.ctx

    def body(*refs):
        lists_ref, k_ref, v_ref = refs[:3]
        ins, outs = refs[3 : 2 + n], refs[2 + n : 2 + n + slots]
        buf, sem_own, sem_in, sem_out = refs[2 + n + slots :]
        me, z = lax.axis_index("ctx"), lax.axis_index("head")
        own = plan.cols(z, 0, chunk)
        loads = [
            pltpu.make_async_copy(k_ref.at[:, own], buf.at[0, 0, 0], sem_own.at[0]),
            pltpu.make_async_copy(v_ref.at[:, own], buf.at[0, 1, 0], sem_own.at[1]),
        ]
        for m in range(1, n):
            loads.append(
                pltpu.make_async_copy(
                    ins[m - 1], buf.at[m // per, :, m % per], sem_in.at[m - 1]
                )
            )
        run_all(loads)
        choice = [wanted(plan, lists_ref, me ^ s, me, z)[1] for s in range(slots)]
        wait_all(loads)
        wait_all(
            run_all(
                [
                    pltpu.make_async_copy(buf.at[choice[s]], outs[s], sem_out.at[s])
                    for s in range(slots)
                ]
            )
        )

    return pl.pallas_call(
        body,
        out_shape=[jax.ShapeDtypeStruct(plan.tile, BF)] * slots,
        in_specs=[SMEM] + [HBM] * (n + 1),
        out_specs=[HBM] * slots,
        scratch_shapes=[
            pltpu.VMEM((plan.bh,) + plan.tile, BF),
            pltpu.SemaphoreType.DMA((2,)),
            pltpu.SemaphoreType.DMA((n - 1,)),
            pltpu.SemaphoreType.DMA((slots,)),
        ],
        cost_estimate=cost((slots + plan.bh) * plan.tile_bytes),
        name="select",
    )(lists, kclean, vclean, *got)


def dot(a, b, ca, cb):
    return lax.dot_general(a, b, (((ca,), (cb,)), ((), ())), preferred_element_type=F32)


def attend(plan, noisy, got, tiles, lists, chunk):
    n, per, slots, rows, bh = plan.n, plan.per, plan.ctx, plan.rows, plan.bh
    heads = plan.width // HD
    scale = 1.0 / math.sqrt(HD)
    log2e = 1.0 / math.log(2.0)
    side = (4, rows, plan.width)

    def body(*refs):
        at = 0

        def take(count):
            nonlocal at
            at += count
            return refs[at - count : at]

        (lists_ref,) = take(1)
        own_refs = take(4)
        got_refs = take(n - 1)
        tile_refs = take(slots)
        side_refs = take(n)
        term_refs = take(slots)
        rows_in, tiles_in, rows_out, terms_out, sem_own, sem_got, sem_tile, sem_side, sem_term = (
            refs[at:]
        )
        me, z = lax.axis_index("ctx"), lax.axis_index("head")
        home = lax.div(z, jnp.int32(per))
        own = plan.cols(z, 0, chunk)
        loads = [
            pltpu.make_async_copy(own_refs[i].at[:, own], rows_in.at[i, 0, 0], sem_own.at[i])
            for i in range(4)
        ]
        loads += [
            pltpu.make_async_copy(
                got_refs[m - 1], rows_in.at[:, m // per, m % per], sem_got.at[m - 1]
            )
            for m in range(1, n)
        ]
        loads += [
            pltpu.make_async_copy(tile_refs[s], tiles_in.at[s], sem_tile.at[s])
            for s in range(slots)
        ]
        run_all(loads)
        wait_all(loads)

        def step(i, carry):
            h, b = lax.div(i, jnp.int32(bh)), lax.rem(i, jnp.int32(bh))
            cols = pl.ds(pl.multiple_of(h * HD, HD), HD)

            def block(ref, *index):
                return ref[(*index, slice(None), slice(None), cols)].reshape(BLK, HD)

            def put(ref, value, *index):
                ref[(*index, slice(None), slice(None), cols)] = value.astype(BF).reshape(
                    per, rows, HD
                )

            q, k0, v0, g = (block(rows_in, j, b) for j in range(4))
            row = me * bh + (b ^ home)
            keys, values, bias, target = [k0], [v0], [None], []
            for s in range(SEL):
                entry = lists_ref[row, s]
                live = entry >= 0
                slot = jnp.where(live, lax.div(entry, jnp.int32(bh)) ^ me, 0)
                keys.append(block(tiles_in, slot, 0))
                values.append(block(tiles_in, slot, 1))
                bias.append(jnp.where(live, 0.0, MASKED).astype(F32))
                target.append(jnp.where(live, slot, slots))
            scores = []
            for kt, extra in zip(keys, bias):
                s = dot(kt, q, 1, 1) * (scale * log2e)
                scores.append(s if extra is None else s + extra)
            top = functools.reduce(
                jnp.maximum, [jnp.max(s, axis=0, keepdims=True) for s in scores]
            )
            weights = [jnp.exp2(s - top) for s in scores]
            total = functools.reduce(
                jnp.add, [jnp.sum(w, axis=0, keepdims=True) for w in weights]
            )
            inverse = 1.0 / total
            probs = [w * inverse for w in weights]
            probs_bf = [p.astype(BF) for p in probs]
            out_t = functools.reduce(
                jnp.add, [dot(vt.T, p, 1, 0) for vt, p in zip(values, probs_bf)]
            )
            out_bf = out_t.astype(BF)
            put(rows_out, out_bf.T, 0, b)
            delta = jnp.sum(g.T.astype(F32) * out_bf.astype(F32), axis=0, keepdims=True)
            dq_t = jnp.zeros((HD, BLK), F32)
            for t in range(1 + SEL):
                ds = (probs[t] * (dot(values[t], g, 1, 1) - delta)).astype(BF)
                dq_t = dq_t + dot(keys[t].T, ds, 1, 0)
                kterm = dot(ds, q, 1, 0) * scale
                vterm = dot(probs_bf[t], g, 1, 0)
                if t == 0:
                    put(rows_out, kterm, 2, b)
                    put(rows_out, vterm, 3, b)
                else:
                    put(terms_out, kterm, target[t - 1], 0)
                    put(terms_out, vterm, target[t - 1], 1)
            put(rows_out, (dq_t * scale).astype(BF).T, 1, b)
            return carry

        lax.fori_loop(0, heads * bh, step, 0)
        stores = [
            pltpu.make_async_copy(terms_out.at[s], term_refs[s], sem_term.at[s])
            for s in range(slots)
        ]
        stores += [
            pltpu.make_async_copy(rows_out.at[:, m // per, m % per], side_refs[m], sem_side.at[m])
            for m in range(n)
        ]
        run_all(stores)
        wait_all(stores)

    flops = heads * bh * 6 * 2 * BLK * (1 + SEL) * BLK * HD
    result = pl.pallas_call(
        body,
        out_shape=[jax.ShapeDtypeStruct(side, BF)] * n
        + [jax.ShapeDtypeStruct(plan.tile, BF)] * slots,
        in_specs=[SMEM] + [HBM] * (4 + n - 1 + slots),
        out_specs=[HBM] * (n + slots),
        scratch_shapes=[
            pltpu.VMEM((4, bh, per, rows, plan.width), BF),
            pltpu.VMEM((slots,) + plan.tile, BF),
            pltpu.VMEM((4, bh, per, rows, plan.width), BF),
            pltpu.VMEM((slots + 1,) + plan.tile, BF),
            pltpu.SemaphoreType.DMA((4,)),
            pltpu.SemaphoreType.DMA((n - 1,)),
            pltpu.SemaphoreType.DMA((slots,)),
            pltpu.SemaphoreType.DMA((n,)),
            pltpu.SemaphoreType.DMA((slots,)),
        ],
        compiler_params=pltpu.CompilerParams(vmem_limit_bytes=48 * 1024 * 1024),
        cost_estimate=cost(
            2 * (slots * plan.tile_bytes + 4 * bh * BLK * plan.width * 2),
            flops,
            heads * bh * BLK * (1 + SEL) * BLK,
        ),
        name="attend",
    )(lists, *noisy, *got, *tiles)
    return result[:n], result[n:]


def total_terms(plan, terms, lists):
    n, per, slots, rows, bh = plan.n, plan.per, plan.ctx, plan.rows, plan.bh

    def body(*refs):
        lists_ref, ins, outs = refs[0], refs[1 : 1 + slots], refs[1 + slots : 1 + slots + n]
        buf, summed, sem_in, sem_out = refs[1 + slots + n :]
        me, z = lax.axis_index("ctx"), lax.axis_index("head")
        loads = run_all(
            [pltpu.make_async_copy(ins[s], buf.at[s], sem_in.at[s]) for s in range(slots)]
        )
        asked = [wanted(plan, lists_ref, me ^ s, me, z) for s in range(slots)]
        wait_all(loads)
        stripe = math.gcd(rows, 32)

        def step(i, carry):
            at = pl.ds(pl.multiple_of(i * stripe, stripe), stripe)
            for kv in range(2):
                for p in range(per):
                    parts = [buf[s, kv, p, at, :].astype(F32) for s in range(slots)]
                    for j in range(bh):
                        acc = jnp.zeros((stripe, plan.width), F32)
                        for (live, which), part in zip(asked, parts):
                            acc = acc + jnp.where((live > 0) & (which == j), part, 0.0)
                        summed[j, kv, p, at, :] = acc.astype(BF)
            return carry

        lax.fori_loop(0, rows // stripe, step, 0)
        wait_all(
            run_all(
                [
                    pltpu.make_async_copy(summed.at[m // per, :, m % per], outs[m], sem_out.at[m])
                    for m in range(n)
                ]
            )
        )

    shape = (2, rows, plan.width)
    return pl.pallas_call(
        body,
        out_shape=[jax.ShapeDtypeStruct(shape, BF)] * n,
        in_specs=[SMEM] + [HBM] * slots,
        out_specs=[HBM] * n,
        scratch_shapes=[
            pltpu.VMEM((slots,) + plan.tile, BF),
            pltpu.VMEM((bh,) + plan.tile, BF),
            pltpu.SemaphoreType.DMA((slots,)),
            pltpu.SemaphoreType.DMA((n,)),
        ],
        cost_estimate=cost((slots + bh) * plan.tile_bytes),
        name="total_terms",
    )(lists, *terms)


def slot_order(slots):
    return sorted(range(1, slots), key=lambda s: (-bin(s >> 1).count("1"), s >> 1 == 0, s))


def over_head(parts):
    got = {}
    for m in range(len(parts), 0, -1):
        got[m] = swap(parts[m - 1], "head", m)
    return [got[m] for m in range(1, len(parts) + 1)]


def over_ctx(parts):
    got = {}
    for s in slot_order(len(parts)):
        got[s] = swap(parts[s], "ctx", s)
    return [parts[0]] + [got[s] for s in range(1, len(parts))]


def shards(query, key, value, kclean, vclean, grad, lists):
    plan = Plan(query.shape[0], query.shape[1], lists.shape[0], CHUNKS)
    noisy = (query, key, value, grad)
    chunks = range(plan.chunks)
    got_clean = [over_head(pack(plan, (kclean, vclean), c)) for c in chunks]
    got_noisy = [over_head(pack(plan, noisy, c)) for c in chunks]
    tiles = [over_ctx(select(plan, kclean, vclean, got_clean[c], lists, c)) for c in chunks]
    sides, cleans = [], []
    for c in chunks:
        side, terms = attend(plan, noisy, got_noisy[c], tiles[c], lists, c)
        sides.append([side[0]] + over_head(side[1:]))
        terms = over_ctx(terms)
        clean = total_terms(plan, terms, lists)
        cleans.append([clean[0]] + over_head(clean[1:]))
    return (*unpack(plan, sides, 4), *unpack(plan, cleans, 2))


def solution(mesh):
    rows = P(("ctx", "head"), None)
    return jax.shard_map(
        shards,
        mesh=mesh,
        in_specs=(rows,) * 6 + (P(),),
        out_specs=(rows,) * 6,
        check_vma=False,
    )
```

profile of v0, /device:TPU:0, one launch (start us, length us, event | category | flops | bytes accessed | tf_op | source)
XLA Modules:
  0.0 233.8 jit_solution(1879321174737826938)
XLA Ops:
  2.4 3.1 %collective-permute-start.3 = (bf16[2,128,256]{2,1,0:T(8,128)(2,1)}, bf16[2,128,256]{2,1,0:T(8,128)(2,1)S(1)}, u32[]{:S(2)}, u32[]{:S(2)}) collective-permute-start(bf16[2,128,256]{2,1,0:T(8,128)(2,1)} %get-tuple-element.75), channel_id=1, source_target_pairs={{0,1},{1,0},{2,3},{3,2},{4,5},{5,4},{6,7},{7,6},{8,9},{9,8},{10,11... | collective-permute-start | bytes 393224 | tf_op jit(solution)/shard_map/ppermute | solution.py:31
  5.5 2.6 %collective-permute-start.4 = (bf16[2,128,256]{2,1,0:T(8,128)(2,1)}, bf16[2,128,256]{2,1,0:T(8,128)(2,1)S(1)}, u32[]{:S(2)}, u32[]{:S(2)}) collective-permute-start(bf16[2,128,256]{2,1,0:T(8,128)(2,1)} %get-tuple-element.76), channel_id=1, source_target_pairs={{0,2},{1,3},{2,0},{3,1},{4,6},{5,7},{6,4},{7,5},{8,10},{9,11},{10,... | collective-permute-start | bytes 393224 | tf_op jit(solution)/shard_map/ppermute | solution.py:31
  10.8 3.5 %collective-permute-start.20 = (bf16[2,128,256]{2,1,0:T(8,128)(2,1)}, bf16[2,128,256]{2,1,0:T(8,128)(2,1)S(1)}, u32[]{:S(2)}, u32[]{:S(2)}) collective-permute-start(bf16[2,128,256]{2,1,0:T(8,128)(2,1)} %get-tuple-element.94), channel_id=1, source_target_pairs={{0,2},{1,3},{2,0},{3,1},{4,6},{5,7},{6,4},{7,5},{8,10},{9,11},{10,... | collective-permute-start | bytes 393224 | tf_op jit(solution)/shard_map/ppermute | solution.py:31
  14.6 2.0 pack.4
  16.6 2.0 collective-permute-done.4.refs_4_
  18.6 2.1 pack.6
  20.7 7.7 %collective-permute-start.1 = (bf16[4,128,256]{2,1,0:T(8,128)(2,1)S(1)}, bf16[4,128,256]{2,1,0:T(8,128)(2,1)S(1)}, u32[]{:S(2)}, u32[]{:S(2)}) collective-permute-start(bf16[4,128,256]{2,1,0:T(8,128)(2,1)S(1)} %copy-done.38), channel_id=1, source_target_pairs={{0,2},{1,3},{2,0},{3,1},{4,6},{5,7},{6,4},{7,5},{8,10},{9,11},{10,... | collective-permute-start | bytes 786440 | tf_op jit(solution)/shard_map/ppermute | solution.py:31
  30.1 15.2 %collective-permute-start.17 = (bf16[4,128,256]{2,1,0:T(8,128)(2,1)}, bf16[4,128,256]{2,1,0:T(8,128)(2,1)S(1)}, u32[]{:S(2)}, u32[]{:S(2)}) collective-permute-start(bf16[4,128,256]{2,1,0:T(8,128)(2,1)} %get-tuple-element.91), channel_id=1, source_target_pairs={{0,2},{1,3},{2,0},{3,1},{4,6},{5,7},{6,4},{7,5},{8,10},{9,11},{10,... | collective-permute-start | bytes 786440 | tf_op jit(solution)/shard_map/ppermute | solution.py:31
  47.5 3.6 %select.3 = (bf16[2,2,128,256]{3,2,1,0:T(8,128)(2,1)}, bf16[2,2,128,256]{3,2,1,0:T(8,128)(2,1)}, bf16[2,2,128,256]{3,2,1,0:T(8,128)(2,1)}, bf16[2,2,128,256]{3,2...) custom-call(s32[16,4]{1,0:T(8,128)} %copy.14.refs_0_, ...), custom_call_target="tpu_custom_call" | custom-call | bytes 2621440 | tf_op jit(solution)/shard_map/select/pallas_call | solution.py:190
  51.1 9.6 %collective-permute-done.1.refs_6_ = bf16[4,128,256]{2,1,0:T(8,128)(2,1)S(1)} collective-permute-done((bf16[4,128,256]{2,1,0:T(8,128)(2,1)S(1)}, bf16[4,128,256]{2,1,0:T(8,128)(2,1)S(1)}, u32[]{:S(2)}, u32[]{:S(2)}) %collective-permute-start.1) | collective-permute-done | bytes 262176 | tf_op jit(solution)/shard_map/ppermute | solution.py:31
  62.6 9.4 %collective-permute-done.17.refs_6_ = bf16[4,128,256]{2,1,0:T(8,128)(2,1)S(1)} collective-permute-done((bf16[4,128,256]{2,1,0:T(8,128)(2,1)}, bf16[4,128,256]{2,1,0:T(8,128)(2,1)S(1)}, u32[]{:S(2)}, u32[]{:S(2)}) %collective-permute-start.17) | collective-permute-done | bytes 262176 | tf_op jit(solution)/shard_map/ppermute | solution.py:31
  73.5 3.7 %select.2 = (bf16[2,2,128,256]{3,2,1,0:T(8,128)(2,1)}, bf16[2,2,128,256]{3,2,1,0:T(8,128)(2,1)}, bf16[2,2,128,256]{3,2,1,0:T(8,128)(2,1)}, bf16[2,2,128,256]{3,2...) custom-call(s32[16,4]{1,0:T(8,128)} %copy.14.refs_0_, ...), custom_call_target="tpu_custom_call" | custom-call | bytes 2621440 | tf_op jit(solution)/shard_map/select/pallas_call | solution.py:190
  80.4 11.3 %collective-permute-done.25.refs_12_ = bf16[2,2,128,256]{3,2,1,0:T(8,128)(2,1)S(1)} collective-permute-done((bf16[2,2,128,256]{3,2,1,0:T(8,128)(2,1)}, bf16[2,2,128,256]{3,2,1,0:T(8,128)(2,1)S(1)}, u32[]{:S(2)}, u32[]{:S(2)}) %collective-permute-start.25) | collective-permute-done | bytes 262176 | tf_op jit(solution)/shard_map/ppermute | solution.py:31
  94.5 1.8 collective-permute-start.8
  100.7 10.3 %attend.3 = (bf16[4,128,256]{2,1,0:T(8,128)(2,1)S(1)}, bf16[4,128,256]{2,1,0:T(8,128)(2,1)S(1)}, bf16[4,128,256]{2,1,0:T(8,128)(2,1)S(1)}, bf16[4,128,256]{2,1,0...) custom-call(s32[16,4]{1,0:T(8,128)S(1)} %copy-done.4, ...), custom_call_target="tpu_custom_call" | custom-call | flops 2013265920 | bytes 6291456 | tf_op jit(solution)/shard_map/attend/pallas_call | solution.py:325
  112.5 3.2 %collective-permute-start.29 = (bf16[4,128,256]{2,1,0:T(8,128)(2,1)S(1)}, bf16[4,128,256]{2,1,0:T(8,128)(2,1)S(1)}, u32[]{:S(2)}, u32[]{:S(2)}) collective-permute-start(bf16[4,128,256]{2,1,0:T(8,128)(2,1)S(1)} %get-tuple-element.105), channel_id=1, source_target_pairs={{0,1},{1,0},{2,3},{3,2},{4,5},{5,4},{6,7},{7,6},{8,9},{9,8},{10,11... | collective-permute-start | bytes 786440 | tf_op jit(solution)/shard_map/ppermute | solution.py:31
  116.8 3.4 %collective-permute-done.10.refs_13_ = bf16[2,2,128,256]{3,2,1,0:T(8,128)(2,1)S(1)} collective-permute-done((bf16[2,2,128,256]{3,2,1,0:T(8,128)(2,1)}, bf16[2,2,128,256]{3,2,1,0:T(8,128)(2,1)S(1)}, u32[]{:S(2)}, u32[]{:S(2)}) %collective-permute-start.10) | collective-permute-done | bytes 262176 | tf_op jit(solution)/shard_map/ppermute | solution.py:31
  122.9 4.0 %collective-permute-done.29.refs_5_ = bf16[4,128,256]{2,1,0:T(8,128)(2,1)S(1)} collective-permute-done((bf16[4,128,256]{2,1,0:T(8,128)(2,1)S(1)}, bf16[4,128,256]{2,1,0:T(8,128)(2,1)S(1)}, u32[]{:S(2)}, u32[]{:S(2)}) %collective-permute-start.29) | collective-permute-done | bytes 262176 | tf_op jit(solution)/shard_map/ppermute | solution.py:31
  128.0 10.3 %attend.2 = (bf16[4,128,256]{2,1,0:T(8,128)(2,1)S(1)}, bf16[4,128,256]{2,1,0:T(8,128)(2,1)S(1)}, bf16[4,128,256]{2,1,0:T(8,128)(2,1)S(1)}, bf16[4,128,256]{2,1,0...) custom-call(s32[16,4]{1,0:T(8,128)S(1)} %copy-done.4, ...), custom_call_target="tpu_custom_call" | custom-call | flops 2013265920 | bytes 6291456 | tf_op jit(solution)/shard_map/attend/pallas_call | solution.py:325
  145.0 14.1 %collective-permute-done.46.refs_6_ = bf16[2,2,128,256]{3,2,1,0:T(8,128)(2,1)S(1)} collective-permute-done((bf16[2,2,128,256]{3,2,1,0:T(8,128)(2,1)S(1)}, bf16[2,2,128,256]{3,2,1,0:T(8,128)(2,1)S(1)}, u32[]{:S(2)}, u32[]{:S(2)}) %collective-permute-start.46) | collective-permute-done | bytes 262176 | tf_op jit(solution)/shard_map/ppermute | solution.py:31
  164.8 2.3 collective-permute-done.34.refs_4_
  168.5 12.2 %collective-permute-done.35.refs_5_ = bf16[2,2,128,256]{3,2,1,0:T(8,128)(2,1)S(1)} collective-permute-done((bf16[2,2,128,256]{3,2,1,0:T(8,128)(2,1)S(1)}, bf16[2,2,128,256]{3,2,1,0:T(8,128)(2,1)S(1)}, u32[]{:S(2)}, u32[]{:S(2)}) %collective-permute-start.35) | collective-permute-done | bytes 262176 | tf_op jit(solution)/shard_map/ppermute | solution.py:31
  180.8 4.6 %collective-permute-done.36.refs_6_ = bf16[2,2,128,256]{3,2,1,0:T(8,128)(2,1)S(1)} collective-permute-done((bf16[2,2,128,256]{3,2,1,0:T(8,128)(2,1)S(1)}, bf16[2,2,128,256]{3,2,1,0:T(8,128)(2,1)S(1)}, u32[]{:S(2)}, u32[]{:S(2)}) %collective-permute-start.36) | collective-permute-done | bytes 262176 | tf_op jit(solution)/shard_map/ppermute | solution.py:31
  185.4 1.9 collective-permute-start.15
  187.3 3.9 %total_terms.3 = (bf16[2,128,256]{2,1,0:T(8,128)(2,1)}, bf16[2,128,256]{2,1,0:T(8,128)(2,1)}, bf16[2,128,256]{2,1,0:T(8,128)(2,1)}, bf16[2,128,256]{2,1,0:T(8,128)(2,1)}) custom-call(s32[16,4]{1,0:T(8,128)} %copy.14.refs_0_, bf16[2,2,128,256]{3,2,1,0:T(8,128)(2,1)} %copy-done.2, bf16[2,2,128,256]{3,2,1,0:T(8,128)(2,1)} %copy-done.9, ...), custom_call_target="tpu_custom_call" | custom-call | bytes 2621440 | tf_op jit(solution)/shard_map/total_terms/pallas_call | solution.py:390
  193.0 4.0 %total_terms.2 = (bf16[2,128,256]{2,1,0:T(8,128)(2,1)}, bf16[2,128,256]{2,1,0:T(8,128)(2,1)}, bf16[2,128,256]{2,1,0:T(8,128)(2,1)}, bf16[2,128,256]{2,1,0:T(8,128)(2,1)}) custom-call(s32[16,4]{1,0:T(8,128)} %copy.14.refs_0_, bf16[2,2,128,256]{3,2,1,0:T(8,128)(2,1)} %copy-done.3, bf16[2,2,128,256]{3,2,1,0:T(8,128)(2,1)} %copy-done.15, ...), custom_call_target="tpu_custom_call" | custom-call | bytes 2621440 | tf_op jit(solution)/shard_map/total_terms/pallas_call | solution.py:390
  198.1 1.8 collective-permute-start.51
  199.9 11.3 %collective-permute-done.14.refs_2_ = bf16[4,128,256]{2,1,0:T(8,128)(2,1)} collective-permute-done((bf16[4,128,256]{2,1,0:T(8,128)(2,1)S(1)}, bf16[4,128,256]{2,1,0:T(8,128)(2,1)}, u32[]{:S(2)}, u32[]{:S(2)}) %collective-permute-start.14) | collective-permute-done | bytes 262176 | tf_op jit(solution)/shard_map/ppermute | solution.py:31
  211.2 6.9 %collective-permute-start.40 = (bf16[2,128,256]{2,1,0:T(8,128)(2,1)}, bf16[2,128,256]{2,1,0:T(8,128)(2,1)S(1)}, u32[]{:S(2)}, u32[]{:S(2)}) collective-permute-start(bf16[2,128,256]{2,1,0:T(8,128)(2,1)} %get-tuple-element.122), channel_id=1, source_target_pairs={{0,2},{1,3},{2,0},{3,1},{4,6},{5,7},{6,4},{7,5},{8,10},{9,11},{10,... | collective-permute-start | bytes 393224 | tf_op jit(solution)/shard_map/ppermute | solution.py:31
  219.7 2.9 %unpack.2 = (bf16[128,2048]{1,0:T(8,128)(2,1)}, bf16[128,2048]{1,0:T(8,128)(2,1)}, bf16[128,2048]{1,0:T(8,128)(2,1)}, bf16[128,2048]{1,0:T(8,128)(2,1)}) custom-call(bf16[4,128,256]{2,1,0:T(8,128)(2,1)} %copy-done.1, bf16[4,128,256]{2,1,0:T(8,128)(2,1)} %collective-permute-done.13.refs_1_, bf16[4,128,256]{2,1,0:T(8,128)(2,1)} %collective-permute-done.14.refs_2_, ...), custom_call_target="tpu_custom_call" | custom-call | bytes 4194304 | tf_op jit(solution)/shard_map/unpack/pallas_call | solution.py:133
  222.7 8.1 %collective-permute-done.40.refs_2_ = bf16[2,128,256]{2,1,0:T(8,128)(2,1)S(1)} collective-permute-done((bf16[2,128,256]{2,1,0:T(8,128)(2,1)}, bf16[2,128,256]{2,1,0:T(8,128)(2,1)S(1)}, u32[]{:S(2)}, u32[]{:S(2)}) %collective-permute-start.40) | collective-permute-done | bytes 131104 | tf_op jit(solution)/shard_map/ppermute | solution.py:31
  231.5 2.3 unpack.3
  (167 shorter events, 47.6 us)
Async XLA Ops:
  10.8 19.2 %collective-permute-start.20 = (bf16[2,128,256]{2,1,0:T(8,128)(2,1)}, bf16[2,128,256]{2,1,0:T(8,128)(2,1)S(1)}, u32[]{:S(2)}, u32[]{:S(2)}) collective-permute-start(bf16[2,128,256]{2,1,0:T(8,128)(2,1)} %get-tuple-element.94), channel_id=1, source_target_pairs={{0,2},{1,3},{2,0},{3,1},{4,6},{5,7},{6,4},{7,5},{8,10},{9,11},{10,... | collective-permute-start | bytes 393224 | tf_op jit(solution)/shard_map/ppermute | solution.py:31
  18.6 26.7 %collective-permute-start = (bf16[4,128,256]{2,1,0:T(8,128)(2,1)}, bf16[4,128,256]{2,1,0:T(8,128)(2,1)S(1)}, u32[]{:S(2)}, u32[]{:S(2)}) collective-permute-start(bf16[4,128,256]{2,1,0:T(8,128)(2,1)} %get-tuple-element.72), channel_id=1, source_target_pairs={{0,1},{1,0},{2,3},{3,2},{4,5},{5,4},{6,7},{7,6},{8,9},{9,8},{10,11... | collective-permute-start | bytes 786440 | tf_op jit(solution)/shard_map/ppermute | solution.py:31
  20.7 40.0 %collective-permute-start.1 = (bf16[4,128,256]{2,1,0:T(8,128)(2,1)S(1)}, bf16[4,128,256]{2,1,0:T(8,128)(2,1)S(1)}, u32[]{:S(2)}, u32[]{:S(2)}) collective-permute-start(bf16[4,128,256]{2,1,0:T(8,128)(2,1)S(1)} %copy-done.38), channel_id=1, source_target_pairs={{0,2},{1,3},{2,0},{3,1},{4,6},{5,7},{6,4},{7,5},{8,10},{9,11},{10,... | collective-permute-start | bytes 786440 | tf_op jit(solution)/shard_map/ppermute | solution.py:31
  28.5 32.3 %collective-permute-start.2 = (bf16[4,128,256]{2,1,0:T(8,128)(2,1)S(1)}, bf16[4,128,256]{2,1,0:T(8,128)(2,1)S(1)}, u32[]{:S(2)}, u32[]{:S(2)}) collective-permute-start(bf16[4,128,256]{2,1,0:T(8,128)(2,1)S(1)} %copy-done.37), channel_id=1, source_target_pairs={{0,3},{1,2},{2,1},{3,0},{4,7},{5,6},{6,5},{7,4},{8,11},{9,10},{10,... | collective-permute-start | bytes 786440 | tf_op jit(solution)/shard_map/ppermute | solution.py:31
  30.0 32.2 %collective-permute-start.16 = (bf16[4,128,256]{2,1,0:T(8,128)(2,1)}, bf16[4,128,256]{2,1,0:T(8,128)(2,1)S(1)}, u32[]{:S(2)}, u32[]{:S(2)}) collective-permute-start(bf16[4,128,256]{2,1,0:T(8,128)(2,1)} %get-tuple-element.90), channel_id=1, source_target_pairs={{0,1},{1,0},{2,3},{3,2},{4,5},{5,4},{6,7},{7,6},{8,9},{9,8},{10,11... | collective-permute-start | bytes 786440 | tf_op jit(solution)/shard_map/ppermute | solution.py:31
  30.1 41.9 %collective-permute-start.17 = (bf16[4,128,256]{2,1,0:T(8,128)(2,1)}, bf16[4,128,256]{2,1,0:T(8,128)(2,1)S(1)}, u32[]{:S(2)}, u32[]{:S(2)}) collective-permute-start(bf16[4,128,256]{2,1,0:T(8,128)(2,1)} %get-tuple-element.91), channel_id=1, source_target_pairs={{0,2},{1,3},{2,0},{3,1},{4,6},{5,7},{6,4},{7,5},{8,10},{9,11},{10,... | collective-permute-start | bytes 786440 | tf_op jit(solution)/shard_map/ppermute | solution.py:31
  45.3 28.2 %collective-permute-start.18 = (bf16[4,128,256]{2,1,0:T(8,128)(2,1)}, bf16[4,128,256]{2,1,0:T(8,128)(2,1)S(1)}, u32[]{:S(2)}, u32[]{:S(2)}) collective-permute-start(bf16[4,128,256]{2,1,0:T(8,128)(2,1)} %get-tuple-element.92), channel_id=1, source_target_pairs={{0,3},{1,2},{2,1},{3,0},{4,7},{5,6},{6,5},{7,4},{8,11},{9,10},{10,... | collective-permute-start | bytes 786440 | tf_op jit(solution)/shard_map/ppermute | solution.py:31
  72.0 19.7 %collective-permute-start.25 = (bf16[2,2,128,256]{3,2,1,0:T(8,128)(2,1)}, bf16[2,2,128,256]{3,2,1,0:T(8,128)(2,1)S(1)}, u32[]{:S(2)}, u32[]{:S(2)}) collective-permute-start(bf16[2,2,128,256]{3,2,1,0:T(8,128)(2,1)} %get-tuple-element.100), channel_id=1, source_target_pairs={{0,16},{4,20},{8,24},{12,28},{16,0},{20,4},{24,8},{28,12},{1,17},{... | collective-permute-start | bytes 786440 | tf_op jit(solution)/shard_map/ppermute | solution.py:31
  73.5 21.0 %collective-permute-start.26 = (bf16[2,2,128,256]{3,2,1,0:T(8,128)(2,1)}, bf16[2,2,128,256]{3,2,1,0:T(8,128)(2,1)S(1)}, u32[]{:S(2)}, u32[]{:S(2)}) collective-permute-start(bf16[2,2,128,256]{3,2,1,0:T(8,128)(2,1)} %get-tuple-element.101), channel_id=1, source_target_pairs={{0,20},{4,16},{8,28},{12,24},{16,4},{20,0},{24,12},{28,8},{1,21},{... | collective-permute-start | bytes 786440 | tf_op jit(solution)/shard_map/ppermute | solution.py:31
  77.3 19.1 %collective-permute-start.27 = (bf16[2,2,128,256]{3,2,1,0:T(8,128)(2,1)}, bf16[2,2,128,256]{3,2,1,0:T(8,128)(2,1)S(1)}, u32[]{:S(2)}, u32[]{:S(2)}) collective-permute-start(bf16[2,2,128,256]{3,2,1,0:T(8,128)(2,1)} %get-tuple-element.102), channel_id=1, source_target_pairs={{0,24},{4,28},{8,16},{12,20},{16,8},{20,12},{24,0},{28,4},{1,25},{... | collective-permute-start | bytes 786440 | tf_op jit(solution)/shard_map/ppermute | solution.py:31
  96.3 19.7 %collective-permute-start.9 = (bf16[2,2,128,256]{3,2,1,0:T(8,128)(2,1)}, bf16[2,2,128,256]{3,2,1,0:T(8,128)(2,1)S(1)}, u32[]{:S(2)}, u32[]{:S(2)}) collective-permute-start(bf16[2,2,128,256]{3,2,1,0:T(8,128)(2,1)} %get-tuple-element.82), channel_id=1, source_target_pairs={{0,16},{4,20},{8,24},{12,28},{16,0},{20,4},{24,8},{28,12},{1,17},{... | collective-permute-start | bytes 786440 | tf_op jit(solution)/shard_map/ppermute | solution.py:31
  97.8 22.4 %collective-permute-start.10 = (bf16[2,2,128,256]{3,2,1,0:T(8,128)(2,1)}, bf16[2,2,128,256]{3,2,1,0:T(8,128)(2,1)S(1)}, u32[]{:S(2)}, u32[]{:S(2)}) collective-permute-start(bf16[2,2,128,256]{3,2,1,0:T(8,128)(2,1)} %get-tuple-element.83), channel_id=1, source_target_pairs={{0,20},{4,16},{8,28},{12,24},{16,4},{20,0},{24,12},{28,8},{1,21},{... | collective-permute-start | bytes 786440 | tf_op jit(solution)/shard_map/ppermute | solution.py:31
  97.8 23.7 %collective-permute-start.11 = (bf16[2,2,128,256]{3,2,1,0:T(8,128)(2,1)}, bf16[2,2,128,256]{3,2,1,0:T(8,128)(2,1)S(1)}, u32[]{:S(2)}, u32[]{:S(2)}) collective-permute-start(bf16[2,2,128,256]{3,2,1,0:T(8,128)(2,1)} %get-tuple-element.84), channel_id=1, source_target_pairs={{0,24},{4,28},{8,16},{12,20},{16,8},{20,12},{24,0},{28,4},{1,25},{... | collective-permute-start | bytes 786440 | tf_op jit(solution)/shard_map/ppermute | solution.py:31
  99.0 23.1 %collective-permute-start.12 = (bf16[2,2,128,256]{3,2,1,0:T(8,128)(2,1)}, bf16[2,2,128,256]{3,2,1,0:T(8,128)(2,1)S(1)}, u32[]{:S(2)}, u32[]{:S(2)}) collective-permute-start(bf16[2,2,128,256]{3,2,1,0:T(8,128)(2,1)} %get-tuple-element.85), channel_id=1, source_target_pairs={{0,28},{4,24},{8,20},{12,16},{16,12},{20,8},{24,4},{28,0},{1,29},{... | collective-permute-start | bytes 786440 | tf_op jit(solution)/shard_map/ppermute | solution.py:31
  116.0 23.7 %collective-permute-start.30 = (bf16[4,128,256]{2,1,0:T(8,128)(2,1)S(1)}, bf16[4,128,256]{2,1,0:T(8,128)(2,1)S(1)}, u32[]{:S(2)}, u32[]{:S(2)}) collective-permute-start(bf16[4,128,256]{2,1,0:T(8,128)(2,1)S(1)} %get-tuple-element.106), channel_id=1, source_target_pairs={{0,2},{1,3},{2,0},{3,1},{4,6},{5,7},{6,4},{7,5},{8,10},{9,11},{10,... | collective-permute-start | bytes 786440 | tf_op jit(solution)/shard_map/ppermute | solution.py:31
  120.2 21.1 %collective-permute-start.42 = (bf16[2,2,128,256]{3,2,1,0:T(8,128)(2,1)S(1)}, bf16[2,2,128,256]{3,2,1,0:T(8,128)(2,1)S(1)}, u32[]{:S(2)}, u32[]{:S(2)}) collective-permute-start(bf16[2,2,128,256]{3,2,1,0:T(8,128)(2,1)S(1)} %get-tuple-element.125), channel_id=1, source_target_pairs={{0,4},{4,0},{8,12},{12,8},{16,20},{20,16},{24,28},{28,24},{1,5},{5... | collective-permute-start | bytes 786440 | tf_op jit(solution)/shard_map/ppermute | solution.py:31
  121.5 20.3 %collective-permute-start.43 = (bf16[2,2,128,256]{3,2,1,0:T(8,128)(2,1)S(1)}, bf16[2,2,128,256]{3,2,1,0:T(8,128)(2,1)S(1)}, u32[]{:S(2)}, u32[]{:S(2)}) collective-permute-start(bf16[2,2,128,256]{3,2,1,0:T(8,128)(2,1)S(1)} %get-tuple-element.126), channel_id=1, source_target_pairs={{0,8},{4,12},{8,0},{12,4},{16,24},{20,28},{24,16},{28,20},{1,9},{5... | collective-permute-start | bytes 786440 | tf_op jit(solution)/shard_map/ppermute | solution.py:31
  122.1 20.9 %collective-permute-start.44 = (bf16[2,2,128,256]{3,2,1,0:T(8,128)(2,1)S(1)}, bf16[2,2,128,256]{3,2,1,0:T(8,128)(2,1)S(1)}, u32[]{:S(2)}, u32[]{:S(2)}) collective-permute-start(bf16[2,2,128,256]{3,2,1,0:T(8,128)(2,1)S(1)} %get-tuple-element.127), channel_id=1, source_target_pairs={{0,12},{4,8},{8,4},{12,0},{16,28},{20,24},{24,20},{28,16},{1,13},{... | collective-permute-start | bytes 786440 | tf_op jit(solution)/shard_map/ppermute | solution.py:31
  139.7 19.4 %collective-permute-start.46 = (bf16[2,2,128,256]{3,2,1,0:T(8,128)(2,1)S(1)}, bf16[2,2,128,256]{3,2,1,0:T(8,128)(2,1)S(1)}, u32[]{:S(2)}, u32[]{:S(2)}) collective-permute-start(bf16[2,2,128,256]{3,2,1,0:T(8,128)(2,1)S(1)} %get-tuple-element.129), channel_id=1, source_target_pairs={{0,20},{4,16},{8,28},{12,24},{16,4},{20,0},{24,12},{28,8},{1,21},{... | collective-permute-start | bytes 786440 | tf_op jit(solution)/shard_map/ppermute | solution.py:31
  141.8 20.0 %collective-permute-start.48 = (bf16[2,2,128,256]{3,2,1,0:T(8,128)(2,1)S(1)}, bf16[2,2,128,256]{3,2,1,0:T(8,128)(2,1)S(1)}, u32[]{:S(2)}, u32[]{:S(2)}) collective-permute-start(bf16[2,2,128,256]{3,2,1,0:T(8,128)(2,1)S(1)} %get-tuple-element.131), channel_id=1, source_target_pairs={{0,28},{4,24},{8,20},{12,16},{16,12},{20,8},{24,4},{28,0},{1,29},{... | collective-permute-start | bytes 786440 | tf_op jit(solution)/shard_map/ppermute | solution.py:31
  143.1 19.1 %collective-permute-start.32 = (bf16[2,2,128,256]{3,2,1,0:T(8,128)(2,1)S(1)}, bf16[2,2,128,256]{3,2,1,0:T(8,128)(2,1)S(1)}, u32[]{:S(2)}, u32[]{:S(2)}) collective-permute-start(bf16[2,2,128,256]{3,2,1,0:T(8,128)(2,1)S(1)} %get-tuple-element.113), channel_id=1, source_target_pairs={{0,4},{4,0},{8,12},{12,8},{16,20},{20,16},{24,28},{28,24},{1,5},{5... | collective-permute-start | bytes 786440 | tf_op jit(solution)/shard_map/ppermute | solution.py:31
  160.3 20.4 %collective-permute-start.35 = (bf16[2,2,128,256]{3,2,1,0:T(8,128)(2,1)S(1)}, bf16[2,2,128,256]{3,2,1,0:T(8,128)(2,1)S(1)}, u32[]{:S(2)}, u32[]{:S(2)}) collective-permute-start(bf16[2,2,128,256]{3,2,1,0:T(8,128)(2,1)S(1)} %get-tuple-element.116), channel_id=1, source_target_pairs={{0,16},{4,20},{8,24},{12,28},{16,0},{20,4},{24,8},{28,12},{1,17},{... | collective-permute-start | bytes 786440 | tf_op jit(solution)/shard_map/ppermute | solution.py:31
  161.8 23.5 %collective-permute-start.36 = (bf16[2,2,128,256]{3,2,1,0:T(8,128)(2,1)S(1)}, bf16[2,2,128,256]{3,2,1,0:T(8,128)(2,1)S(1)}, u32[]{:S(2)}, u32[]{:S(2)}) collective-permute-start(bf16[2,2,128,256]{3,2,1,0:T(8,128)(2,1)S(1)} %get-tuple-element.117), channel_id=1, source_target_pairs={{0,20},{4,16},{8,28},{12,24},{16,4},{20,0},{24,12},{28,8},{1,21},{... | collective-permute-start | bytes 786440 | tf_op jit(solution)/shard_map/ppermute | solution.py:31
  162.2 23.2 %collective-permute-start.37 = (bf16[2,2,128,256]{3,2,1,0:T(8,128)(2,1)S(1)}, bf16[2,2,128,256]{3,2,1,0:T(8,128)(2,1)S(1)}, u32[]{:S(2)}, u32[]{:S(2)}) collective-permute-start(bf16[2,2,128,256]{3,2,1,0:T(8,128)(2,1)S(1)} %get-tuple-element.118), channel_id=1, source_target_pairs={{0,24},{4,28},{8,16},{12,20},{16,8},{20,12},{24,0},{28,4},{1,25},{... | collective-permute-start | bytes 786440 | tf_op jit(solution)/shard_map/ppermute | solution.py:31
  163.1 28.2 %collective-permute-start.38 = (bf16[2,2,128,256]{3,2,1,0:T(8,128)(2,1)S(1)}, bf16[2,2,128,256]{3,2,1,0:T(8,128)(2,1)}, u32[]{:S(2)}, u32[]{:S(2)}) collective-permute-start(bf16[2,2,128,256]{3,2,1,0:T(8,128)(2,1)S(1)} %get-tuple-element.119), channel_id=1, source_target_pairs={{0,28},{4,24},{8,20},{12,16},{16,12},{20,8},{24,4},{28,0},{1,29},{... | collective-permute-start | bytes 786440 | tf_op jit(solution)/shard_map/ppermute | solution.py:31
  167.0 30.0 %collective-permute-start.31 = (bf16[4,128,256]{2,1,0:T(8,128)(2,1)S(1)}, bf16[4,128,256]{2,1,0:T(8,128)(2,1)S(1)}, u32[]{:S(2)}, u32[]{:S(2)}) collective-permute-start(bf16[4,128,256]{2,1,0:T(8,128)(2,1)S(1)} %get-tuple-element.107), channel_id=1, source_target_pairs={{0,3},{1,2},{2,1},{3,0},{4,7},{5,6},{6,5},{7,4},{8,11},{9,10},{10,... | collective-permute-start | bytes 786440 | tf_op jit(solution)/shard_map/ppermute | solution.py:31
  185.3 25.8 %collective-permute-start.14 = (bf16[4,128,256]{2,1,0:T(8,128)(2,1)S(1)}, bf16[4,128,256]{2,1,0:T(8,128)(2,1)}, u32[]{:S(2)}, u32[]{:S(2)}) collective-permute-start(bf16[4,128,256]{2,1,0:T(8,128)(2,1)S(1)} %get-tuple-element.88), channel_id=1, source_target_pairs={{0,2},{1,3},{2,0},{3,1},{4,6},{5,7},{6,4},{7,5},{8,10},{9,11},{10,... | collective-permute-start | bytes 786440 | tf_op jit(solution)/shard_map/ppermute | solution.py:31
  185.4 25.8 %collective-permute-start.15 = (bf16[4,128,256]{2,1,0:T(8,128)(2,1)S(1)}, bf16[4,128,256]{2,1,0:T(8,128)(2,1)}, u32[]{:S(2)}, u32[]{:S(2)}) collective-permute-start(bf16[4,128,256]{2,1,0:T(8,128)(2,1)S(1)} %get-tuple-element.89), channel_id=1, source_target_pairs={{0,3},{1,2},{2,1},{3,0},{4,7},{5,6},{6,5},{7,4},{8,11},{9,10},{10,... | collective-permute-start | bytes 786440 | tf_op jit(solution)/shard_map/ppermute | solution.py:31
  191.3 26.8 %collective-permute-start.49 = (bf16[2,128,256]{2,1,0:T(8,128)(2,1)}, bf16[2,128,256]{2,1,0:T(8,128)(2,1)S(1)}, u32[]{:S(2)}, u32[]{:S(2)}) collective-permute-start(bf16[2,128,256]{2,1,0:T(8,128)(2,1)} %get-tuple-element.133), channel_id=1, source_target_pairs={{0,1},{1,0},{2,3},{3,2},{4,5},{5,4},{6,7},{7,6},{8,9},{9,8},{10,11... | collective-permute-start | bytes 393224 | tf_op jit(solution)/shard_map/ppermute | solution.py:31
  197.0 25.6 %collective-permute-start.50 = (bf16[2,128,256]{2,1,0:T(8,128)(2,1)S(1)}, bf16[2,128,256]{2,1,0:T(8,128)(2,1)S(1)}, u32[]{:S(2)}, u32[]{:S(2)}) collective-permute-start(bf16[2,128,256]{2,1,0:T(8,128)(2,1)S(1)} %copy-done.40), channel_id=1, source_target_pairs={{0,2},{1,3},{2,0},{3,1},{4,6},{5,7},{6,4},{7,5},{8,10},{9,11},{10,... | collective-permute-start | bytes 393224 | tf_op jit(solution)/shard_map/ppermute | solution.py:31
  198.1 24.6 %collective-permute-start.51 = (bf16[2,128,256]{2,1,0:T(8,128)(2,1)S(1)}, bf16[2,128,256]{2,1,0:T(8,128)(2,1)S(1)}, u32[]{:S(2)}, u32[]{:S(2)}) collective-permute-start(bf16[2,128,256]{2,1,0:T(8,128)(2,1)S(1)} %copy-done.39), channel_id=1, source_target_pairs={{0,3},{1,2},{2,1},{3,0},{4,7},{5,6},{6,5},{7,4},{8,11},{9,10},{10,... | collective-permute-start | bytes 393224 | tf_op jit(solution)/shard_map/ppermute | solution.py:31
  211.2 19.6 %collective-permute-start.40 = (bf16[2,128,256]{2,1,0:T(8,128)(2,1)}, bf16[2,128,256]{2,1,0:T(8,128)(2,1)S(1)}, u32[]{:S(2)}, u32[]{:S(2)}) collective-permute-start(bf16[2,128,256]{2,1,0:T(8,128)(2,1)} %get-tuple-element.122), channel_id=1, source_target_pairs={{0,2},{1,3},{2,0},{3,1},{4,6},{5,7},{6,4},{7,5},{8,10},{9,11},{10,... | collective-permute-start | bytes 393224 | tf_op jit(solution)/shard_map/ppermute | solution.py:31
  (61 other events, 975.7 us)
where the time goes:
time: 235 us; the launch traced here: 234 us
  waiting for transfers between devices  94 us (40%)
  starting transfers between devices  85.7 us (36%)
  Pallas kernels  48.7 us (21%)
  local copies, waits for them, and re-layouts  4.26 us (2%)
    ppermute x52, waiting for transfers between devices, swap(): return lax.ppermute(x, axis, [(i, i ^ mask) for i in range(count)])  94 us
    ppermute x52, starting transfers between devices, swap(): return lax.ppermute(x, axis, [(i, i ^ mask) for i in range(count)])  85.7 us
    pallas_call x2, Pallas kernels, attend(): pl.pallas_call(body, out_shape=[jax.ShapeDtypeStruct(side, BF)] * n + [ja...  20.6 us
    pallas_call x2, Pallas kernels, total_terms(): pl.pallas_call(body, out_shape=[jax.ShapeDtypeStruct(shape, BF)] * n, in_...  7.94 us
    pallas_call x4, Pallas kernels, pack(): pl.pallas_call(body, out_shape=[jax.ShapeDtypeStruct(shape, BF)] * (n - 1...  7.54 us
    pallas_call x2, Pallas kernels, select(): pl.pallas_call(body, out_shape=[jax.ShapeDtypeStruct(plan.tile, BF)] * sl...  7.3 us
    pallas_call x2, Pallas kernels, unpack(): pl.pallas_call(body, out_shape=[jax.ShapeDtypeStruct(shape, BF)] * k, in_...  5.24 us
  transfers between devices with their start and end apart: 52, of which 14 were waited for; matrix products, arithmetic and copies ran while one was open for 0% of the time, Pallas kernels for 19%

commit v1 on v0

v1 whole, which is shorter than its diff:
```python
import functools
import math

import jax
import jax.numpy as jnp
from jax import lax
from jax.experimental import pallas as pl
from jax.experimental.pallas import tpu as pltpu
from jax.sharding import PartitionSpec as P

HD = 128
BLK = 256
SEL = 4
CHUNKS = 2

MASKED = -1e30
BF = jnp.bfloat16
F32 = jnp.float32


HBM = pl.BlockSpec(memory_space=pl.ANY)
SMEM = pl.BlockSpec(memory_space=pltpu.SMEM)
VMEM = pl.BlockSpec(memory_space=pltpu.VMEM)


def cost(nbytes, flops=0, trans=0):
    return pl.CostEstimate(flops=flops, bytes_accessed=nbytes, transcendentals=trans)


def swap(x, axis, mask):
    count = lax.axis_size(axis)
    return lax.ppermute(x, axis, [(i, i ^ mask) for i in range(count)])


class Plan:
    def __init__(self, rows, features, blocks, chunks):
        self.ctx = lax.axis_size("ctx")
        self.n = lax.axis_size("head")
        self.rows = rows
        self.features = features
        self.bh = blocks // self.ctx
        self.per = self.n // self.bh
        self.group = features // self.n
        self.heads = self.group // HD
        self.chunks = min(chunks, self.heads)
        self.width = self.group // self.chunks
        self.tile = (2, self.per, rows, self.width)
        self.tile_bytes = 2 * BLK * self.width * 2

    def cols(self, z, mask, chunk):
        start = (z ^ mask) * self.group + chunk * self.width
        return pl.ds(pl.multiple_of(start, HD), self.width)


def run_all(copies):
    for c in copies:
        c.start()
    for c in copies:
        c.wait()


def on_chip(arrays):
    return [pltpu.with_memory_space_constraint(x, pltpu.VMEM) for x in arrays]


def grant(mib):
    return pltpu.CompilerParams(vmem_limit_bytes=mib * 1024 * 1024)


def pack(plan, arrays, chunk):
    k, n = len(arrays), plan.n

    def body(*refs):
        ins, outs, sem = refs[:k], refs[k : k + n], refs[k + n]
        z = lax.axis_index("head")
        run_all(
            [
                pltpu.make_async_copy(
                    ins[i].at[:, plan.cols(z, m, chunk)], outs[m].at[i], sem.at[m, i]
                )
                for m in range(n)
                for i in range(k)
            ]
        )

    shape = (k, plan.rows, plan.width)
    return pl.pallas_call(
        body,
        out_shape=[pltpu.VMEM(shape, BF)] * n,
        in_specs=[HBM] * k,
        out_specs=[VMEM] * n,
        scratch_shapes=[pltpu.SemaphoreType.DMA((n, k))],
        compiler_params=grant(1),
        cost_estimate=cost(2 * k * n * plan.rows * plan.width * 2),
        name="pack",
    )(*arrays)


def unpack(plan, pieces, k):
    n, chunks = plan.n, plan.chunks
    flat = [p for chunk in pieces for p in chunk]

    def body(*refs):
        ins, outs, sem = refs[: n * chunks], refs[n * chunks : n * chunks + k], refs[-1]
        z = lax.axis_index("head")
        run_all(
            [
                pltpu.make_async_copy(
                    ins[c * n + m].at[i], outs[i].at[:, plan.cols(z, m, c)], sem.at[c * n + m, i]
                )
                for c in range(chunks)
                for m in range(n)
                for i in range(k)
            ]
        )

    shape = (plan.rows, plan.features)
    return pl.pallas_call(
        body,
        out_shape=[jax.ShapeDtypeStruct(shape, BF)] * k,
        in_specs=[VMEM] * len(flat),
        out_specs=[HBM] * k,
        scratch_shapes=[pltpu.SemaphoreType.DMA((len(flat), k))],
        compiler_params=grant(1),
        cost_estimate=cost(2 * k * plan.rows * plan.features * 2),
        name="unpack",
    )(*on_chip(flat))


def wanted(plan, lists, reader, owner, z):
    live, which = jnp.int32(0), jnp.int32(0)
    for e in range(plan.bh * SEL):
        entry = lists[reader * plan.bh + e // SEL, e % SEL]
        hit = (entry >= 0) & (lax.div(entry, jnp.int32(plan.bh)) == owner)
        local = lax.rem(entry, jnp.int32(plan.bh)) ^ lax.div(z, jnp.int32(plan.per))
        live = jnp.where(hit, 1, live)
        which = jnp.where(hit, local, which)
    return live, which


def select(plan, rows, lists):
    n, per, slots, bh = plan.n, plan.per, plan.ctx, plan.bh

    def body(*refs):
        lists_ref, ins, outs = refs[0], refs[1 : 1 + n], refs[1 + n :]
        me, z = lax.axis_index("ctx"), lax.axis_index("head")
        for s in range(slots):
            which = wanted(plan, lists_ref, me ^ s, me, z)[1]
            for j in range(bh):

                @pl.when(which == j)
                def _():
                    for p in range(per):
                        outs[s][:, p] = ins[j * per + p][...]

    return pl.pallas_call(
        body,
        out_shape=[pltpu.VMEM(plan.tile, BF)] * slots,
        in_specs=[SMEM] + [VMEM] * n,
        out_specs=[VMEM] * slots,
        compiler_params=grant(1),
        cost_estimate=cost((slots + plan.bh) * plan.tile_bytes),
        name="select",
    )(lists, *on_chip(rows))


def dot(a, b, ca, cb):
    return lax.dot_general(a, b, (((ca,), (cb,)), ((), ())), preferred_element_type=F32)


def attend(plan, noisy, tiles, lists):
    n, per, slots, rows, bh = plan.n, plan.per, plan.ctx, plan.rows, plan.bh
    heads = plan.width // HD
    scale = 1.0 / math.sqrt(HD)
    log2e = 1.0 / math.log(2.0)
    side = (4, rows, plan.width)

    def body(*refs):
        lists_ref, rows_in, tile_refs = refs[0], refs[1 : 1 + n], refs[1 + n : 1 + n + slots]
        rows_out = refs[1 + n + slots : 1 + 2 * n + slots]
        term_refs = refs[1 + 2 * n + slots : 1 + 2 * n + 2 * slots]
        tiles_in, terms_out = refs[1 + 2 * n + 2 * slots :]
        me, z = lax.axis_index("ctx"), lax.axis_index("head")
        home = lax.div(z, jnp.int32(per))
        for s in range(slots):
            tiles_in[s] = tile_refs[s][...]

        def step(h, carry):
            cols = pl.ds(pl.multiple_of(h * HD, HD), HD)
            for b in range(bh):
                part = range(b * per, (b + 1) * per)

                def noisy_block(j):
                    return jnp.concatenate([rows_in[m][j, :, cols] for m in part], 0)

                def put_noisy(j, value):
                    value = value.astype(BF).reshape(per, rows, HD)
                    for p in range(per):
                        rows_out[b * per + p][j, :, cols] = value[p]

                def clean_block(slot, kv):
                    return tiles_in[slot, kv, :, :, cols].reshape(BLK, HD)

                def put_clean(slot, kv, value):
                    terms_out[slot, kv, :, :, cols] = value.astype(BF).reshape(per, rows, HD)

                q, k0, v0, g = (noisy_block(j) for j in range(4))
                row = me * bh + (b ^ home)
                keys, values, bias, target = [k0], [v0], [None], []
                for s in range(SEL):
                    entry = lists_ref[row, s]
                    live = entry >= 0
                    slot = jnp.where(live, lax.div(entry, jnp.int32(bh)) ^ me, 0)
                    keys.append(clean_block(slot, 0))
                    values.append(clean_block(slot, 1))
                    bias.append(jnp.where(live, 0.0, MASKED).astype(F32))
                    target.append(jnp.where(live, slot, slots))
                scores = []
                for kt, extra in zip(keys, bias):
                    s = dot(kt, q, 1, 1) * (scale * log2e)
                    scores.append(s if extra is None else s + extra)
                top = functools.reduce(
                    jnp.maximum, [jnp.max(s, axis=0, keepdims=True) for s in scores]
                )
                weights = [jnp.exp2(s - top) for s in scores]
                total = functools.reduce(
                    jnp.add, [jnp.sum(w, axis=0, keepdims=True) for w in weights]
                )
                inverse = 1.0 / total
                probs = [w * inverse for w in weights]
                probs_bf = [p.astype(BF) for p in probs]
                out_t = functools.reduce(
                    jnp.add, [dot(vt.T, p, 1, 0) for vt, p in zip(values, probs_bf)]
                )
                out_bf = out_t.astype(BF)
                put_noisy(0, out_bf.T)
                delta = jnp.sum(g.T.astype(F32) * out_bf.astype(F32), axis=0, keepdims=True)
                dq_t = jnp.zeros((HD, BLK), F32)
                for t in range(1 + SEL):
                    ds = (probs[t] * (dot(values[t], g, 1, 1) - delta)).astype(BF)
                    dq_t = dq_t + dot(keys[t].T, ds, 1, 0)
                    kterm = dot(ds, q, 1, 0) * scale
                    vterm = dot(probs_bf[t], g, 1, 0)
                    if t == 0:
                        put_noisy(2, kterm)
                        put_noisy(3, vterm)
                    else:
                        put_clean(target[t - 1], 0, kterm)
                        put_clean(target[t - 1], 1, vterm)
                put_noisy(1, (dq_t * scale).astype(BF).T)
            return carry

        lax.fori_loop(0, heads, step, 0)
        for s in range(slots):
            term_refs[s][...] = terms_out[s]

    flops = heads * bh * 6 * 2 * BLK * (1 + SEL) * BLK * HD
    result = pl.pallas_call(
        body,
        out_shape=[pltpu.VMEM(side, BF)] * n + [pltpu.VMEM(plan.tile, BF)] * slots,
        in_specs=[SMEM] + [VMEM] * (n + slots),
        out_specs=[VMEM] * (n + slots),
        scratch_shapes=[
            pltpu.VMEM((slots,) + plan.tile, BF),
            pltpu.VMEM((slots + 1,) + plan.tile, BF),
        ],
        compiler_params=grant(24),
        cost_estimate=cost(
            2 * (slots * plan.tile_bytes + 4 * bh * BLK * plan.width * 2),
            flops,
            heads * bh * BLK * (1 + SEL) * BLK,
        ),
        name="attend",
    )(lists, *on_chip(noisy), *on_chip(tiles))
    return result[:n], result[n:]


def total_terms(plan, terms, lists):
    n, per, slots, rows, bh = plan.n, plan.per, plan.ctx, plan.rows, plan.bh

    def body(*refs):
        lists_ref, ins, outs = refs[0], refs[1 : 1 + slots], refs[1 + slots :]
        me, z = lax.axis_index("ctx"), lax.axis_index("head")
        asked = [wanted(plan, lists_ref, me ^ s, me, z) for s in range(slots)]
        stripe = math.gcd(rows, 32)

        def step(i, carry):
            at = pl.ds(pl.multiple_of(i * stripe, stripe), stripe)
            for kv in range(2):
                for p in range(per):
                    parts = [ins[s][kv, p, at, :].astype(F32) for s in range(slots)]
                    for j in range(bh):
                        acc = jnp.zeros((stripe, plan.width), F32)
                        for (live, which), part in zip(asked, parts):
                            acc = acc + jnp.where((live > 0) & (which == j), part, 0.0)
                        outs[j * per + p][kv, at, :] = acc.astype(BF)
            return carry

        lax.fori_loop(0, rows // stripe, step, 0)

    shape = (2, rows, plan.width)
    return pl.pallas_call(
        body,
        out_shape=[pltpu.VMEM(shape, BF)] * n,
        in_specs=[SMEM] + [VMEM] * slots,
        out_specs=[VMEM] * n,
        compiler_params=grant(4),
        cost_estimate=cost((slots + bh) * plan.tile_bytes),
        name="total_terms",
    )(lists, *on_chip(terms))


def slot_order(slots):
    return sorted(range(1, slots), key=lambda s: (-bin(s >> 1).count("1"), s >> 1 == 0, s))


def over_head(parts):
    got = {0: parts[0]}
    for m in range(len(parts) - 1, 0, -1):
        got[m] = swap(parts[m], "head", m)
    return [got[m] for m in range(len(parts))]


def over_ctx(parts):
    got = {0: parts[0]}
    for s in slot_order(len(parts)):
        got[s] = swap(parts[s], "ctx", s)
    return [got[s] for s in range(len(parts))]


def shards(query, key, value, kclean, vclean, grad, lists):
    plan = Plan(query.shape[0], query.shape[1], lists.shape[0], CHUNKS)
    chunks = range(plan.chunks)
    clean = [over_head(pack(plan, (kclean, vclean), c)) for c in chunks]
    noisy = [over_head(pack(plan, (query, key, value, grad), c)) for c in chunks]
    tiles = [over_ctx(select(plan, clean[c], lists)) for c in chunks]
    sides, sums = [], []
    for c in chunks:
        side, terms = attend(plan, noisy[c], tiles[c], lists)
        sides.append(over_head(side))
        terms = over_ctx(terms)
        sums.append(over_head(total_terms(plan, terms, lists)))
    return (*unpack(plan, sides, 4), *unpack(plan, sums, 2))


def solution(mesh):
    rows = P(("ctx", "head"), None)
    return jax.shard_map(
        shards,
        mesh=mesh,
        in_specs=(rows,) * 6 + (P(),),
        out_specs=(rows,) * 6,
        check_vma=False,
    )
```

time: 235 us -> 226 us (0.962)
  Pallas kernels: 48.7 us -> 28.5 us
  starting transfers between devices: 85.7 us -> 95.4 us
    pallas_call x10, Pallas kernels: 43.4 us -> 25.8 us  [the longest x2 17.1 us: attend(): pl.pallas_call(body, out_shape=[pltpu.VMEM(side, BF)] * n + [pltpu.VMEM(p...]
    ppermute x52, starting transfers between devices: 85.7 us -> 95.4 us  [swap(): return lax.ppermute(x, axis, [(i, i ^ mask) for i in range(count)])]
    pallas_call x2, Pallas kernels: 5.24 us -> 2.65 us  [unpack(): pl.pallas_call(body, out_shape=[jax.ShapeDtypeStruct(shape, BF)] * k, in_...]
  transfers between devices with their start and end apart: 52 -> 52, of which waited for: 14 -> 11; matrix products, arithmetic and copies ran while one was open for 0% -> 0% of each run, Pallas kernels for 19% -> 12%
where the time goes in v1:
time: 226 us; the launch traced here: 224 us
  starting transfers between devices  95.4 us (42%)
  waiting for transfers between devices  95.1 us (42%)
  Pallas kernels  28.5 us (13%)
  local copies, waits for them, and re-layouts  4.42 us (2%)
    ppermute x52, starting transfers between devices, swap(): return lax.ppermute(x, axis, [(i, i ^ mask) for i in range(count)])  95.4 us
    ppermute x52, waiting for transfers between devices, swap(): return lax.ppermute(x, axis, [(i, i ^ mask) for i in range(count)])  95.1 us
    pallas_call x2, Pallas kernels, attend(): pl.pallas_call(body, out_shape=[pltpu.VMEM(side, BF)] * n + [pltpu.VMEM(p...  17.1 us
  transfers between devices with their start and end apart: 52, of which 11 were waited for; matrix products, arithmetic and copies ran while one was open for 0% of the time, Pallas kernels for 12%

profile of v1, /device:TPU:0, one launch (start us, length us, event | category | flops | bytes accessed | tf_op | source)
XLA Modules:
  0.0 224.5 jit_solution(4165289199950745066)
XLA Ops:
  2.9 3.1 %collective-permute-start.19 = (bf16[2,128,256]{2,1,0:T(8,128)(2,1)S(1)}, bf16[2,128,256]{2,1,0:T(8,128)(2,1)S(1)}, u32[]{:S(2)}, u32[]{:S(2)}) collective-permute-start(bf16[2,128,256]{2,1,0:T(8,128)(2,1)S(1)} %get-tuple-element.101), channel_id=1, source_target_pairs={{0,1},{1,0},{2,3},{3,2},{4,5},{5,4},{6,7},{7,6},{8,9},{9,8},{10,11... | collective-permute-start | bytes 393224 | tf_op jit(solution)/shard_map/ppermute | solution.py:32
  6.0 2.6 %collective-permute-start.20 = (bf16[2,128,256]{2,1,0:T(8,128)(2,1)S(1)}, bf16[2,128,256]{2,1,0:T(8,128)(2,1)S(1)}, u32[]{:S(2)}, u32[]{:S(2)}) collective-permute-start(bf16[2,128,256]{2,1,0:T(8,128)(2,1)S(1)} %get-tuple-element.102), channel_id=1, source_target_pairs={{0,2},{1,3},{2,0},{3,1},{4,6},{5,7},{6,4},{7,5},{8,10},{9,11},{10,... | collective-permute-start | bytes 393224 | tf_op jit(solution)/shard_map/ppermute | solution.py:32
  9.8 3.5 %collective-permute-start.4 = (bf16[2,128,256]{2,1,0:T(8,128)(2,1)S(1)}, bf16[2,128,256]{2,1,0:T(8,128)(2,1)S(1)}, u32[]{:S(2)}, u32[]{:S(2)}) collective-permute-start(bf16[2,128,256]{2,1,0:T(8,128)(2,1)S(1)} %get-tuple-element.82), channel_id=1, source_target_pairs={{0,2},{1,3},{2,0},{3,1},{4,6},{5,7},{6,4},{7,5},{8,10},{9,11},{10,... | collective-permute-start | bytes 393224 | tf_op jit(solution)/shard_map/ppermute | solution.py:32
  13.2 2.6 %collective-permute-start.5 = (bf16[2,128,256]{2,1,0:T(8,128)(2,1)S(1)}, bf16[2,128,256]{2,1,0:T(8,128)(2,1)S(1)}, u32[]{:S(2)}, u32[]{:S(2)}) collective-permute-start(bf16[2,128,256]{2,1,0:T(8,128)(2,1)S(1)} %get-tuple-element.83), channel_id=1, source_target_pairs={{0,3},{1,2},{2,1},{3,0},{4,7},{5,6},{6,5},{7,4},{8,11},{9,10},{10,... | collective-permute-start | bytes 393224 | tf_op jit(solution)/shard_map/ppermute | solution.py:32
  20.4 8.3 %collective-permute-start.17 = (bf16[4,128,256]{2,1,0:T(8,128)(2,1)}, bf16[4,128,256]{2,1,0:T(8,128)(2,1)S(1)}, u32[]{:S(2)}, u32[]{:S(2)}) collective-permute-start(bf16[4,128,256]{2,1,0:T(8,128)(2,1)} %get-tuple-element.98), channel_id=1, source_target_pairs={{0,2},{1,3},{2,0},{3,1},{4,6},{5,7},{6,4},{7,5},{8,10},{9,11},{10,... | collective-permute-start | bytes 786440 | tf_op jit(solution)/shard_map/ppermute | solution.py:32
  30.3 15.3 %collective-permute-start.1 = (bf16[4,128,256]{2,1,0:T(8,128)(2,1)}, bf16[4,128,256]{2,1,0:T(8,128)(2,1)S(1)}, u32[]{:S(2)}, u32[]{:S(2)}) collective-permute-start(bf16[4,128,256]{2,1,0:T(8,128)(2,1)} %get-tuple-element.78), channel_id=1, source_target_pairs={{0,2},{1,3},{2,0},{3,1},{4,6},{5,7},{6,4},{7,5},{8,10},{9,11},{10,... | collective-permute-start | bytes 786440 | tf_op jit(solution)/shard_map/ppermute | solution.py:32
  48.4 12.7 %collective-permute-done.17.refs_3_ = bf16[4,128,256]{2,1,0:T(8,128)(2,1)S(1)} collective-permute-done((bf16[4,128,256]{2,1,0:T(8,128)(2,1)}, bf16[4,128,256]{2,1,0:T(8,128)(2,1)S(1)}, u32[]{:S(2)}, u32[]{:S(2)}) %collective-permute-start.17) | collective-permute-done | bytes 262176 | tf_op jit(solution)/shard_map/ppermute | solution.py:32
  62.9 9.4 %collective-permute-done.1.refs_3_ = bf16[4,128,256]{2,1,0:T(8,128)(2,1)S(1)} collective-permute-done((bf16[4,128,256]{2,1,0:T(8,128)(2,1)}, bf16[4,128,256]{2,1,0:T(8,128)(2,1)S(1)}, u32[]{:S(2)}, u32[]{:S(2)}) %collective-permute-start.1) | collective-permute-done | bytes 262176 | tf_op jit(solution)/shard_map/ppermute | solution.py:32
  72.3 1.5 collective-permute-start.9
  78.3 13.5 %collective-permute-done.9.refs_9_ = bf16[2,2,128,256]{3,2,1,0:T(8,128)(2,1)S(1)} collective-permute-done((bf16[2,2,128,256]{3,2,1,0:T(8,128)(2,1)S(1)}, bf16[2,2,128,256]{3,2,1,0:T(8,128)(2,1)S(1)}, u32[]{:S(2)}, u32[]{:S(2)}) %collective-permute-start.9) | collective-permute-done | bytes 262176 | tf_op jit(solution)/shard_map/ppermute | solution.py:32
  94.5 2.2 collective-permute-start.24
  99.1 2.0 collective-permute-start.28
  101.1 8.5 %attend.2 = (bf16[4,128,256]{2,1,0:T(8,128)(2,1)S(1)}, bf16[4,128,256]{2,1,0:T(8,128)(2,1)S(1)}, bf16[4,128,256]{2,1,0:T(8,128)(2,1)S(1)}, bf16[4,128,256]{2,1,0...) custom-call(s32[16,4]{1,0:T(8,128)S(1)} %copy.14.refs_0_, ...), custom_call_target="tpu_custom_call" | custom-call | flops 2013265920 | bytes 6291456 | tf_op jit(solution)/shard_map/attend/pallas_call | solution.py:258
  111.2 5.9 %collective-permute-done.25.refs_9_ = bf16[2,2,128,256]{3,2,1,0:T(8,128)(2,1)S(1)} collective-permute-done((bf16[2,2,128,256]{3,2,1,0:T(8,128)(2,1)S(1)}, bf16[2,2,128,256]{3,2,1,0:T(8,128)(2,1)S(1)}, u32[]{:S(2)}, u32[]{:S(2)}) %collective-permute-start.25) | collective-permute-done | bytes 262176 | tf_op jit(solution)/shard_map/ppermute | solution.py:32
  117.1 2.5 %collective-permute-start.14 = (bf16[4,128,256]{2,1,0:T(8,128)(2,1)S(1)}, bf16[4,128,256]{2,1,0:T(8,128)(2,1)S(1)}, u32[]{:S(2)}, u32[]{:S(2)}) collective-permute-start(bf16[4,128,256]{2,1,0:T(8,128)(2,1)S(1)} %get-tuple-element.94), channel_id=1, source_target_pairs={{0,2},{1,3},{2,0},{3,1},{4,6},{5,7},{6,4},{7,5},{8,10},{9,11},{10,... | collective-permute-start | bytes 786440 | tf_op jit(solution)/shard_map/ppermute | solution.py:32
  123.2 8.5 %attend.3 = (bf16[4,128,256]{2,1,0:T(8,128)(2,1)S(1)}, bf16[4,128,256]{2,1,0:T(8,128)(2,1)S(1)}, bf16[4,128,256]{2,1,0:T(8,128)(2,1)S(1)}, bf16[4,128,256]{2,1,0...) custom-call(s32[16,4]{1,0:T(8,128)S(1)} %copy.14.refs_0_, ...), custom_call_target="tpu_custom_call" | custom-call | flops 2013265920 | bytes 6291456 | tf_op jit(solution)/shard_map/attend/pallas_call | solution.py:258
  133.1 1.6 collective-permute-start.37
  137.5 13.7 %collective-permute-done.36.refs_6_ = bf16[2,2,128,256]{3,2,1,0:T(8,128)(2,1)S(1)} collective-permute-done((bf16[2,2,128,256]{3,2,1,0:T(8,128)(2,1)S(1)}, bf16[2,2,128,256]{3,2,1,0:T(8,128)(2,1)S(1)}, u32[]{:S(2)}, u32[]{:S(2)}) %collective-permute-start.36) | collective-permute-done | bytes 262176 | tf_op jit(solution)/shard_map/ppermute | solution.py:32
  155.2 2.0 collective-permute-start.48
  157.1 2.3 %collective-permute-done.44.refs_4_ = bf16[2,2,128,256]{3,2,1,0:T(8,128)(2,1)S(1)} collective-permute-done((bf16[2,2,128,256]{3,2,1,0:T(8,128)(2,1)S(1)}, bf16[2,2,128,256]{3,2,1,0:T(8,128)(2,1)S(1)}, u32[]{:S(2)}, u32[]{:S(2)}) %collective-permute-start.44) | collective-permute-done | bytes 262176 | tf_op jit(solution)/shard_map/ppermute | solution.py:32
  159.4 2.3 %collective-permute-start.15 = (bf16[4,128,256]{2,1,0:T(8,128)(2,1)S(1)}, bf16[4,128,256]{2,1,0:T(8,128)(2,1)S(1)}, u32[]{:S(2)}, u32[]{:S(2)}) collective-permute-start(bf16[4,128,256]{2,1,0:T(8,128)(2,1)S(1)} %get-tuple-element.95), channel_id=1, source_target_pairs={{0,3},{1,2},{2,1},{3,0},{4,7},{5,6},{6,5},{7,4},{8,11},{9,10},{10,... | collective-permute-start | bytes 786440 | tf_op jit(solution)/shard_map/ppermute | solution.py:32
  161.7 11.4 %collective-permute-done.45.refs_5_ = bf16[2,2,128,256]{3,2,1,0:T(8,128)(2,1)S(1)} collective-permute-done((bf16[2,2,128,256]{3,2,1,0:T(8,128)(2,1)S(1)}, bf16[2,2,128,256]{3,2,1,0:T(8,128)(2,1)S(1)}, u32[]{:S(2)}, u32[]{:S(2)}) %collective-permute-start.45) | collective-permute-done | bytes 262176 | tf_op jit(solution)/shard_map/ppermute | solution.py:32
  173.1 1.9 collective-permute-start.29
  176.2 3.6 %collective-permute-start.30 = (bf16[4,128,256]{2,1,0:T(8,128)(2,1)S(1)}, bf16[4,128,256]{2,1,0:T(8,128)(2,1)S(1)}, u32[]{:S(2)}, u32[]{:S(2)}) collective-permute-start(bf16[4,128,256]{2,1,0:T(8,128)(2,1)S(1)} %get-tuple-element.114), channel_id=1, source_target_pairs={{0,2},{1,3},{2,0},{3,1},{4,6},{5,7},{6,4},{7,5},{8,10},{9,11},{10,... | collective-permute-start | bytes 786440 | tf_op jit(solution)/shard_map/ppermute | solution.py:32
  181.1 1.8 total_terms.2
  183.1 1.8 total_terms.3
  184.9 3.1 %collective-permute-start.40 = (bf16[2,128,256]{2,1,0:T(8,128)(2,1)S(1)}, bf16[2,128,256]{2,1,0:T(8,128)(2,1)S(1)}, u32[]{:S(2)}, u32[]{:S(2)}) collective-permute-start(bf16[2,128,256]{2,1,0:T(8,128)(2,1)S(1)} %get-tuple-element.130), channel_id=1, source_target_pairs={{0,2},{1,3},{2,0},{3,1},{4,6},{5,7},{6,4},{7,5},{8,10},{9,11},{10,... | collective-permute-start | bytes 393224 | tf_op jit(solution)/shard_map/ppermute | solution.py:32
  189.4 14.2 %collective-permute-done.30.refs_6_ = bf16[4,128,256]{2,1,0:T(8,128)(2,1)S(1)} collective-permute-done((bf16[4,128,256]{2,1,0:T(8,128)(2,1)S(1)}, bf16[4,128,256]{2,1,0:T(8,128)(2,1)S(1)}, u32[]{:S(2)}, u32[]{:S(2)}) %collective-permute-start.30) | collective-permute-done | bytes 262176 | tf_op jit(solution)/shard_map/ppermute | solution.py:32
  203.6 6.3 %collective-permute-start.50 = (bf16[2,128,256]{2,1,0:T(8,128)(2,1)S(1)}, bf16[2,128,256]{2,1,0:T(8,128)(2,1)S(1)}, u32[]{:S(2)}, u32[]{:S(2)}) collective-permute-start(bf16[2,128,256]{2,1,0:T(8,128)(2,1)S(1)} %get-tuple-element.142), channel_id=1, source_target_pairs={{0,2},{1,3},{2,0},{3,1},{4,6},{5,7},{6,4},{7,5},{8,10},{9,11},{10,... | collective-permute-start | bytes 393224 | tf_op jit(solution)/shard_map/ppermute | solution.py:32
  209.8 2.3 %collective-permute-start.51 = (bf16[2,128,256]{2,1,0:T(8,128)(2,1)S(1)}, bf16[2,128,256]{2,1,0:T(8,128)(2,1)S(1)}, u32[]{:S(2)}, u32[]{:S(2)}) collective-permute-start(bf16[2,128,256]{2,1,0:T(8,128)(2,1)S(1)} %get-tuple-element.143), channel_id=1, source_target_pairs={{0,3},{1,2},{2,1},{3,0},{4,7},{5,6},{6,5},{7,4},{8,11},{9,10},{10,... | collective-permute-start | bytes 393224 | tf_op jit(solution)/shard_map/ppermute | solution.py:32
  212.1 1.6 unpack.2
  213.7 9.5 %collective-permute-done.50.refs_6_ = bf16[2,128,256]{2,1,0:T(8,128)(2,1)S(1)} collective-permute-done((bf16[2,128,256]{2,1,0:T(8,128)(2,1)S(1)}, bf16[2,128,256]{2,1,0:T(8,128)(2,1)S(1)}, u32[]{:S(2)}, u32[]{:S(2)}) %collective-permute-start.50) | collective-permute-done | bytes 131104 | tf_op jit(solution)/shard_map/ppermute | solution.py:32
  (107 shorter events, 41.7 us)
Async XLA Ops:
  8.8 19.9 %collective-permute-start.3 = (bf16[2,128,256]{2,1,0:T(8,128)(2,1)S(1)}, bf16[2,128,256]{2,1,0:T(8,128)(2,1)S(1)}, u32[]{:S(2)}, u32[]{:S(2)}) collective-permute-start(bf16[2,128,256]{2,1,0:T(8,128)(2,1)S(1)} %get-tuple-element.81), channel_id=1, source_target_pairs={{0,1},{1,0},{2,3},{3,2},{4,5},{5,4},{6,7},{7,6},{8,9},{9,8},{10,11... | collective-permute-start | bytes 393224 | tf_op jit(solution)/shard_map/ppermute | solution.py:32
  9.8 20.5 %collective-permute-start.4 = (bf16[2,128,256]{2,1,0:T(8,128)(2,1)S(1)}, bf16[2,128,256]{2,1,0:T(8,128)(2,1)S(1)}, u32[]{:S(2)}, u32[]{:S(2)}) collective-permute-start(bf16[2,128,256]{2,1,0:T(8,128)(2,1)S(1)} %get-tuple-element.82), channel_id=1, source_target_pairs={{0,2},{1,3},{2,0},{3,1},{4,6},{5,7},{6,4},{7,5},{8,10},{9,11},{10,... | collective-permute-start | bytes 393224 | tf_op jit(solution)/shard_map/ppermute | solution.py:32
  19.0 26.6 %collective-permute-start.16 = (bf16[4,128,256]{2,1,0:T(8,128)(2,1)S(1)}, bf16[4,128,256]{2,1,0:T(8,128)(2,1)S(1)}, u32[]{:S(2)}, u32[]{:S(2)}) collective-permute-start(bf16[4,128,256]{2,1,0:T(8,128)(2,1)S(1)} %get-tuple-element.97), channel_id=1, source_target_pairs={{0,1},{1,0},{2,3},{3,2},{4,5},{5,4},{6,7},{7,6},{8,9},{9,8},{10,11... | collective-permute-start | bytes 786440 | tf_op jit(solution)/shard_map/ppermute | solution.py:32
  20.4 40.6 %collective-permute-start.17 = (bf16[4,128,256]{2,1,0:T(8,128)(2,1)}, bf16[4,128,256]{2,1,0:T(8,128)(2,1)S(1)}, u32[]{:S(2)}, u32[]{:S(2)}) collective-permute-start(bf16[4,128,256]{2,1,0:T(8,128)(2,1)} %get-tuple-element.98), channel_id=1, source_target_pairs={{0,2},{1,3},{2,0},{3,1},{4,6},{5,7},{6,4},{7,5},{8,10},{9,11},{10,... | collective-permute-start | bytes 786440 | tf_op jit(solution)/shard_map/ppermute | solution.py:32
  28.7 32.3 %collective-permute-start.18 = (bf16[4,128,256]{2,1,0:T(8,128)(2,1)}, bf16[4,128,256]{2,1,0:T(8,128)(2,1)S(1)}, u32[]{:S(2)}, u32[]{:S(2)}) collective-permute-start(bf16[4,128,256]{2,1,0:T(8,128)(2,1)} %get-tuple-element.99), channel_id=1, source_target_pairs={{0,3},{1,2},{2,1},{3,0},{4,7},{5,6},{6,5},{7,4},{8,11},{9,10},{10,... | collective-permute-start | bytes 786440 | tf_op jit(solution)/shard_map/ppermute | solution.py:32
  30.3 32.3 %collective-permute-start = (bf16[4,128,256]{2,1,0:T(8,128)(2,1)}, bf16[4,128,256]{2,1,0:T(8,128)(2,1)S(1)}, u32[]{:S(2)}, u32[]{:S(2)}) collective-permute-start(bf16[4,128,256]{2,1,0:T(8,128)(2,1)} %get-tuple-element.77), channel_id=1, source_target_pairs={{0,1},{1,0},{2,3},{3,2},{4,5},{5,4},{6,7},{7,6},{8,9},{9,8},{10,11... | collective-permute-start | bytes 786440 | tf_op jit(solution)/shard_map/ppermute | solution.py:32
  30.3 42.0 %collective-permute-start.1 = (bf16[4,128,256]{2,1,0:T(8,128)(2,1)}, bf16[4,128,256]{2,1,0:T(8,128)(2,1)S(1)}, u32[]{:S(2)}, u32[]{:S(2)}) collective-permute-start(bf16[4,128,256]{2,1,0:T(8,128)(2,1)} %get-tuple-element.78), channel_id=1, source_target_pairs={{0,2},{1,3},{2,0},{3,1},{4,6},{5,7},{6,4},{7,5},{8,10},{9,11},{10,... | collective-permute-start | bytes 786440 | tf_op jit(solution)/shard_map/ppermute | solution.py:32
  45.6 28.2 %collective-permute-start.2 = (bf16[4,128,256]{2,1,0:T(8,128)(2,1)S(1)}, bf16[4,128,256]{2,1,0:T(8,128)(2,1)S(1)}, u32[]{:S(2)}, u32[]{:S(2)}) collective-permute-start(bf16[4,128,256]{2,1,0:T(8,128)(2,1)S(1)} %get-tuple-element.79), channel_id=1, source_target_pairs={{0,3},{1,2},{2,1},{3,0},{4,7},{5,6},{6,5},{7,4},{8,11},{9,10},{10,... | collective-permute-start | bytes 786440 | tf_op jit(solution)/shard_map/ppermute | solution.py:32
  72.3 19.5 %collective-permute-start.9 = (bf16[2,2,128,256]{3,2,1,0:T(8,128)(2,1)S(1)}, bf16[2,2,128,256]{3,2,1,0:T(8,128)(2,1)S(1)}, u32[]{:S(2)}, u32[]{:S(2)}) collective-permute-start(bf16[2,2,128,256]{3,2,1,0:T(8,128)(2,1)S(1)} %get-tuple-element.88), channel_id=1, source_target_pairs={{0,16},{4,20},{8,24},{12,28},{16,0},{20,4},{24,8},{28,12},{1,17},{... | collective-permute-start | bytes 786440 | tf_op jit(solution)/shard_map/ppermute | solution.py:32
  73.8 20.7 %collective-permute-start.10 = (bf16[2,2,128,256]{3,2,1,0:T(8,128)(2,1)S(1)}, bf16[2,2,128,256]{3,2,1,0:T(8,128)(2,1)S(1)}, u32[]{:S(2)}, u32[]{:S(2)}) collective-permute-start(bf16[2,2,128,256]{3,2,1,0:T(8,128)(2,1)S(1)} %get-tuple-element.89), channel_id=1, source_target_pairs={{0,20},{4,16},{8,28},{12,24},{16,4},{20,0},{24,12},{28,8},{1,21},{... | collective-permute-start | bytes 786440 | tf_op jit(solution)/shard_map/ppermute | solution.py:32
  75.1 21.6 %collective-permute-start.11 = (bf16[2,2,128,256]{3,2,1,0:T(8,128)(2,1)S(1)}, bf16[2,2,128,256]{3,2,1,0:T(8,128)(2,1)S(1)}, u32[]{:S(2)}, u32[]{:S(2)}) collective-permute-start(bf16[2,2,128,256]{3,2,1,0:T(8,128)(2,1)S(1)} %get-tuple-element.90), channel_id=1, source_target_pairs={{0,24},{4,28},{8,16},{12,20},{16,8},{20,12},{24,0},{28,4},{1,25},{... | collective-permute-start | bytes 786440 | tf_op jit(solution)/shard_map/ppermute | solution.py:32
  76.7 21.2 %collective-permute-start.12 = (bf16[2,2,128,256]{3,2,1,0:T(8,128)(2,1)S(1)}, bf16[2,2,128,256]{3,2,1,0:T(8,128)(2,1)S(1)}, u32[]{:S(2)}, u32[]{:S(2)}) collective-permute-start(bf16[2,2,128,256]{3,2,1,0:T(8,128)(2,1)S(1)} %get-tuple-element.91), channel_id=1, source_target_pairs={{0,28},{4,24},{8,20},{12,16},{16,12},{20,8},{24,4},{28,0},{1,29},{... | collective-permute-start | bytes 786440 | tf_op jit(solution)/shard_map/ppermute | solution.py:32
  78.1 19.8 %collective-permute-start.22 = (bf16[2,2,128,256]{3,2,1,0:T(8,128)(2,1)S(1)}, bf16[2,2,128,256]{3,2,1,0:T(8,128)(2,1)S(1)}, u32[]{:S(2)}, u32[]{:S(2)}) collective-permute-start(bf16[2,2,128,256]{3,2,1,0:T(8,128)(2,1)S(1)} %get-tuple-element.105), channel_id=1, source_target_pairs={{0,4},{4,0},{8,12},{12,8},{16,20},{20,16},{24,28},{28,24},{1,5},{5... | collective-permute-start | bytes 786440 | tf_op jit(solution)/shard_map/ppermute | solution.py:32
  96.7 20.4 %collective-permute-start.25 = (bf16[2,2,128,256]{3,2,1,0:T(8,128)(2,1)S(1)}, bf16[2,2,128,256]{3,2,1,0:T(8,128)(2,1)S(1)}, u32[]{:S(2)}, u32[]{:S(2)}) collective-permute-start(bf16[2,2,128,256]{3,2,1,0:T(8,128)(2,1)S(1)} %get-tuple-element.108), channel_id=1, source_target_pairs={{0,16},{4,20},{8,24},{12,28},{16,0},{20,4},{24,8},{28,12},{1,17},{... | collective-permute-start | bytes 786440 | tf_op jit(solution)/shard_map/ppermute | solution.py:32
  97.9 21.7 %collective-permute-start.26 = (bf16[2,2,128,256]{3,2,1,0:T(8,128)(2,1)S(1)}, bf16[2,2,128,256]{3,2,1,0:T(8,128)(2,1)S(1)}, u32[]{:S(2)}, u32[]{:S(2)}) collective-permute-start(bf16[2,2,128,256]{3,2,1,0:T(8,128)(2,1)S(1)} %get-tuple-element.109), channel_id=1, source_target_pairs={{0,20},{4,16},{8,28},{12,24},{16,4},{20,0},{24,12},{28,8},{1,21},{... | collective-permute-start | bytes 786440 | tf_op jit(solution)/shard_map/ppermute | solution.py:32
  97.9 23.1 %collective-permute-start.27 = (bf16[2,2,128,256]{3,2,1,0:T(8,128)(2,1)S(1)}, bf16[2,2,128,256]{3,2,1,0:T(8,128)(2,1)S(1)}, u32[]{:S(2)}, u32[]{:S(2)}) collective-permute-start(bf16[2,2,128,256]{3,2,1,0:T(8,128)(2,1)S(1)} %get-tuple-element.110), channel_id=1, source_target_pairs={{0,24},{4,28},{8,16},{12,20},{16,8},{20,12},{24,0},{28,4},{1,25},{... | collective-permute-start | bytes 786440 | tf_op jit(solution)/shard_map/ppermute | solution.py:32
  99.1 23.2 %collective-permute-start.28 = (bf16[2,2,128,256]{3,2,1,0:T(8,128)(2,1)S(1)}, bf16[2,2,128,256]{3,2,1,0:T(8,128)(2,1)S(1)}, u32[]{:S(2)}, u32[]{:S(2)}) collective-permute-start(bf16[2,2,128,256]{3,2,1,0:T(8,128)(2,1)S(1)} %get-tuple-element.111), channel_id=1, source_target_pairs={{0,28},{4,24},{8,20},{12,16},{16,12},{20,8},{24,4},{28,0},{1,29},{... | collective-permute-start | bytes 786440 | tf_op jit(solution)/shard_map/ppermute | solution.py:32
  131.8 19.4 %collective-permute-start.36 = (bf16[2,2,128,256]{3,2,1,0:T(8,128)(2,1)S(1)}, bf16[2,2,128,256]{3,2,1,0:T(8,128)(2,1)S(1)}, u32[]{:S(2)}, u32[]{:S(2)}) collective-permute-start(bf16[2,2,128,256]{3,2,1,0:T(8,128)(2,1)S(1)} %get-tuple-element.125), channel_id=1, source_target_pairs={{0,20},{4,16},{8,28},{12,24},{16,4},{20,0},{24,12},{28,8},{1,21},{... | collective-permute-start | bytes 786440 | tf_op jit(solution)/shard_map/ppermute | solution.py:32
  133.1 19.6 %collective-permute-start.37 = (bf16[2,2,128,256]{3,2,1,0:T(8,128)(2,1)S(1)}, bf16[2,2,128,256]{3,2,1,0:T(8,128)(2,1)S(1)}, u32[]{:S(2)}, u32[]{:S(2)}) collective-permute-start(bf16[2,2,128,256]{3,2,1,0:T(8,128)(2,1)S(1)} %get-tuple-element.126), channel_id=1, source_target_pairs={{0,24},{4,28},{8,16},{12,20},{16,8},{20,12},{24,0},{28,4},{1,25},{... | collective-permute-start | bytes 786440 | tf_op jit(solution)/shard_map/ppermute | solution.py:32
  134.7 19.1 %collective-permute-start.38 = (bf16[2,2,128,256]{3,2,1,0:T(8,128)(2,1)S(1)}, bf16[2,2,128,256]{3,2,1,0:T(8,128)(2,1)S(1)}, u32[]{:S(2)}, u32[]{:S(2)}) collective-permute-start(bf16[2,2,128,256]{3,2,1,0:T(8,128)(2,1)S(1)} %get-tuple-element.127), channel_id=1, source_target_pairs={{0,28},{4,24},{8,20},{12,16},{16,12},{20,8},{24,4},{28,0},{1,29},{... | collective-permute-start | bytes 786440 | tf_op jit(solution)/shard_map/ppermute | solution.py:32
  136.2 19.0 %collective-permute-start.43 = (bf16[2,2,128,256]{3,2,1,0:T(8,128)(2,1)S(1)}, bf16[2,2,128,256]{3,2,1,0:T(8,128)(2,1)S(1)}, u32[]{:S(2)}, u32[]{:S(2)}) collective-permute-start(bf16[2,2,128,256]{3,2,1,0:T(8,128)(2,1)S(1)} %get-tuple-element.134), channel_id=1, source_target_pairs={{0,8},{4,12},{8,0},{12,4},{16,24},{20,28},{24,16},{28,20},{1,9},{5... | collective-permute-start | bytes 786440 | tf_op jit(solution)/shard_map/ppermute | solution.py:32
  152.7 20.4 %collective-permute-start.45 = (bf16[2,2,128,256]{3,2,1,0:T(8,128)(2,1)S(1)}, bf16[2,2,128,256]{3,2,1,0:T(8,128)(2,1)S(1)}, u32[]{:S(2)}, u32[]{:S(2)}) collective-permute-start(bf16[2,2,128,256]{3,2,1,0:T(8,128)(2,1)S(1)} %get-tuple-element.136), channel_id=1, source_target_pairs={{0,16},{4,20},{8,24},{12,28},{16,0},{20,4},{24,8},{28,12},{1,17},{... | collective-permute-start | bytes 786440 | tf_op jit(solution)/shard_map/ppermute | solution.py:32
  153.9 22.3 %collective-permute-start.46 = (bf16[2,2,128,256]{3,2,1,0:T(8,128)(2,1)S(1)}, bf16[2,2,128,256]{3,2,1,0:T(8,128)(2,1)S(1)}, u32[]{:S(2)}, u32[]{:S(2)}) collective-permute-start(bf16[2,2,128,256]{3,2,1,0:T(8,128)(2,1)S(1)} %get-tuple-element.137), channel_id=1, source_target_pairs={{0,20},{4,16},{8,28},{12,24},{16,4},{20,0},{24,12},{28,8},{1,21},{... | collective-permute-start | bytes 786440 | tf_op jit(solution)/shard_map/ppermute | solution.py:32
  153.9 26.0 %collective-permute-start.47 = (bf16[2,2,128,256]{3,2,1,0:T(8,128)(2,1)S(1)}, bf16[2,2,128,256]{3,2,1,0:T(8,128)(2,1)S(1)}, u32[]{:S(2)}, u32[]{:S(2)}) collective-permute-start(bf16[2,2,128,256]{3,2,1,0:T(8,128)(2,1)S(1)} %get-tuple-element.138), channel_id=1, source_target_pairs={{0,24},{4,28},{8,16},{12,20},{16,8},{20,12},{24,0},{28,4},{1,25},{... | collective-permute-start | bytes 786440 | tf_op jit(solution)/shard_map/ppermute | solution.py:32
  155.2 27.8 %collective-permute-start.48 = (bf16[2,2,128,256]{3,2,1,0:T(8,128)(2,1)S(1)}, bf16[2,2,128,256]{3,2,1,0:T(8,128)(2,1)S(1)}, u32[]{:S(2)}, u32[]{:S(2)}) collective-permute-start(bf16[2,2,128,256]{3,2,1,0:T(8,128)(2,1)S(1)} %get-tuple-element.139), channel_id=1, source_target_pairs={{0,28},{4,24},{8,20},{12,16},{16,12},{20,8},{24,4},{28,0},{1,29},{... | collective-permute-start | bytes 786440 | tf_op jit(solution)/shard_map/ppermute | solution.py:32
  159.4 25.5 %collective-permute-start.15 = (bf16[4,128,256]{2,1,0:T(8,128)(2,1)S(1)}, bf16[4,128,256]{2,1,0:T(8,128)(2,1)S(1)}, u32[]{:S(2)}, u32[]{:S(2)}) collective-permute-start(bf16[4,128,256]{2,1,0:T(8,128)(2,1)S(1)} %get-tuple-element.95), channel_id=1, source_target_pairs={{0,3},{1,2},{2,1},{3,0},{4,7},{5,6},{6,5},{7,4},{8,11},{9,10},{10,... | collective-permute-start | bytes 786440 | tf_op jit(solution)/shard_map/ppermute | solution.py:32
  176.2 27.3 %collective-permute-start.30 = (bf16[4,128,256]{2,1,0:T(8,128)(2,1)S(1)}, bf16[4,128,256]{2,1,0:T(8,128)(2,1)S(1)}, u32[]{:S(2)}, u32[]{:S(2)}) collective-permute-start(bf16[4,128,256]{2,1,0:T(8,128)(2,1)S(1)} %get-tuple-element.114), channel_id=1, source_target_pairs={{0,2},{1,3},{2,0},{3,1},{4,6},{5,7},{6,4},{7,5},{8,10},{9,11},{10,... | collective-permute-start | bytes 786440 | tf_op jit(solution)/shard_map/ppermute | solution.py:32
  179.9 23.7 %collective-permute-start.31 = (bf16[4,128,256]{2,1,0:T(8,128)(2,1)S(1)}, bf16[4,128,256]{2,1,0:T(8,128)(2,1)S(1)}, u32[]{:S(2)}, u32[]{:S(2)}) collective-permute-start(bf16[4,128,256]{2,1,0:T(8,128)(2,1)S(1)} %get-tuple-element.115), channel_id=1, source_target_pairs={{0,3},{1,2},{2,1},{3,0},{4,7},{5,6},{6,5},{7,4},{8,11},{9,10},{10,... | collective-permute-start | bytes 786440 | tf_op jit(solution)/shard_map/ppermute | solution.py:32
  183.0 26.8 %collective-permute-start.39 = (bf16[2,128,256]{2,1,0:T(8,128)(2,1)S(1)}, bf16[2,128,256]{2,1,0:T(8,128)(2,1)S(1)}, u32[]{:S(2)}, u32[]{:S(2)}) collective-permute-start(bf16[2,128,256]{2,1,0:T(8,128)(2,1)S(1)} %get-tuple-element.129), channel_id=1, source_target_pairs={{0,1},{1,0},{2,3},{3,2},{4,5},{5,4},{6,7},{7,6},{8,9},{9,8},{10,11... | collective-permute-start | bytes 393224 | tf_op jit(solution)/shard_map/ppermute | solution.py:32
  184.9 28.8 %collective-permute-start.40 = (bf16[2,128,256]{2,1,0:T(8,128)(2,1)S(1)}, bf16[2,128,256]{2,1,0:T(8,128)(2,1)S(1)}, u32[]{:S(2)}, u32[]{:S(2)}) collective-permute-start(bf16[2,128,256]{2,1,0:T(8,128)(2,1)S(1)} %get-tuple-element.130), channel_id=1, source_target_pairs={{0,2},{1,3},{2,0},{3,1},{4,6},{5,7},{6,4},{7,5},{8,10},{9,11},{10,... | collective-permute-start | bytes 393224 | tf_op jit(solution)/shard_map/ppermute | solution.py:32
  188.1 25.6 %collective-permute-start.41 = (bf16[2,128,256]{2,1,0:T(8,128)(2,1)S(1)}, bf16[2,128,256]{2,1,0:T(8,128)(2,1)S(1)}, u32[]{:S(2)}, u32[]{:S(2)}) collective-permute-start(bf16[2,128,256]{2,1,0:T(8,128)(2,1)S(1)} %get-tuple-element.131), channel_id=1, source_target_pairs={{0,3},{1,2},{2,1},{3,0},{4,7},{5,6},{6,5},{7,4},{8,11},{9,10},{10,... | collective-permute-start | bytes 393224 | tf_op jit(solution)/shard_map/ppermute | solution.py:32
  203.6 19.7 %collective-permute-start.50 = (bf16[2,128,256]{2,1,0:T(8,128)(2,1)S(1)}, bf16[2,128,256]{2,1,0:T(8,128)(2,1)S(1)}, u32[]{:S(2)}, u32[]{:S(2)}) collective-permute-start(bf16[2,128,256]{2,1,0:T(8,128)(2,1)S(1)} %get-tuple-element.142), channel_id=1, source_target_pairs={{0,2},{1,3},{2,0},{3,1},{4,6},{5,7},{6,4},{7,5},{8,10},{9,11},{10,... | collective-permute-start | bytes 393224 | tf_op jit(solution)/shard_map/ppermute | solution.py:32
  (31 other events, 316.5 us)

commit v2 on v1

--- a/solution.py
+++ b/solution.py
@@ -11,6 +11,7 @@
 HD = 128
 BLK = 256
 SEL = 4
+STATS = 16
 CHUNKS = 2
 
 MASKED = -1e30
@@ -93,7 +94,7 @@
         compiler_params=grant(1),
         cost_estimate=cost(2 * k * n * plan.rows * plan.width * 2),
         name="pack",
-    )(*arrays)
+    )(*(pltpu.with_memory_space_constraint(x, pltpu.HBM) for x in arrays))
 
 
 def unpack(plan, pieces, k):
@@ -168,12 +169,37 @@
     return lax.dot_general(a, b, (((ca,), (cb,)), ((), ())), preferred_element_type=F32)
 
 
+def stat_rows(*vectors):
+    pieces = []
+    for v in vectors:
+        for _ in range(3):
+            piece = v.astype(BF)
+            v = v - piece.astype(F32)
+            pieces += [piece.astype(F32)[:, i : i + HD] for i in range(0, BLK, HD)]
+    pieces.append(jnp.zeros((STATS - len(pieces), HD), F32))
+    return jnp.concatenate(pieces, 0).astype(BF)
+
+
+def read_stats(rows, count):
+    rows, wide, vectors = rows.astype(F32), BLK // HD, []
+    for v in range(count):
+        at = v * 3 * wide
+        parts = [
+            rows[at + i : at + i + 1]
+            + rows[at + wide + i : at + wide + i + 1]
+            + rows[at + 2 * wide + i : at + 2 * wide + i + 1]
+            for i in range(wide)
+        ]
+        vectors.append(jnp.concatenate(parts, 1))
+    return vectors
+
+
 def attend(plan, noisy, tiles, lists):
     n, per, slots, rows, bh = plan.n, plan.per, plan.ctx, plan.rows, plan.bh
     heads = plan.width // HD
     scale = 1.0 / math.sqrt(HD)
     log2e = 1.0 / math.log(2.0)
-    side = (4, rows, plan.width)
+    side = (2 * rows + STATS, plan.width)
 
     def body(*refs):
         lists_ref, rows_in, tile_refs = refs[0], refs[1 : 1 + n], refs[1 + n : 1 + n + slots]
@@ -196,7 +222,7 @@
                 def put_noisy(j, value):
                     value = value.astype(BF).reshape(per, rows, HD)
                     for p in range(per):
-                        rows_out[b * per + p][j, :, cols] = value[p]
+                        rows_out[b * per + p][j * rows : (j + 1) * rows, cols] = value[p]
 
                 def clean_block(slot, kv):
                     return tiles_in[slot, kv, :, :, cols].reshape(BLK, HD)
@@ -227,6 +253,7 @@
                     jnp.add, [jnp.sum(w, axis=0, keepdims=True) for w in weights]
                 )
                 inverse = 1.0 / total
+                log_total = top + jnp.log(total) * log2e
                 probs = [w * inverse for w in weights]
                 probs_bf = [p.astype(BF) for p in probs]
                 out_t = functools.reduce(
@@ -235,18 +262,16 @@
                 out_bf = out_t.astype(BF)
                 put_noisy(0, out_bf.T)
                 delta = jnp.sum(g.T.astype(F32) * out_bf.astype(F32), axis=0, keepdims=True)
+                stats = stat_rows(log_total, delta)
+                for p in range(per):
+                    rows_out[b * per + p][2 * rows :, cols] = stats
                 dq_t = jnp.zeros((HD, BLK), F32)
                 for t in range(1 + SEL):
                     ds = (probs[t] * (dot(values[t], g, 1, 1) - delta)).astype(BF)
                     dq_t = dq_t + dot(keys[t].T, ds, 1, 0)
-                    kterm = dot(ds, q, 1, 0) * scale
-                    vterm = dot(probs_bf[t], g, 1, 0)
-                    if t == 0:
-                        put_noisy(2, kterm)
-                        put_noisy(3, vterm)
-                    else:
-                        put_clean(target[t - 1], 0, kterm)
-                        put_clean(target[t - 1], 1, vterm)
+                    if t > 0:
+                        put_clean(target[t - 1], 0, dot(ds, q, 1, 0) * scale)
+                        put_clean(target[t - 1], 1, dot(probs_bf[t], g, 1, 0))
                 put_noisy(1, (dq_t * scale).astype(BF).T)
             return carry
 
@@ -310,6 +335,76 @@
     )(lists, *on_chip(terms))
 
 
+def finish(plan, sides, query, grad, key, value):
+    n, per, rows, chunks = plan.n, plan.per, plan.rows, plan.chunks
+    flat = [p for chunk in sides for p in chunk]
+    heads = plan.width // HD
+    scale = 1.0 / math.sqrt(HD)
+    log2e = 1.0 / math.log(2.0)
+
+    def body(*refs):
+        ins, at = refs[: n * chunks], n * chunks
+        q_refs, g_refs = refs[at : at + per], refs[at + per : at + 2 * per]
+        k_ref, v_ref = refs[at + 2 * per : at + 2 * per + 2]
+        outs = refs[at + 2 * per + 2 : at + 2 * per + 6]
+        dk_buf, dv_buf, sem, sem_own = refs[at + 2 * per + 6 :]
+        z = lax.axis_index("head")
+        moves = [
+            pltpu.make_async_copy(
+                ins[c * n + m].at[pl.ds(j * rows, rows), :],
+                outs[j].at[:, plan.cols(z, m, c)],
+                sem.at[c * n + m, j],
+            )
+            for c in range(chunks)
+            for m in range(n)
+            for j in range(2)
+        ]
+        for move in moves:
+            move.start()
+        for c in range(chunks):
+            for m in range(n):
+                order = [p ^ (m % per) for p in range(per)]
+                start = (z ^ m) * plan.group + c * plan.width
+                for h in range(heads):
+                    cols = pl.ds(pl.multiple_of(start + h * HD, HD), HD)
+                    q = jnp.concatenate([q_refs[p][:, cols] for p in order], 0)
+                    g = jnp.concatenate([g_refs[p][:, cols] for p in order], 0)
+                    log_total, delta = read_stats(
+                        ins[c * n + m][2 * rows :, h * HD : (h + 1) * HD], 2
+                    )
+                    s = dot(k_ref[:, cols], q, 1, 1) * (scale * log2e)
+                    prob = jnp.exp2(s - log_total)
+                    ds = prob * (dot(v_ref[:, cols], g, 1, 1) - delta)
+                    dk_buf[:, cols] = (dot(ds.astype(BF), q, 1, 0) * scale).astype(BF)
+                    dv_buf[:, cols] = dot(prob.astype(BF), g, 1, 0).astype(BF)
+        own = [
+            pltpu.make_async_copy(dk_buf, outs[2], sem_own.at[0]),
+            pltpu.make_async_copy(dv_buf, outs[3], sem_own.at[1]),
+        ]
+        run_all(own)
+        for move in moves:
+            move.wait()
+
+    shape = (rows, plan.features)
+    return pl.pallas_call(
+        body,
+        out_shape=[jax.ShapeDtypeStruct(shape, BF)] * 4,
+        in_specs=[VMEM] * (len(flat) + 2 * per + 2),
+        out_specs=[HBM] * 4,
+        scratch_shapes=[
+            pltpu.VMEM(shape, BF),
+            pltpu.VMEM(shape, BF),
+            pltpu.SemaphoreType.DMA((len(flat), 2)),
+            pltpu.SemaphoreType.DMA((2,)),
+        ],
+        compiler_params=grant(6),
+        cost_estimate=cost(
+            12 * rows * plan.features * 2, 4 * 2 * rows * BLK * plan.features, rows * BLK * 16
+        ),
+        name="finish",
+    )(*on_chip(flat), *on_chip(query), *on_chip(grad), *on_chip([key, value]))
+
+
 def slot_order(slots):
     return sorted(range(1, slots), key=lambda s: (-bin(s >> 1).count("1"), s >> 1 == 0, s))
 
@@ -340,7 +435,11 @@
         sides.append(over_head(side))
         terms = over_ctx(terms)
         sums.append(over_head(total_terms(plan, terms, lists)))
-    return (*unpack(plan, sides, 4), *unpack(plan, sums, 2))
+    masks = range(plan.per)
+    block_q = [query if m == 0 else swap(query, "head", m) for m in masks]
+    block_g = [grad if m == 0 else swap(grad, "head", m) for m in masks]
+    rows = finish(plan, sides, block_q, block_g, key, value)
+    return (*rows, *unpack(plan, sums, 2))
 
 
 def solution(mesh):

time: 226 us -> 227 us (level)
  starting transfers between devices: 95.4 us -> 80.8 us
  waiting for transfers between devices: 95.1 us -> 109 us
  Pallas kernels: 28.5 us -> 34.7 us
  local copies, waits for them, and re-layouts: 4.42 us -> 0.11 us
    ppermute x52 -> x54, starting transfers between devices: 95.4 us -> 80.8 us  [swap(): return lax.ppermute(x, axis, [(i, i ^ mask) for i in range(count)])]
    ppermute x52 -> x54, waiting for transfers between devices: 95.1 us -> 109 us  [swap(): return lax.ppermute(x, axis, [(i, i ^ mask) for i in range(count)])]
    pallas_call x0 -> x1, Pallas kernels: none -> 4.34 us  [finish(): pl.pallas_call(body, out_shape=[jax.ShapeDtypeStruct(shape, BF)] * 4, in_...]
    unnamed x23 -> x11, local copies, waits for them, and re-layouts: 4.42 us -> 0.11 us
    pallas_call x4, Pallas kernels: 2.59 us -> 6.63 us  [pack(): pl.pallas_call(body, out_shape=[pltpu.VMEM(shape, BF)] * n, in_specs=[HBM...]
  transfers between devices with their start and end apart: 52 -> 54, of which waited for: 11 -> 15; matrix products, arithmetic and copies ran while one was open for 0% -> 0% of each run, Pallas kernels for 12% -> 14%
where the time goes in v2:
time: 227 us; the launch traced here: 226 us
  waiting for transfers between devices  109 us (48%)
  starting transfers between devices  80.8 us (36%)
  Pallas kernels  34.7 us (15%)
    ppermute x54, waiting for transfers between devices, swap(): return lax.ppermute(x, axis, [(i, i ^ mask) for i in range(count)])  109 us
    ppermute x54, starting transfers between devices, swap(): return lax.ppermute(x, axis, [(i, i ^ mask) for i in range(count)])  80.8 us
    pallas_call x2, Pallas kernels, attend(): pl.pallas_call(body, out_shape=[pltpu.VMEM(side, BF)] * n + [pltpu.VMEM(p...  16.7 us
    pallas_call x4, Pallas kernels, pack(): pl.pallas_call(body, out_shape=[pltpu.VMEM(shape, BF)] * n, in_specs=[HBM...  6.63 us
  transfers between devices with their start and end apart: 54, of which 15 were waited for; matrix products, arithmetic and copies ran while one was open for 0% of the time, Pallas kernels for 14%

profile of v2, /device:TPU:0, one launch (start us, length us, event | category | flops | bytes accessed | tf_op | source)
XLA Modules:
  0.0 226.1 jit_solution(17293456207772775323)
XLA Ops:
  1.8 3.1 %collective-permute-start.19 = (bf16[2,128,256]{2,1,0:T(8,128)(2,1)S(1)}, bf16[2,128,256]{2,1,0:T(8,128)(2,1)S(1)}, u32[]{:S(2)}, u32[]{:S(2)}) collective-permute-start(bf16[2,128,256]{2,1,0:T(8,128)(2,1)S(1)} %get-tuple-element.101), channel_id=1, source_target_pairs={{0,1},{1,0},{2,3},{3,2},{4,5},{5,4},{6,7},{7,6},{8,9},{9,8},{10,11... | collective-permute-start | bytes 393224 | tf_op jit(solution)/shard_map/ppermute | solution.py:33
  4.9 2.6 %collective-permute-start.20 = (bf16[2,128,256]{2,1,0:T(8,128)(2,1)S(1)}, bf16[2,128,256]{2,1,0:T(8,128)(2,1)S(1)}, u32[]{:S(2)}, u32[]{:S(2)}) collective-permute-start(bf16[2,128,256]{2,1,0:T(8,128)(2,1)S(1)} %get-tuple-element.102), channel_id=1, source_target_pairs={{0,2},{1,3},{2,0},{3,1},{4,6},{5,7},{6,4},{7,5},{8,10},{9,11},{10,... | collective-permute-start | bytes 393224 | tf_op jit(solution)/shard_map/ppermute | solution.py:33
  9.6 3.5 %collective-permute-start.4 = (bf16[2,128,256]{2,1,0:T(8,128)(2,1)S(1)}, bf16[2,128,256]{2,1,0:T(8,128)(2,1)S(1)}, u32[]{:S(2)}, u32[]{:S(2)}) collective-permute-start(bf16[2,128,256]{2,1,0:T(8,128)(2,1)S(1)} %get-tuple-element.82), channel_id=1, source_target_pairs={{0,2},{1,3},{2,0},{3,1},{4,6},{5,7},{6,4},{7,5},{8,10},{9,11},{10,... | collective-permute-start | bytes 393224 | tf_op jit(solution)/shard_map/ppermute | solution.py:33
  13.1 2.2 pack.6
  15.4 2.4 %collective-permute-done.20.refs_3_ = bf16[2,128,256]{2,1,0:T(8,128)(2,1)S(1)} collective-permute-done((bf16[2,128,256]{2,1,0:T(8,128)(2,1)S(1)}, bf16[2,128,256]{2,1,0:T(8,128)(2,1)S(1)}, u32[]{:S(2)}, u32[]{:S(2)}) %collective-permute-start.20) | collective-permute-done | bytes 131104 | tf_op jit(solution)/shard_map/ppermute | solution.py:33
  17.8 2.9 %collective-permute-start.18 = (bf16[4,128,256]{2,1,0:T(8,128)(2,1)S(1)}, bf16[4,128,256]{2,1,0:T(8,128)(2,1)S(1)}, u32[]{:S(2)}, u32[]{:S(2)}) collective-permute-start(bf16[4,128,256]{2,1,0:T(8,128)(2,1)S(1)} %get-tuple-element.99), channel_id=1, source_target_pairs={{0,3},{1,2},{2,1},{3,0},{4,7},{5,6},{6,5},{7,4},{8,11},{9,10},{10,... | collective-permute-start | bytes 786440 | tf_op jit(solution)/shard_map/ppermute | solution.py:33
  20.7 2.2 pack.4
  22.9 4.7 %collective-permute-start = (bf16[4,128,256]{2,1,0:T(8,128)(2,1)}, bf16[4,128,256]{2,1,0:T(8,128)(2,1)S(1)}, u32[]{:S(2)}, u32[]{:S(2)}) collective-permute-start(bf16[4,128,256]{2,1,0:T(8,128)(2,1)} %get-tuple-element.77), channel_id=1, source_target_pairs={{0,1},{1,0},{2,3},{3,2},{4,5},{5,4},{6,7},{7,6},{8,9},{9,8},{10,11... | collective-permute-start | bytes 786440 | tf_op jit(solution)/shard_map/ppermute | solution.py:33
  29.2 18.2 %collective-permute-done.5.refs_4_ = bf16[2,128,256]{2,1,0:T(8,128)(2,1)S(1)} collective-permute-done((bf16[2,128,256]{2,1,0:T(8,128)(2,1)S(1)}, bf16[2,128,256]{2,1,0:T(8,128)(2,1)S(1)}, u32[]{:S(2)}, u32[]{:S(2)}) %collective-permute-start.5) | collective-permute-done | bytes 131104 | tf_op jit(solution)/shard_map/ppermute | solution.py:33
  47.3 7.3 %collective-permute-start.1 = (bf16[4,128,256]{2,1,0:T(8,128)(2,1)}, bf16[4,128,256]{2,1,0:T(8,128)(2,1)S(1)}, u32[]{:S(2)}, u32[]{:S(2)}) collective-permute-start(bf16[4,128,256]{2,1,0:T(8,128)(2,1)} %get-tuple-element.78), channel_id=1, source_target_pairs={{0,2},{1,3},{2,0},{3,1},{4,6},{5,7},{6,4},{7,5},{8,10},{9,11},{10,... | collective-permute-start | bytes 786440 | tf_op jit(solution)/shard_map/ppermute | solution.py:33
  59.2 13.3 %collective-permute-done.1.refs_3_ = bf16[4,128,256]{2,1,0:T(8,128)(2,1)S(1)} collective-permute-done((bf16[4,128,256]{2,1,0:T(8,128)(2,1)}, bf16[4,128,256]{2,1,0:T(8,128)(2,1)S(1)}, u32[]{:S(2)}, u32[]{:S(2)}) %collective-permute-start.1) | collective-permute-done | bytes 262176 | tf_op jit(solution)/shard_map/ppermute | solution.py:33
  78.4 16.5 %collective-permute-done.25.refs_9_ = bf16[2,2,128,256]{3,2,1,0:T(8,128)(2,1)S(1)} collective-permute-done((bf16[2,2,128,256]{3,2,1,0:T(8,128)(2,1)S(1)}, bf16[2,2,128,256]{3,2,1,0:T(8,128)(2,1)S(1)}, u32[]{:S(2)}, u32[]{:S(2)}) %collective-permute-start.25) | collective-permute-done | bytes 262176 | tf_op jit(solution)/shard_map/ppermute | solution.py:33
  94.9 3.2 %collective-permute-start.11 = (bf16[2,2,128,256]{3,2,1,0:T(8,128)(2,1)S(1)}, bf16[2,2,128,256]{3,2,1,0:T(8,128)(2,1)S(1)}, u32[]{:S(2)}, u32[]{:S(2)}) collective-permute-start(bf16[2,2,128,256]{3,2,1,0:T(8,128)(2,1)S(1)} %get-tuple-element.90), channel_id=1, source_target_pairs={{0,24},{4,28},{8,16},{12,20},{16,8},{20,12},{24,0},{28,4},{1,25},{... | collective-permute-start | bytes 786440 | tf_op jit(solution)/shard_map/ppermute | solution.py:33
  98.1 5.0 %collective-permute-done.26.refs_10_ = bf16[2,2,128,256]{3,2,1,0:T(8,128)(2,1)S(1)} collective-permute-done((bf16[2,2,128,256]{3,2,1,0:T(8,128)(2,1)S(1)}, bf16[2,2,128,256]{3,2,1,0:T(8,128)(2,1)S(1)}, u32[]{:S(2)}, u32[]{:S(2)}) %collective-permute-start.26) | collective-permute-done | bytes 262176 | tf_op jit(solution)/shard_map/ppermute | solution.py:33
  103.1 3.1 %collective-permute-start.12 = (bf16[2,2,128,256]{3,2,1,0:T(8,128)(2,1)S(1)}, bf16[2,2,128,256]{3,2,1,0:T(8,128)(2,1)S(1)}, u32[]{:S(2)}, u32[]{:S(2)}) collective-permute-start(bf16[2,2,128,256]{3,2,1,0:T(8,128)(2,1)S(1)} %get-tuple-element.91), channel_id=1, source_target_pairs={{0,28},{4,24},{8,20},{12,16},{16,12},{20,8},{24,4},{28,0},{1,29},{... | collective-permute-start | bytes 786440 | tf_op jit(solution)/shard_map/ppermute | solution.py:33
  106.3 5.3 %collective-permute-done.10.refs_10_ = bf16[2,2,128,256]{3,2,1,0:T(8,128)(2,1)S(1)} collective-permute-done((bf16[2,2,128,256]{3,2,1,0:T(8,128)(2,1)S(1)}, bf16[2,2,128,256]{3,2,1,0:T(8,128)(2,1)S(1)}, u32[]{:S(2)}, u32[]{:S(2)}) %collective-permute-start.10) | collective-permute-done | bytes 262176 | tf_op jit(solution)/shard_map/ppermute | solution.py:33
  111.7 2.7 %collective-permute-start.33 = (bf16[128,2048]{1,0:T(8,128)(2,1)S(1)}, bf16[128,2048]{1,0:T(8,128)(2,1)S(1)}, u32[]{:S(2)}, u32[]{:S(2)}) collective-permute-start(bf16[128,2048]{1,0:T(8,128)(2,1)S(1)} %copy-done.3), channel_id=1, source_target_pairs={{0,1},{1,0},{2,3},{3,2},{4,5},{5,4},{6,7},{7,6},{8,9},{9,8},{10,11... | collective-permute-start | bytes 1572872 | tf_op jit(solution)/shard_map/ppermute | solution.py:33
  116.9 8.4 %attend.3 = (bf16[272,256]{1,0:T(8,128)(2,1)S(1)}, bf16[272,256]{1,0:T(8,128)(2,1)S(1)}, bf16[272,256]{1,0:T(8,128)(2,1)S(1)}, bf16[272,256]{1,0:T(8,128)(2,1)S(...) custom-call(s32[16,4]{1,0:T(8,128)S(1)} %copy.14.refs_0_, ...), custom_call_target="tpu_custom_call" | custom-call | flops 2013265920 | bytes 6291456 | tf_op jit(solution)/shard_map/attend/pallas_call | solution.py:283
  129.7 2.7 %collective-permute-done.33.refs_11_ = bf16[128,2048]{1,0:T(8,128)(2,1)S(1)} collective-permute-done((bf16[128,2048]{1,0:T(8,128)(2,1)S(1)}, bf16[128,2048]{1,0:T(8,128)(2,1)S(1)}, u32[]{:S(2)}, u32[]{:S(2)}) %collective-permute-start.33) | collective-permute-done | bytes 524320 | tf_op jit(solution)/shard_map/ppermute | solution.py:33
  132.4 2.4 %collective-permute-done.29.refs_5_ = bf16[272,256]{1,0:T(8,128)(2,1)S(1)} collective-permute-done((bf16[272,256]{1,0:T(8,128)(2,1)S(1)}, bf16[272,256]{1,0:T(8,128)(2,1)S(1)}, u32[]{:S(2)}, u32[]{:S(2)}) %collective-permute-start.29) | collective-permute-done | bytes 139296 | tf_op jit(solution)/shard_map/ppermute | solution.py:33
  135.6 8.2 %attend.2 = (bf16[272,256]{1,0:T(8,128)(2,1)S(1)}, bf16[272,256]{1,0:T(8,128)(2,1)S(1)}, bf16[272,256]{1,0:T(8,128)(2,1)S(1)}, bf16[272,256]{1,0:T(8,128)(2,1)S(...) custom-call(s32[16,4]{1,0:T(8,128)S(1)} %copy.14.refs_0_, ...), custom_call_target="tpu_custom_call" | custom-call | flops 2013265920 | bytes 6291456 | tf_op jit(solution)/shard_map/attend/pallas_call | solution.py:283
  147.6 16.1 %collective-permute-done.48.refs_6_ = bf16[2,2,128,256]{3,2,1,0:T(8,128)(2,1)S(1)} collective-permute-done((bf16[2,2,128,256]{3,2,1,0:T(8,128)(2,1)S(1)}, bf16[2,2,128,256]{3,2,1,0:T(8,128)(2,1)S(1)}, u32[]{:S(2)}, u32[]{:S(2)}) %collective-permute-start.48) | collective-permute-done | bytes 262176 | tf_op jit(solution)/shard_map/ppermute | solution.py:33
  168.5 3.5 %collective-permute-done.36.refs_4_ = bf16[2,2,128,256]{3,2,1,0:T(8,128)(2,1)S(1)} collective-permute-done((bf16[2,2,128,256]{3,2,1,0:T(8,128)(2,1)S(1)}, bf16[2,2,128,256]{3,2,1,0:T(8,128)(2,1)S(1)}, u32[]{:S(2)}, u32[]{:S(2)}) %collective-permute-start.36) | collective-permute-done | bytes 262176 | tf_op jit(solution)/shard_map/ppermute | solution.py:33
  173.6 10.9 %collective-permute-done.37.refs_5_ = bf16[2,2,128,256]{3,2,1,0:T(8,128)(2,1)S(1)} collective-permute-done((bf16[2,2,128,256]{3,2,1,0:T(8,128)(2,1)S(1)}, bf16[2,2,128,256]{3,2,1,0:T(8,128)(2,1)S(1)}, u32[]{:S(2)}, u32[]{:S(2)}) %collective-permute-start.37) | collective-permute-done | bytes 262176 | tf_op jit(solution)/shard_map/ppermute | solution.py:33
  185.4 3.3 %collective-permute-done.38.refs_6_ = bf16[2,2,128,256]{3,2,1,0:T(8,128)(2,1)S(1)} collective-permute-done((bf16[2,2,128,256]{3,2,1,0:T(8,128)(2,1)S(1)}, bf16[2,2,128,256]{3,2,1,0:T(8,128)(2,1)S(1)}, u32[]{:S(2)}, u32[]{:S(2)}) %collective-permute-start.38) | collective-permute-done | bytes 262176 | tf_op jit(solution)/shard_map/ppermute | solution.py:33
  190.8 2.0 collective-permute-start.15
  196.6 2.4 %collective-permute-start.52 = (bf16[2,128,256]{2,1,0:T(8,128)(2,1)S(1)}, bf16[2,128,256]{2,1,0:T(8,128)(2,1)S(1)}, u32[]{:S(2)}, u32[]{:S(2)}) collective-permute-start(bf16[2,128,256]{2,1,0:T(8,128)(2,1)S(1)} %get-tuple-element.142), channel_id=1, source_target_pairs={{0,2},{1,3},{2,0},{3,1},{4,6},{5,7},{6,4},{7,5},{8,10},{9,11},{10,... | collective-permute-start | bytes 393224 | tf_op jit(solution)/shard_map/ppermute | solution.py:33
  199.0 2.0 collective-permute-start.53
  202.9 8.7 %collective-permute-start.42 = (bf16[2,128,256]{2,1,0:T(8,128)(2,1)S(1)}, bf16[2,128,256]{2,1,0:T(8,128)(2,1)S(1)}, u32[]{:S(2)}, u32[]{:S(2)}) collective-permute-start(bf16[2,128,256]{2,1,0:T(8,128)(2,1)S(1)} %get-tuple-element.130), channel_id=1, source_target_pairs={{0,2},{1,3},{2,0},{3,1},{4,6},{5,7},{6,4},{7,5},{8,10},{9,11},{10,... | collective-permute-start | bytes 393224 | tf_op jit(solution)/shard_map/ppermute | solution.py:33
  211.6 2.2 collective-permute-start.43
  213.8 4.3 %finish.1 = (bf16[128,2048]{1,0:T(8,128)(2,1)}, bf16[128,2048]{1,0:T(8,128)(2,1)}, bf16[128,2048]{1,0:T(8,128)(2,1)}, bf16[128,2048]{1,0:T(8,128)(2,1)}) custom-call(bf16[272,256]{1,0:T(8,128)(2,1)S(1)} %get-tuple-element.92.refs_0_, bf16[272,256]{1,0:T(8,128)(2,1)S(1)} %collective-permute-done.13.refs_1_, ...), custom_call_target="tpu_custom_call" | custom-call | flops 536870912 | bytes 6291456 | tf_op jit(solution)/shard_map/finish/pallas_call | solution.py:389
  218.1 6.7 %collective-permute-done.42.refs_2_ = bf16[2,128,256]{2,1,0:T(8,128)(2,1)S(1)} collective-permute-done((bf16[2,128,256]{2,1,0:T(8,128)(2,1)S(1)}, bf16[2,128,256]{2,1,0:T(8,128)(2,1)S(1)}, u32[]{:S(2)}, u32[]{:S(2)}) %collective-permute-start.42) | collective-permute-done | bytes 131104 | tf_op jit(solution)/shard_map/ppermute | solution.py:33
  (99 shorter events, 43.0 us)
Async XLA Ops:
  9.6 18.1 %collective-permute-start.4 = (bf16[2,128,256]{2,1,0:T(8,128)(2,1)S(1)}, bf16[2,128,256]{2,1,0:T(8,128)(2,1)S(1)}, u32[]{:S(2)}, u32[]{:S(2)}) collective-permute-start(bf16[2,128,256]{2,1,0:T(8,128)(2,1)S(1)} %get-tuple-element.82), channel_id=1, source_target_pairs={{0,2},{1,3},{2,0},{3,1},{4,6},{5,7},{6,4},{7,5},{8,10},{9,11},{10,... | collective-permute-start | bytes 393224 | tf_op jit(solution)/shard_map/ppermute | solution.py:33
  15.3 40.6 %collective-permute-start.16 = (bf16[4,128,256]{2,1,0:T(8,128)(2,1)}, bf16[4,128,256]{2,1,0:T(8,128)(2,1)S(1)}, u32[]{:S(2)}, u32[]{:S(2)}) collective-permute-start(bf16[4,128,256]{2,1,0:T(8,128)(2,1)} %get-tuple-element.97), channel_id=1, source_target_pairs={{0,1},{1,0},{2,3},{3,2},{4,5},{5,4},{6,7},{7,6},{8,9},{9,8},{10,11... | collective-permute-start | bytes 786440 | tf_op jit(solution)/shard_map/ppermute | solution.py:33
  17.8 39.5 %collective-permute-start.17 = (bf16[4,128,256]{2,1,0:T(8,128)(2,1)}, bf16[4,128,256]{2,1,0:T(8,128)(2,1)S(1)}, u32[]{:S(2)}, u32[]{:S(2)}) collective-permute-start(bf16[4,128,256]{2,1,0:T(8,128)(2,1)} %get-tuple-element.98), channel_id=1, source_target_pairs={{0,2},{1,3},{2,0},{3,1},{4,6},{5,7},{6,4},{7,5},{8,10},{9,11},{10,... | collective-permute-start | bytes 786440 | tf_op jit(solution)/shard_map/ppermute | solution.py:33
  17.8 39.5 %collective-permute-start.18 = (bf16[4,128,256]{2,1,0:T(8,128)(2,1)S(1)}, bf16[4,128,256]{2,1,0:T(8,128)(2,1)S(1)}, u32[]{:S(2)}, u32[]{:S(2)}) collective-permute-start(bf16[4,128,256]{2,1,0:T(8,128)(2,1)S(1)} %get-tuple-element.99), channel_id=1, source_target_pairs={{0,3},{1,2},{2,1},{3,0},{4,7},{5,6},{6,5},{7,4},{8,11},{9,10},{10,... | collective-permute-start | bytes 786440 | tf_op jit(solution)/shard_map/ppermute | solution.py:33
  22.9 35.9 %collective-permute-start = (bf16[4,128,256]{2,1,0:T(8,128)(2,1)}, bf16[4,128,256]{2,1,0:T(8,128)(2,1)S(1)}, u32[]{:S(2)}, u32[]{:S(2)}) collective-permute-start(bf16[4,128,256]{2,1,0:T(8,128)(2,1)} %get-tuple-element.77), channel_id=1, source_target_pairs={{0,1},{1,0},{2,3},{3,2},{4,5},{5,4},{6,7},{7,6},{8,9},{9,8},{10,11... | collective-permute-start | bytes 786440 | tf_op jit(solution)/shard_map/ppermute | solution.py:33
  27.7 19.7 %collective-permute-start.5 = (bf16[2,128,256]{2,1,0:T(8,128)(2,1)S(1)}, bf16[2,128,256]{2,1,0:T(8,128)(2,1)S(1)}, u32[]{:S(2)}, u32[]{:S(2)}) collective-permute-start(bf16[2,128,256]{2,1,0:T(8,128)(2,1)S(1)} %get-tuple-element.83), channel_id=1, source_target_pairs={{0,3},{1,2},{2,1},{3,0},{4,7},{5,6},{6,5},{7,4},{8,11},{9,10},{10,... | collective-permute-start | bytes 393224 | tf_op jit(solution)/shard_map/ppermute | solution.py:33
  47.3 25.1 %collective-permute-start.1 = (bf16[4,128,256]{2,1,0:T(8,128)(2,1)}, bf16[4,128,256]{2,1,0:T(8,128)(2,1)S(1)}, u32[]{:S(2)}, u32[]{:S(2)}) collective-permute-start(bf16[4,128,256]{2,1,0:T(8,128)(2,1)} %get-tuple-element.78), channel_id=1, source_target_pairs={{0,2},{1,3},{2,0},{3,1},{4,6},{5,7},{6,4},{7,5},{8,10},{9,11},{10,... | collective-permute-start | bytes 786440 | tf_op jit(solution)/shard_map/ppermute | solution.py:33
  55.9 18.0 %collective-permute-start.2 = (bf16[4,128,256]{2,1,0:T(8,128)(2,1)S(1)}, bf16[4,128,256]{2,1,0:T(8,128)(2,1)S(1)}, u32[]{:S(2)}, u32[]{:S(2)}) collective-permute-start(bf16[4,128,256]{2,1,0:T(8,128)(2,1)S(1)} %get-tuple-element.79), channel_id=1, source_target_pairs={{0,3},{1,2},{2,1},{3,0},{4,7},{5,6},{6,5},{7,4},{8,11},{9,10},{10,... | collective-permute-start | bytes 786440 | tf_op jit(solution)/shard_map/ppermute | solution.py:33
  57.3 18.2 %collective-permute-start.23 = (bf16[2,2,128,256]{3,2,1,0:T(8,128)(2,1)S(1)}, bf16[2,2,128,256]{3,2,1,0:T(8,128)(2,1)S(1)}, u32[]{:S(2)}, u32[]{:S(2)}) collective-permute-start(bf16[2,2,128,256]{3,2,1,0:T(8,128)(2,1)S(1)} %get-tuple-element.106), channel_id=1, source_target_pairs={{0,8},{4,12},{8,0},{12,4},{16,24},{20,28},{24,16},{28,20},{1,9},{5... | collective-permute-start | bytes 786440 | tf_op jit(solution)/shard_map/ppermute | solution.py:33
  58.9 19.1 %collective-permute-start.24 = (bf16[2,2,128,256]{3,2,1,0:T(8,128)(2,1)S(1)}, bf16[2,2,128,256]{3,2,1,0:T(8,128)(2,1)S(1)}, u32[]{:S(2)}, u32[]{:S(2)}) collective-permute-start(bf16[2,2,128,256]{3,2,1,0:T(8,128)(2,1)S(1)} %get-tuple-element.107), channel_id=1, source_target_pairs={{0,12},{4,8},{8,4},{12,0},{16,28},{20,24},{24,20},{28,16},{1,13},{... | collective-permute-start | bytes 786440 | tf_op jit(solution)/shard_map/ppermute | solution.py:33
  72.4 22.5 %collective-permute-start.25 = (bf16[2,2,128,256]{3,2,1,0:T(8,128)(2,1)S(1)}, bf16[2,2,128,256]{3,2,1,0:T(8,128)(2,1)S(1)}, u32[]{:S(2)}, u32[]{:S(2)}) collective-permute-start(bf16[2,2,128,256]{3,2,1,0:T(8,128)(2,1)S(1)} %get-tuple-element.108), channel_id=1, source_target_pairs={{0,16},{4,20},{8,24},{12,28},{16,0},{20,4},{24,8},{28,12},{1,17},{... | collective-permute-start | bytes 786440 | tf_op jit(solution)/shard_map/ppermute | solution.py:33
  73.9 29.2 %collective-permute-start.26 = (bf16[2,2,128,256]{3,2,1,0:T(8,128)(2,1)S(1)}, bf16[2,2,128,256]{3,2,1,0:T(8,128)(2,1)S(1)}, u32[]{:S(2)}, u32[]{:S(2)}) collective-permute-start(bf16[2,2,128,256]{3,2,1,0:T(8,128)(2,1)S(1)} %get-tuple-element.109), channel_id=1, source_target_pairs={{0,20},{4,16},{8,28},{12,24},{16,4},{20,0},{24,12},{28,8},{1,21},{... | collective-permute-start | bytes 786440 | tf_op jit(solution)/shard_map/ppermute | solution.py:33
  74.0 32.3 %collective-permute-start.27 = (bf16[2,2,128,256]{3,2,1,0:T(8,128)(2,1)S(1)}, bf16[2,2,128,256]{3,2,1,0:T(8,128)(2,1)S(1)}, u32[]{:S(2)}, u32[]{:S(2)}) collective-permute-start(bf16[2,2,128,256]{3,2,1,0:T(8,128)(2,1)S(1)} %get-tuple-element.110), channel_id=1, source_target_pairs={{0,24},{4,28},{8,16},{12,20},{16,8},{20,12},{24,0},{28,4},{1,25},{... | collective-permute-start | bytes 786440 | tf_op jit(solution)/shard_map/ppermute | solution.py:33
  75.5 30.8 %collective-permute-start.28 = (bf16[2,2,128,256]{3,2,1,0:T(8,128)(2,1)S(1)}, bf16[2,2,128,256]{3,2,1,0:T(8,128)(2,1)S(1)}, u32[]{:S(2)}, u32[]{:S(2)}) collective-permute-start(bf16[2,2,128,256]{3,2,1,0:T(8,128)(2,1)S(1)} %get-tuple-element.111), channel_id=1, source_target_pairs={{0,28},{4,24},{8,20},{12,16},{16,12},{20,8},{24,4},{28,0},{1,29},{... | collective-permute-start | bytes 786440 | tf_op jit(solution)/shard_map/ppermute | solution.py:33
  78.0 33.6 %collective-permute-start.10 = (bf16[2,2,128,256]{3,2,1,0:T(8,128)(2,1)S(1)}, bf16[2,2,128,256]{3,2,1,0:T(8,128)(2,1)S(1)}, u32[]{:S(2)}, u32[]{:S(2)}) collective-permute-start(bf16[2,2,128,256]{3,2,1,0:T(8,128)(2,1)S(1)} %get-tuple-element.89), channel_id=1, source_target_pairs={{0,20},{4,16},{8,28},{12,24},{16,4},{20,0},{24,12},{28,8},{1,21},{... | collective-permute-start | bytes 786440 | tf_op jit(solution)/shard_map/ppermute | solution.py:33
  94.9 19.4 %collective-permute-start.11 = (bf16[2,2,128,256]{3,2,1,0:T(8,128)(2,1)S(1)}, bf16[2,2,128,256]{3,2,1,0:T(8,128)(2,1)S(1)}, u32[]{:S(2)}, u32[]{:S(2)}) collective-permute-start(bf16[2,2,128,256]{3,2,1,0:T(8,128)(2,1)S(1)} %get-tuple-element.90), channel_id=1, source_target_pairs={{0,24},{4,28},{8,16},{12,20},{16,8},{20,12},{24,0},{28,4},{1,25},{... | collective-permute-start | bytes 786440 | tf_op jit(solution)/shard_map/ppermute | solution.py:33
  106.3 23.4 %collective-permute-start.32 = (bf16[128,2048]{1,0:T(8,128)(2,1)S(1)}, bf16[128,2048]{1,0:T(8,128)(2,1)S(1)}, u32[]{:S(2)}, u32[]{:S(2)}) collective-permute-start(bf16[128,2048]{1,0:T(8,128)(2,1)S(1)} %copy-done), channel_id=1, source_target_pairs={{0,1},{1,0},{2,3},{3,2},{4,5},{5,4},{6,7},{7,6},{8,9},{9,8},{10,11... | collective-permute-start | bytes 1572872 | tf_op jit(solution)/shard_map/ppermute | solution.py:33
  111.7 20.7 %collective-permute-start.33 = (bf16[128,2048]{1,0:T(8,128)(2,1)S(1)}, bf16[128,2048]{1,0:T(8,128)(2,1)S(1)}, u32[]{:S(2)}, u32[]{:S(2)}) collective-permute-start(bf16[128,2048]{1,0:T(8,128)(2,1)S(1)} %copy-done.3), channel_id=1, source_target_pairs={{0,1},{1,0},{2,3},{3,2},{4,5},{5,4},{6,7},{7,6},{8,9},{9,8},{10,11... | collective-permute-start | bytes 1572872 | tf_op jit(solution)/shard_map/ppermute | solution.py:33
  128.2 17.3 %collective-permute-start.45 = (bf16[2,2,128,256]{3,2,1,0:T(8,128)(2,1)S(1)}, bf16[2,2,128,256]{3,2,1,0:T(8,128)(2,1)S(1)}, u32[]{:S(2)}, u32[]{:S(2)}) collective-permute-start(bf16[2,2,128,256]{3,2,1,0:T(8,128)(2,1)S(1)} %get-tuple-element.134), channel_id=1, source_target_pairs={{0,8},{4,12},{8,0},{12,4},{16,24},{20,28},{24,16},{28,20},{1,9},{5... | collective-permute-start | bytes 786440 | tf_op jit(solution)/shard_map/ppermute | solution.py:33
  143.9 19.8 %collective-permute-start.48 = (bf16[2,2,128,256]{3,2,1,0:T(8,128)(2,1)S(1)}, bf16[2,2,128,256]{3,2,1,0:T(8,128)(2,1)S(1)}, u32[]{:S(2)}, u32[]{:S(2)}) collective-permute-start(bf16[2,2,128,256]{3,2,1,0:T(8,128)(2,1)S(1)} %get-tuple-element.137), channel_id=1, source_target_pairs={{0,20},{4,16},{8,28},{12,24},{16,4},{20,0},{24,12},{28,8},{1,21},{... | collective-permute-start | bytes 786440 | tf_op jit(solution)/shard_map/ppermute | solution.py:33
  144.0 20.1 %collective-permute-start.49 = (bf16[2,2,128,256]{3,2,1,0:T(8,128)(2,1)S(1)}, bf16[2,2,128,256]{3,2,1,0:T(8,128)(2,1)S(1)}, u32[]{:S(2)}, u32[]{:S(2)}) collective-permute-start(bf16[2,2,128,256]{3,2,1,0:T(8,128)(2,1)S(1)} %get-tuple-element.138), channel_id=1, source_target_pairs={{0,24},{4,28},{8,16},{12,20},{16,8},{20,12},{24,0},{28,4},{1,25},{... | collective-permute-start | bytes 786440 | tf_op jit(solution)/shard_map/ppermute | solution.py:33
  145.5 18.6 %collective-permute-start.50 = (bf16[2,2,128,256]{3,2,1,0:T(8,128)(2,1)S(1)}, bf16[2,2,128,256]{3,2,1,0:T(8,128)(2,1)S(1)}, u32[]{:S(2)}, u32[]{:S(2)}) collective-permute-start(bf16[2,2,128,256]{3,2,1,0:T(8,128)(2,1)S(1)} %get-tuple-element.139), channel_id=1, source_target_pairs={{0,28},{4,24},{8,20},{12,16},{16,12},{20,8},{24,4},{28,0},{1,29},{... | collective-permute-start | bytes 786440 | tf_op jit(solution)/shard_map/ppermute | solution.py:33
  146.1 19.6 %collective-permute-start.34 = (bf16[2,2,128,256]{3,2,1,0:T(8,128)(2,1)S(1)}, bf16[2,2,128,256]{3,2,1,0:T(8,128)(2,1)S(1)}, u32[]{:S(2)}, u32[]{:S(2)}) collective-permute-start(bf16[2,2,128,256]{3,2,1,0:T(8,128)(2,1)S(1)} %get-tuple-element.121), channel_id=1, source_target_pairs={{0,4},{4,0},{8,12},{12,8},{16,20},{20,16},{24,28},{28,24},{1,5},{5... | collective-permute-start | bytes 786440 | tf_op jit(solution)/shard_map/ppermute | solution.py:33
  147.1 20.0 %collective-permute-start.35 = (bf16[2,2,128,256]{3,2,1,0:T(8,128)(2,1)S(1)}, bf16[2,2,128,256]{3,2,1,0:T(8,128)(2,1)S(1)}, u32[]{:S(2)}, u32[]{:S(2)}) collective-permute-start(bf16[2,2,128,256]{3,2,1,0:T(8,128)(2,1)S(1)} %get-tuple-element.122), channel_id=1, source_target_pairs={{0,8},{4,12},{8,0},{12,4},{16,24},{20,28},{24,16},{28,20},{1,9},{5... | collective-permute-start | bytes 786440 | tf_op jit(solution)/shard_map/ppermute | solution.py:33
  164.1 20.4 %collective-permute-start.37 = (bf16[2,2,128,256]{3,2,1,0:T(8,128)(2,1)S(1)}, bf16[2,2,128,256]{3,2,1,0:T(8,128)(2,1)S(1)}, u32[]{:S(2)}, u32[]{:S(2)}) collective-permute-start(bf16[2,2,128,256]{3,2,1,0:T(8,128)(2,1)S(1)} %get-tuple-element.124), channel_id=1, source_target_pairs={{0,16},{4,20},{8,24},{12,28},{16,0},{20,4},{24,8},{28,12},{1,17},{... | collective-permute-start | bytes 786440 | tf_op jit(solution)/shard_map/ppermute | solution.py:33
  164.1 24.7 %collective-permute-start.38 = (bf16[2,2,128,256]{3,2,1,0:T(8,128)(2,1)S(1)}, bf16[2,2,128,256]{3,2,1,0:T(8,128)(2,1)S(1)}, u32[]{:S(2)}, u32[]{:S(2)}) collective-permute-start(bf16[2,2,128,256]{3,2,1,0:T(8,128)(2,1)S(1)} %get-tuple-element.125), channel_id=1, source_target_pairs={{0,20},{4,16},{8,28},{12,24},{16,4},{20,0},{24,12},{28,8},{1,21},{... | collective-permute-start | bytes 786440 | tf_op jit(solution)/shard_map/ppermute | solution.py:33
  165.7 25.0 %collective-permute-start.39 = (bf16[2,2,128,256]{3,2,1,0:T(8,128)(2,1)S(1)}, bf16[2,2,128,256]{3,2,1,0:T(8,128)(2,1)S(1)}, u32[]{:S(2)}, u32[]{:S(2)}) collective-permute-start(bf16[2,2,128,256]{3,2,1,0:T(8,128)(2,1)S(1)} %get-tuple-element.126), channel_id=1, source_target_pairs={{0,24},{4,28},{8,16},{12,20},{16,8},{20,12},{24,0},{28,4},{1,25},{... | collective-permute-start | bytes 786440 | tf_op jit(solution)/shard_map/ppermute | solution.py:33
  167.1 27.5 %collective-permute-start.40 = (bf16[2,2,128,256]{3,2,1,0:T(8,128)(2,1)S(1)}, bf16[2,2,128,256]{3,2,1,0:T(8,128)(2,1)S(1)}, u32[]{:S(2)}, u32[]{:S(2)}) collective-permute-start(bf16[2,2,128,256]{3,2,1,0:T(8,128)(2,1)S(1)} %get-tuple-element.127), channel_id=1, source_target_pairs={{0,28},{4,24},{8,20},{12,16},{16,12},{20,8},{24,4},{28,0},{1,29},{... | collective-permute-start | bytes 786440 | tf_op jit(solution)/shard_map/ppermute | solution.py:33
  171.9 24.6 %collective-permute-start.31 = (bf16[272,256]{1,0:T(8,128)(2,1)S(1)}, bf16[272,256]{1,0:T(8,128)(2,1)S(1)}, u32[]{:S(2)}, u32[]{:S(2)}) collective-permute-start(bf16[272,256]{1,0:T(8,128)(2,1)S(1)} %get-tuple-element.115), channel_id=1, source_target_pairs={{0,3},{1,2},{2,1},{3,0},{4,7},{5,6},{6,5},{7,4},{8,11},{9,10},{10,... | collective-permute-start | bytes 417800 | tf_op jit(solution)/shard_map/ppermute | solution.py:33
  196.6 21.5 %collective-permute-start.52 = (bf16[2,128,256]{2,1,0:T(8,128)(2,1)S(1)}, bf16[2,128,256]{2,1,0:T(8,128)(2,1)S(1)}, u32[]{:S(2)}, u32[]{:S(2)}) collective-permute-start(bf16[2,128,256]{2,1,0:T(8,128)(2,1)S(1)} %get-tuple-element.142), channel_id=1, source_target_pairs={{0,2},{1,3},{2,0},{3,1},{4,6},{5,7},{6,4},{7,5},{8,10},{9,11},{10,... | collective-permute-start | bytes 393224 | tf_op jit(solution)/shard_map/ppermute | solution.py:33
  199.0 19.1 %collective-permute-start.53 = (bf16[2,128,256]{2,1,0:T(8,128)(2,1)S(1)}, bf16[2,128,256]{2,1,0:T(8,128)(2,1)S(1)}, u32[]{:S(2)}, u32[]{:S(2)}) collective-permute-start(bf16[2,128,256]{2,1,0:T(8,128)(2,1)S(1)} %get-tuple-element.143), channel_id=1, source_target_pairs={{0,3},{1,2},{2,1},{3,0},{4,7},{5,6},{6,5},{7,4},{8,11},{9,10},{10,... | collective-permute-start | bytes 393224 | tf_op jit(solution)/shard_map/ppermute | solution.py:33
  202.9 22.0 %collective-permute-start.42 = (bf16[2,128,256]{2,1,0:T(8,128)(2,1)S(1)}, bf16[2,128,256]{2,1,0:T(8,128)(2,1)S(1)}, u32[]{:S(2)}, u32[]{:S(2)}) collective-permute-start(bf16[2,128,256]{2,1,0:T(8,128)(2,1)S(1)} %get-tuple-element.130), channel_id=1, source_target_pairs={{0,2},{1,3},{2,0},{3,1},{4,6},{5,7},{6,4},{7,5},{8,10},{9,11},{10,... | collective-permute-start | bytes 393224 | tf_op jit(solution)/shard_map/ppermute | solution.py:33
  (27 other events, 463.9 us)

commit v3 on v2

--- a/solution.py
+++ b/solution.py
@@ -13,6 +13,7 @@
 SEL = 4
 STATS = 16
 CHUNKS = 2
+RELAYED = (0,)
 
 MASKED = -1e30
 BF = jnp.bfloat16
@@ -165,6 +166,61 @@
     )(lists, *on_chip(rows))
 
 
+def gather(plan, rows):
+    n, per, bh = plan.n, plan.per, plan.bh
+
+    def body(*refs):
+        ins, outs = refs[:n], refs[n:]
+        for j in range(bh):
+            for p in range(per):
+                outs[j][:, p] = ins[j * per + p][...]
+
+    return pl.pallas_call(
+        body,
+        out_shape=[pltpu.VMEM(plan.tile, BF)] * bh,
+        in_specs=[VMEM] * n,
+        out_specs=[VMEM] * bh,
+        compiler_params=grant(1),
+        cost_estimate=cost(2 * bh * plan.tile_bytes),
+        name="gather",
+    )(*on_chip(rows))
+
+
+def pick(plan, blocks, lists):
+    bh, half = plan.bh, plan.ctx // 2
+
+    def body(*refs):
+        lists_ref, ins, out, note = refs[0], refs[1 : 1 + bh * half], *refs[1 + bh * half :]
+        me, z = lax.axis_index("ctx"), lax.axis_index("head")
+        note[...] = jnp.zeros(note.shape, F32)
+        for i in range(half):
+            which = wanted(plan, lists_ref, me ^ 1, me ^ (2 * i), z)[1]
+            for j in range(bh):
+
+                @pl.when(which == j)
+                def _():
+                    out[i] = ins[i * bh + j][...]
+
+    return pl.pallas_call(
+        body,
+        out_shape=[pltpu.VMEM((half,) + plan.tile, BF), pltpu.VMEM((8, HD), F32)],
+        in_specs=[SMEM] + [VMEM] * (bh * half),
+        out_specs=[VMEM] * 2,
+        compiler_params=grant(1),
+        cost_estimate=cost(2 * half * plan.tile_bytes),
+        name="pick",
+    )(lists, *on_chip(blocks))[0]
+
+
+def relay(plan, rows, lists):
+    own = gather(plan, rows)
+    near = [[swap(block, "ctx", mask) for block in own] for mask in (2, 4)]
+    far = [swap(near[0][0], "ctx", 4), swap(near[1][1], "ctx", 2)]
+    blocks = [*own, *near[0], *near[1], *far]
+    theirs = pick(plan, blocks, lists)
+    return [*blocks, swap(theirs, "ctx", 1)]
+
+
 def dot(a, b, ca, cb):
     return lax.dot_general(a, b, (((ca,), (cb,)), ((), ())), preferred_element_type=F32)
 
@@ -196,20 +252,31 @@
 
 def attend(plan, noisy, tiles, lists):
     n, per, slots, rows, bh = plan.n, plan.per, plan.ctx, plan.rows, plan.bh
-    heads = plan.width // HD
+    heads, count, relayed = plan.width // HD, len(tiles), len(tiles) != plan.ctx
     scale = 1.0 / math.sqrt(HD)
     log2e = 1.0 / math.log(2.0)
     side = (2 * rows + STATS, plan.width)
 
     def body(*refs):
-        lists_ref, rows_in, tile_refs = refs[0], refs[1 : 1 + n], refs[1 + n : 1 + n + slots]
-        rows_out = refs[1 + n + slots : 1 + 2 * n + slots]
-        term_refs = refs[1 + 2 * n + slots : 1 + 2 * n + 2 * slots]
-        tiles_in, terms_out = refs[1 + 2 * n + 2 * slots :]
+        lists_ref, rows_in, tile_refs = refs[0], refs[1 : 1 + n], refs[1 + n : 1 + n + count]
+        rows_out = refs[1 + n + count : 1 + 2 * n + count]
+        term_refs = refs[1 + 2 * n + count : 1 + 2 * n + count + slots]
+        tiles_in, terms_out = refs[1 + 2 * n + count + slots :]
         me, z = lax.axis_index("ctx"), lax.axis_index("head")
         home = lax.div(z, jnp.int32(per))
-        for s in range(slots):
-            tiles_in[s] = tile_refs[s][...]
+        if relayed:
+            for i in range(slots // 2):
+                which = wanted(plan, lists_ref, me, me ^ (2 * i), z)[1]
+                for j in range(bh):
+
+                    @pl.when(which == j)
+                    def _():
+                        tiles_in[2 * i] = tile_refs[i * bh + j][...]
+
+                tiles_in[2 * i + 1] = tile_refs[-1][i]
+        else:
+            for s in range(slots):
+                tiles_in[s] = tile_refs[s][...]
 
         def step(h, carry):
             cols = pl.ds(pl.multiple_of(h * HD, HD), HD)
@@ -283,7 +350,7 @@
     result = pl.pallas_call(
         body,
         out_shape=[pltpu.VMEM(side, BF)] * n + [pltpu.VMEM(plan.tile, BF)] * slots,
-        in_specs=[SMEM] + [VMEM] * (n + slots),
+        in_specs=[SMEM] + [VMEM] * (n + count),
         out_specs=[VMEM] * (n + slots),
         scratch_shapes=[
             pltpu.VMEM((slots,) + plan.tile, BF),
@@ -428,7 +495,12 @@
     chunks = range(plan.chunks)
     clean = [over_head(pack(plan, (kclean, vclean), c)) for c in chunks]
     noisy = [over_head(pack(plan, (query, key, value, grad), c)) for c in chunks]
-    tiles = [over_ctx(select(plan, clean[c], lists)) for c in chunks]
+    tiles = [
+        relay(plan, clean[c], lists)
+        if c in RELAYED and (plan.ctx, plan.bh) == (8, 2)
+        else over_ctx(select(plan, clean[c], lists))
+        for c in chunks
+    ]
     sides, sums = [], []
     for c in chunks:
         side, terms = attend(plan, noisy[c], tiles[c], lists)

time: 227 us -> 202 us (0.89)
  waiting for transfers between devices: 109 us -> 95.6 us
  starting transfers between devices: 80.8 us -> 68.2 us
    ppermute x54, waiting for transfers between devices: 109 us -> 95.6 us  [swap(): return lax.ppermute(x, axis, [(i, i ^ mask) for i in range(count)])]
    ppermute x54, starting transfers between devices: 80.8 us -> 68.2 us  [swap(): return lax.ppermute(x, axis, [(i, i ^ mask) for i in range(count)])]
  transfers between devices with their start and end apart: 54 -> 54, of which waited for: 15 -> 24; matrix products, arithmetic and copies ran while one was open for 0% -> 0% of each run, Pallas kernels for 14% -> 16%
where the time goes in v3:
time: 202 us; the launch traced here: 201 us
  waiting for transfers between devices  95.6 us (47%)
  starting transfers between devices  68.2 us (34%)
  Pallas kernels  34.9 us (17%)
    ppermute x54, waiting for transfers between devices, swap(): return lax.ppermute(x, axis, [(i, i ^ mask) for i in range(count)])  95.6 us
    ppermute x54, starting transfers between devices, swap(): return lax.ppermute(x, axis, [(i, i ^ mask) for i in range(count)])  68.2 us
    pallas_call x2, Pallas kernels, attend(): pl.pallas_call(body, out_shape=[pltpu.VMEM(side, BF)] * n + [pltpu.VMEM(p...  17.2 us
    pallas_call x4, Pallas kernels, pack(): pl.pallas_call(body, out_shape=[pltpu.VMEM(shape, BF)] * n, in_specs=[HBM...  5.93 us
    pallas_call x1, Pallas kernels, finish(): pl.pallas_call(body, out_shape=[jax.ShapeDtypeStruct(shape, BF)] * 4, in_...  4.34 us
  transfers between devices with their start and end apart: 54, of which 24 were waited for; matrix products, arithmetic and copies ran while one was open for 0% of the time, Pallas kernels for 16%

profile of v3, /device:TPU:0, one launch (start us, length us, event | category | flops | bytes accessed | tf_op | source)
XLA Modules:
  0.0 201.3 jit_solution(9508478217796815797)
XLA Ops:
  1.8 3.1 %collective-permute-start.3 = (bf16[2,128,256]{2,1,0:T(8,128)(2,1)S(1)}, bf16[2,128,256]{2,1,0:T(8,128)(2,1)S(1)}, u32[]{:S(2)}, u32[]{:S(2)}) collective-permute-start(bf16[2,128,256]{2,1,0:T(8,128)(2,1)S(1)} %get-tuple-element.76), channel_id=1, source_target_pairs={{0,1},{1,0},{2,3},{3,2},{4,5},{5,4},{6,7},{7,6},{8,9},{9,8},{10,11... | collective-permute-start | bytes 393224 | tf_op jit(solution)/shard_map/ppermute | solution.py:34
  4.9 2.6 %collective-permute-start.4 = (bf16[2,128,256]{2,1,0:T(8,128)(2,1)S(1)}, bf16[2,128,256]{2,1,0:T(8,128)(2,1)S(1)}, u32[]{:S(2)}, u32[]{:S(2)}) collective-permute-start(bf16[2,128,256]{2,1,0:T(8,128)(2,1)S(1)} %get-tuple-element.77), channel_id=1, source_target_pairs={{0,2},{1,3},{2,0},{3,1},{4,6},{5,7},{6,4},{7,5},{8,10},{9,11},{10,... | collective-permute-start | bytes 393224 | tf_op jit(solution)/shard_map/ppermute | solution.py:34
  10.0 7.8 %collective-permute-done.4.refs_2_ = bf16[2,128,256]{2,1,0:T(8,128)(2,1)S(1)} collective-permute-done((bf16[2,128,256]{2,1,0:T(8,128)(2,1)S(1)}, bf16[2,128,256]{2,1,0:T(8,128)(2,1)S(1)}, u32[]{:S(2)}, u32[]{:S(2)}) %collective-permute-start.4) | collective-permute-done | bytes 131104 | tf_op jit(solution)/shard_map/ppermute | solution.py:34
  20.9 3.1 %collective-permute-start.20 = (bf16[2,128,256]{2,1,0:T(8,128)(2,1)S(1)}, bf16[2,128,256]{2,1,0:T(8,128)(2,1)S(1)}, u32[]{:S(2)}, u32[]{:S(2)}) collective-permute-start(bf16[2,128,256]{2,1,0:T(8,128)(2,1)S(1)} %get-tuple-element.92), channel_id=1, source_target_pairs={{0,2},{1,3},{2,0},{3,1},{4,6},{5,7},{6,4},{7,5},{8,10},{9,11},{10,... | collective-permute-start | bytes 393224 | tf_op jit(solution)/shard_map/ppermute | solution.py:34
  25.0 4.3 %collective-permute-done.20.refs_3_ = bf16[2,128,256]{2,1,0:T(8,128)(2,1)S(1)} collective-permute-done((bf16[2,128,256]{2,1,0:T(8,128)(2,1)S(1)}, bf16[2,128,256]{2,1,0:T(8,128)(2,1)S(1)}, u32[]{:S(2)}, u32[]{:S(2)}) %collective-permute-start.20) | collective-permute-done | bytes 131104 | tf_op jit(solution)/shard_map/ppermute | solution.py:34
  32.1 2.3 %pack.6 = (bf16[4,128,256]{2,1,0:T(8,128)(2,1)S(1)}, bf16[4,128,256]{2,1,0:T(8,128)(2,1)}, bf16[4,128,256]{2,1,0:T(8,128)(2,1)}, bf16[4,128,256]{2,1,0:T(8,128)(2,1)}) custom-call(bf16[128,2048]{1,0:T(8,128)(2,1)} %refs_8_.1, bf16[128,2048]{1,0:T(8,128)(2,1)} %refs_12_.1, bf16[128,2048]{1,0:T(8,128)(2,1)} %refs_13_.1, bf16[128,2048]{1,0:T(8,128)(2,1)} %refs_10_.1), custom_call_target="tpu_custom_call" | custom-call | bytes 2097152 | tf_op jit(solution)/shard_map/pack/pallas_call | solution.py:89
  34.4 2.6 %collective-permute-done.21.refs_4_ = bf16[2,128,256]{2,1,0:T(8,128)(2,1)S(1)} collective-permute-done((bf16[2,128,256]{2,1,0:T(8,128)(2,1)S(1)}, bf16[2,128,256]{2,1,0:T(8,128)(2,1)S(1)}, u32[]{:S(2)}, u32[]{:S(2)}) %collective-permute-start.21) | collective-permute-done | bytes 131104 | tf_op jit(solution)/shard_map/ppermute | solution.py:34
  39.1 2.2 %collective-permute-start.18 = (bf16[4,128,256]{2,1,0:T(8,128)(2,1)}, bf16[4,128,256]{2,1,0:T(8,128)(2,1)}, u32[]{:S(2)}, u32[]{:S(2)}) collective-permute-start(bf16[4,128,256]{2,1,0:T(8,128)(2,1)} %get-tuple-element.89), channel_id=1, source_target_pairs={{0,3},{1,2},{2,1},{3,0},{4,7},{5,6},{6,5},{7,4},{8,11},{9,10},{10,... | collective-permute-start | bytes 786440 | tf_op jit(solution)/shard_map/ppermute | solution.py:34
  47.2 3.8 %collective-permute-done.16.refs_2_ = bf16[4,128,256]{2,1,0:T(8,128)(2,1)} collective-permute-done((bf16[4,128,256]{2,1,0:T(8,128)(2,1)}, bf16[4,128,256]{2,1,0:T(8,128)(2,1)}, u32[]{:S(2)}, u32[]{:S(2)}) %collective-permute-start.16) | collective-permute-done | bytes 262176 | tf_op jit(solution)/shard_map/ppermute | solution.py:34
  50.9 5.3 %collective-permute-done.17.refs_3_ = bf16[4,128,256]{2,1,0:T(8,128)(2,1)} collective-permute-done((bf16[4,128,256]{2,1,0:T(8,128)(2,1)}, bf16[4,128,256]{2,1,0:T(8,128)(2,1)}, u32[]{:S(2)}, u32[]{:S(2)}) %collective-permute-start.17) | collective-permute-done | bytes 262176 | tf_op jit(solution)/shard_map/ppermute | solution.py:34
  59.7 5.7 %collective-permute-done.23.refs_7_ = bf16[2,2,128,256]{3,2,1,0:T(8,128)(2,1)S(1)} collective-permute-done((bf16[2,2,128,256]{3,2,1,0:T(8,128)(2,1)S(1)}, bf16[2,2,128,256]{3,2,1,0:T(8,128)(2,1)S(1)}, u32[]{:S(2)}, u32[]{:S(2)}) %collective-permute-start.23) | collective-permute-done | bytes 262176 | tf_op jit(solution)/shard_map/ppermute | solution.py:34
  65.4 2.7 %collective-permute-done.24.refs_8_ = bf16[2,2,128,256]{3,2,1,0:T(8,128)(2,1)S(1)} collective-permute-done((bf16[2,2,128,256]{3,2,1,0:T(8,128)(2,1)S(1)}, bf16[2,2,128,256]{3,2,1,0:T(8,128)(2,1)S(1)}, u32[]{:S(2)}, u32[]{:S(2)}) %collective-permute-start.24) | collective-permute-done | bytes 262176 | tf_op jit(solution)/shard_map/ppermute | solution.py:34
  70.5 9.5 %collective-permute-start.32 = (bf16[128,2048]{1,0:T(8,128)(2,1)S(1)}, bf16[128,2048]{1,0:T(8,128)(2,1)S(1)}, u32[]{:S(2)}, u32[]{:S(2)}) collective-permute-start(bf16[128,2048]{1,0:T(8,128)(2,1)S(1)} %copy-done), channel_id=1, source_target_pairs={{0,1},{1,0},{2,3},{3,2},{4,5},{5,4},{6,7},{7,6},{8,9},{9,8},{10,11... | collective-permute-start | bytes 1572872 | tf_op jit(solution)/shard_map/ppermute | solution.py:34
  80.0 2.3 %collective-permute-done.26.refs_10_ = bf16[2,2,128,256]{3,2,1,0:T(8,128)(2,1)S(1)} collective-permute-done((bf16[2,2,128,256]{3,2,1,0:T(8,128)(2,1)S(1)}, bf16[2,2,128,256]{3,2,1,0:T(8,128)(2,1)S(1)}, u32[]{:S(2)}, u32[]{:S(2)}) %collective-permute-start.26) | collective-permute-done | bytes 262176 | tf_op jit(solution)/shard_map/ppermute | solution.py:34
  82.3 2.7 %collective-permute-start.33 = (bf16[128,2048]{1,0:T(8,128)(2,1)S(1)}, bf16[128,2048]{1,0:T(8,128)(2,1)S(1)}, u32[]{:S(2)}, u32[]{:S(2)}) collective-permute-start(bf16[128,2048]{1,0:T(8,128)(2,1)S(1)} %copy-done.3), channel_id=1, source_target_pairs={{0,1},{1,0},{2,3},{3,2},{4,5},{5,4},{6,7},{7,6},{8,9},{9,8},{10,11... | collective-permute-start | bytes 1572872 | tf_op jit(solution)/shard_map/ppermute | solution.py:34
  87.5 8.6 %attend.3 = (bf16[272,256]{1,0:T(8,128)(2,1)S(1)}, bf16[272,256]{1,0:T(8,128)(2,1)S(1)}, bf16[272,256]{1,0:T(8,128)(2,1)S(1)}, bf16[272,256]{1,0:T(8,128)(2,1)S(...) custom-call(s32[16,4]{1,0:T(8,128)S(1)} %copy.14.refs_0_, ...), custom_call_target="tpu_custom_call" | custom-call | flops 2013265920 | bytes 6291456 | tf_op jit(solution)/shard_map/attend/pallas_call | solution.py:350
  96.1 13.1 %collective-permute-done.1.refs_3_ = bf16[4,128,256]{2,1,0:T(8,128)(2,1)S(1)} collective-permute-done((bf16[4,128,256]{2,1,0:T(8,128)(2,1)S(1)}, bf16[4,128,256]{2,1,0:T(8,128)(2,1)S(1)}, u32[]{:S(2)}, u32[]{:S(2)}) %collective-permute-start.1) | collective-permute-done | bytes 262176 | tf_op jit(solution)/shard_map/ppermute | solution.py:34
  109.2 2.7 %collective-permute-start.29 = (bf16[272,256]{1,0:T(8,128)(2,1)S(1)}, bf16[272,256]{1,0:T(8,128)(2,1)S(1)}, u32[]{:S(2)}, u32[]{:S(2)}) collective-permute-start(bf16[272,256]{1,0:T(8,128)(2,1)S(1)} %get-tuple-element.103), channel_id=1, source_target_pairs={{0,1},{1,0},{2,3},{3,2},{4,5},{5,4},{6,7},{7,6},{8,9},{9,8},{10,11... | collective-permute-start | bytes 417800 | tf_op jit(solution)/shard_map/ppermute | solution.py:34
  112.0 5.0 %collective-permute-done.2.refs_4_ = bf16[4,128,256]{2,1,0:T(8,128)(2,1)S(1)} collective-permute-done((bf16[4,128,256]{2,1,0:T(8,128)(2,1)S(1)}, bf16[4,128,256]{2,1,0:T(8,128)(2,1)S(1)}, u32[]{:S(2)}, u32[]{:S(2)}) %collective-permute-start.2) | collective-permute-done | bytes 262176 | tf_op jit(solution)/shard_map/ppermute | solution.py:34
  118.9 4.8 %collective-permute-done.30.refs_6_ = bf16[272,256]{1,0:T(8,128)(2,1)S(1)} collective-permute-done((bf16[272,256]{1,0:T(8,128)(2,1)S(1)}, bf16[272,256]{1,0:T(8,128)(2,1)S(1)}, u32[]{:S(2)}, u32[]{:S(2)}) %collective-permute-start.30) | collective-permute-done | bytes 139296 | tf_op jit(solution)/shard_map/ppermute | solution.py:34
  125.5 8.5 %attend.2 = (bf16[272,256]{1,0:T(8,128)(2,1)S(1)}, bf16[272,256]{1,0:T(8,128)(2,1)S(1)}, bf16[272,256]{1,0:T(8,128)(2,1)S(1)}, bf16[272,256]{1,0:T(8,128)(2,1)S(...) custom-call(s32[16,4]{1,0:T(8,128)S(1)} %copy.14.refs_0_, ...), custom_call_target="tpu_custom_call" | custom-call | flops 2013265920 | bytes 6291456 | tf_op jit(solution)/shard_map/attend/pallas_call | solution.py:350
  138.6 5.6 %collective-permute-done.49.refs_7_ = bf16[2,2,128,256]{3,2,1,0:T(8,128)(2,1)S(1)} collective-permute-done((bf16[2,2,128,256]{3,2,1,0:T(8,128)(2,1)S(1)}, bf16[2,2,128,256]{3,2,1,0:T(8,128)(2,1)S(1)}, u32[]{:S(2)}, u32[]{:S(2)}) %collective-permute-start.49) | collective-permute-done | bytes 262176 | tf_op jit(solution)/shard_map/ppermute | solution.py:34
  145.6 2.9 %collective-permute-done.50.refs_8_ = bf16[2,2,128,256]{3,2,1,0:T(8,128)(2,1)S(1)} collective-permute-done((bf16[2,2,128,256]{3,2,1,0:T(8,128)(2,1)S(1)}, bf16[2,2,128,256]{3,2,1,0:T(8,128)(2,1)S(1)}, u32[]{:S(2)}, u32[]{:S(2)}) %collective-permute-start.50) | collective-permute-done | bytes 262176 | tf_op jit(solution)/shard_map/ppermute | solution.py:34
  148.5 2.2 %collective-permute-start.38 = (bf16[2,2,128,256]{3,2,1,0:T(8,128)(2,1)S(1)}, bf16[2,2,128,256]{3,2,1,0:T(8,128)(2,1)S(1)}, u32[]{:S(2)}, u32[]{:S(2)}) collective-permute-start(bf16[2,2,128,256]{3,2,1,0:T(8,128)(2,1)S(1)} %get-tuple-element.115), channel_id=1, source_target_pairs={{0,20},{4,16},{8,28},{12,24},{16,4},{20,0},{24,12},{28,8},{1,21},{... | collective-permute-start | bytes 786440 | tf_op jit(solution)/shard_map/ppermute | solution.py:34
  151.4 4.0 %collective-permute-done.35.refs_3_ = bf16[2,2,128,256]{3,2,1,0:T(8,128)(2,1)S(1)} collective-permute-done((bf16[2,2,128,256]{3,2,1,0:T(8,128)(2,1)S(1)}, bf16[2,2,128,256]{3,2,1,0:T(8,128)(2,1)S(1)}, u32[]{:S(2)}, u32[]{:S(2)}) %collective-permute-start.35) | collective-permute-done | bytes 262176 | tf_op jit(solution)/shard_map/ppermute | solution.py:34
  155.4 5.2 %collective-permute-done.36.refs_4_ = bf16[2,2,128,256]{3,2,1,0:T(8,128)(2,1)S(1)} collective-permute-done((bf16[2,2,128,256]{3,2,1,0:T(8,128)(2,1)S(1)}, bf16[2,2,128,256]{3,2,1,0:T(8,128)(2,1)S(1)}, u32[]{:S(2)}, u32[]{:S(2)}) %collective-permute-start.36) | collective-permute-done | bytes 262176 | tf_op jit(solution)/shard_map/ppermute | solution.py:34
  162.1 2.9 %collective-permute-start.14 = (bf16[272,256]{1,0:T(8,128)(2,1)S(1)}, bf16[272,256]{1,0:T(8,128)(2,1)S(1)}, u32[]{:S(2)}, u32[]{:S(2)}) collective-permute-start(bf16[272,256]{1,0:T(8,128)(2,1)S(1)} %get-tuple-element.84), channel_id=1, source_target_pairs={{0,2},{1,3},{2,0},{3,1},{4,6},{5,7},{6,4},{7,5},{8,10},{9,11},{10,... | collective-permute-start | bytes 417800 | tf_op jit(solution)/shard_map/ppermute | solution.py:34
  172.8 3.0 %collective-permute-start.52 = (bf16[2,128,256]{2,1,0:T(8,128)(2,1)S(1)}, bf16[2,128,256]{2,1,0:T(8,128)(2,1)S(1)}, u32[]{:S(2)}, u32[]{:S(2)}) collective-permute-start(bf16[2,128,256]{2,1,0:T(8,128)(2,1)S(1)} %get-tuple-element.132), channel_id=1, source_target_pairs={{0,2},{1,3},{2,0},{3,1},{4,6},{5,7},{6,4},{7,5},{8,10},{9,11},{10,... | collective-permute-start | bytes 393224 | tf_op jit(solution)/shard_map/ppermute | solution.py:34
  175.8 4.1 %collective-permute-done.51.refs_5_ = bf16[2,128,256]{2,1,0:T(8,128)(2,1)S(1)} collective-permute-done((bf16[2,128,256]{2,1,0:T(8,128)(2,1)S(1)}, bf16[2,128,256]{2,1,0:T(8,128)(2,1)S(1)}, u32[]{:S(2)}, u32[]{:S(2)}) %collective-permute-start.51) | collective-permute-done | bytes 131104 | tf_op jit(solution)/shard_map/ppermute | solution.py:34
  182.0 2.3 %collective-permute-start.42 = (bf16[2,128,256]{2,1,0:T(8,128)(2,1)S(1)}, bf16[2,128,256]{2,1,0:T(8,128)(2,1)S(1)}, u32[]{:S(2)}, u32[]{:S(2)}) collective-permute-start(bf16[2,128,256]{2,1,0:T(8,128)(2,1)S(1)} %get-tuple-element.120), channel_id=1, source_target_pairs={{0,2},{1,3},{2,0},{3,1},{4,6},{5,7},{6,4},{7,5},{8,10},{9,11},{10,... | collective-permute-start | bytes 393224 | tf_op jit(solution)/shard_map/ppermute | solution.py:34
  185.9 4.3 %finish.1 = (bf16[128,2048]{1,0:T(8,128)(2,1)}, bf16[128,2048]{1,0:T(8,128)(2,1)}, bf16[128,2048]{1,0:T(8,128)(2,1)}, bf16[128,2048]{1,0:T(8,128)(2,1)}) custom-call(bf16[272,256]{1,0:T(8,128)(2,1)S(1)} %get-tuple-element.82.refs_0_, bf16[272,256]{1,0:T(8,128)(2,1)S(1)} %collective-permute-done.13.refs_1_, ...), custom_call_target="tpu_custom_call" | custom-call | flops 536870912 | bytes 6291456 | tf_op jit(solution)/shard_map/finish/pallas_call | solution.py:456
  191.5 8.6 %collective-permute-done.42.refs_2_ = bf16[2,128,256]{2,1,0:T(8,128)(2,1)S(1)} collective-permute-done((bf16[2,128,256]{2,1,0:T(8,128)(2,1)S(1)}, bf16[2,128,256]{2,1,0:T(8,128)(2,1)S(1)}, u32[]{:S(2)}, u32[]{:S(2)}) %collective-permute-start.42) | collective-permute-done | bytes 131104 | tf_op jit(solution)/shard_map/ppermute | solution.py:34
  (108 shorter events, 52.4 us)
Async XLA Ops:
  8.6 15.9 %collective-permute-start.19 = (bf16[2,128,256]{2,1,0:T(8,128)(2,1)S(1)}, bf16[2,128,256]{2,1,0:T(8,128)(2,1)S(1)}, u32[]{:S(2)}, u32[]{:S(2)}) collective-permute-start(bf16[2,128,256]{2,1,0:T(8,128)(2,1)S(1)} %get-tuple-element.91), channel_id=1, source_target_pairs={{0,1},{1,0},{2,3},{3,2},{4,5},{5,4},{6,7},{7,6},{8,9},{9,8},{10,11... | collective-permute-start | bytes 393224 | tf_op jit(solution)/shard_map/ppermute | solution.py:34
  24.5 14.6 %collective-permute-start.8 = (bf16[2,2,128,256]{3,2,1,0:T(8,128)(2,1)S(1)}, bf16[2,2,128,256]{3,2,1,0:T(8,128)(2,1)S(1)}, u32[]{:S(2)}, u32[]{:S(2)}) collective-permute-start(bf16[2,2,128,256]{3,2,1,0:T(8,128)(2,1)S(1)} %get-tuple-element.79.refs_1_.refs_5_), channel_id=1, source_target_pairs={{0,16},{4,20},{8,24},{12,28},{16,0},{20,4},{24,8},{28,12},{1,17},{... | collective-permute-start | bytes 786440 | tf_op jit(solution)/shard_map/ppermute | solution.py:34
  31.1 14.3 %collective-permute-start.10 = (bf16[2,2,128,256]{3,2,1,0:T(8,128)(2,1)S(1)}, bf16[2,2,128,256]{3,2,1,0:T(8,128)(2,1)S(1)}, u32[]{:S(2)}, u32[]{:S(2)}) collective-permute-start(bf16[2,2,128,256]{3,2,1,0:T(8,128)(2,1)S(1)} %collective-permute-done.6.refs_3_.refs_7_), channel_id=1, source_target_pairs={{0,16},{4,20},{8,24},{12,28},{16,0},{20,4},{24,8},{28,12},{1,17},{... | collective-permute-start | bytes 786440 | tf_op jit(solution)/shard_map/ppermute | solution.py:34
  31.6 13.9 %collective-permute-start.11 = (bf16[2,2,128,256]{3,2,1,0:T(8,128)(2,1)S(1)}, bf16[2,2,128,256]{3,2,1,0:T(8,128)(2,1)S(1)}, u32[]{:S(2)}, u32[]{:S(2)}) collective-permute-start(bf16[2,2,128,256]{3,2,1,0:T(8,128)(2,1)S(1)} %collective-permute-done.9.refs_6_.refs_10_), channel_id=1, source_target_pairs={{0,8},{4,12},{8,0},{12,4},{16,24},{20,28},{24,16},{28,20},{1,9},{5... | collective-permute-start | bytes 786440 | tf_op jit(solution)/shard_map/ppermute | solution.py:34
  37.0 14.0 %collective-permute-start.16 = (bf16[4,128,256]{2,1,0:T(8,128)(2,1)}, bf16[4,128,256]{2,1,0:T(8,128)(2,1)}, u32[]{:S(2)}, u32[]{:S(2)}) collective-permute-start(bf16[4,128,256]{2,1,0:T(8,128)(2,1)} %get-tuple-element.87), channel_id=1, source_target_pairs={{0,1},{1,0},{2,3},{3,2},{4,5},{5,4},{6,7},{7,6},{8,9},{9,8},{10,11... | collective-permute-start | bytes 786440 | tf_op jit(solution)/shard_map/ppermute | solution.py:34
  37.0 19.3 %collective-permute-start.17 = (bf16[4,128,256]{2,1,0:T(8,128)(2,1)}, bf16[4,128,256]{2,1,0:T(8,128)(2,1)}, u32[]{:S(2)}, u32[]{:S(2)}) collective-permute-start(bf16[4,128,256]{2,1,0:T(8,128)(2,1)} %get-tuple-element.88), channel_id=1, source_target_pairs={{0,2},{1,3},{2,0},{3,1},{4,6},{5,7},{6,4},{7,5},{8,10},{9,11},{10,... | collective-permute-start | bytes 786440 | tf_op jit(solution)/shard_map/ppermute | solution.py:34
  39.1 17.7 %collective-permute-start.18 = (bf16[4,128,256]{2,1,0:T(8,128)(2,1)}, bf16[4,128,256]{2,1,0:T(8,128)(2,1)}, u32[]{:S(2)}, u32[]{:S(2)}) collective-permute-start(bf16[4,128,256]{2,1,0:T(8,128)(2,1)} %get-tuple-element.89), channel_id=1, source_target_pairs={{0,3},{1,2},{2,1},{3,0},{4,7},{5,6},{6,5},{7,4},{8,11},{9,10},{10,... | collective-permute-start | bytes 786440 | tf_op jit(solution)/shard_map/ppermute | solution.py:34
  50.9 74.6 %collective-permute-start.12 = (bf16[4,2,2,128,256]{4,3,2,1,0:T(8,128)(2,1)S(1)}, bf16[4,2,2,128,256]{4,3,2,1,0:T(8,128)(2,1)S(1)}, u32[]{:S(2)}, u32[]{:S(2)}) collective-permute-start(bf16[4,2,2,128,256]{4,3,2,1,0:T(8,128)(2,1)S(1)} %get-tuple-element.81), channel_id=1, source_target_pairs={{0,4},{4,0},{8,12},{12,8},{16,20},{20,16},{24,28},{28,24},{1,5},{5... | collective-permute-start | bytes 3145736 | tf_op jit(solution)/shard_map/ppermute | solution.py:34
  59.1 23.2 %collective-permute-start.26 = (bf16[2,2,128,256]{3,2,1,0:T(8,128)(2,1)S(1)}, bf16[2,2,128,256]{3,2,1,0:T(8,128)(2,1)S(1)}, u32[]{:S(2)}, u32[]{:S(2)}) collective-permute-start(bf16[2,2,128,256]{3,2,1,0:T(8,128)(2,1)S(1)} %get-tuple-element.99), channel_id=1, source_target_pairs={{0,20},{4,16},{8,28},{12,24},{16,4},{20,0},{24,12},{28,8},{1,21},{... | collective-permute-start | bytes 786440 | tf_op jit(solution)/shard_map/ppermute | solution.py:34
  65.4 19.6 %collective-permute-start.27 = (bf16[2,2,128,256]{3,2,1,0:T(8,128)(2,1)S(1)}, bf16[2,2,128,256]{3,2,1,0:T(8,128)(2,1)S(1)}, u32[]{:S(2)}, u32[]{:S(2)}) collective-permute-start(bf16[2,2,128,256]{3,2,1,0:T(8,128)(2,1)S(1)} %get-tuple-element.100), channel_id=1, source_target_pairs={{0,24},{4,28},{8,16},{12,20},{16,8},{20,12},{24,0},{28,4},{1,25},{... | collective-permute-start | bytes 786440 | tf_op jit(solution)/shard_map/ppermute | solution.py:34
  68.2 17.2 %collective-permute-start.28 = (bf16[2,2,128,256]{3,2,1,0:T(8,128)(2,1)S(1)}, bf16[2,2,128,256]{3,2,1,0:T(8,128)(2,1)S(1)}, u32[]{:S(2)}, u32[]{:S(2)}) collective-permute-start(bf16[2,2,128,256]{3,2,1,0:T(8,128)(2,1)S(1)} %get-tuple-element.101), channel_id=1, source_target_pairs={{0,28},{4,24},{8,20},{12,16},{16,12},{20,8},{24,4},{28,0},{1,29},{... | collective-permute-start | bytes 786440 | tf_op jit(solution)/shard_map/ppermute | solution.py:34
  70.5 46.5 %collective-permute-start.32 = (bf16[128,2048]{1,0:T(8,128)(2,1)S(1)}, bf16[128,2048]{1,0:T(8,128)(2,1)S(1)}, u32[]{:S(2)}, u32[]{:S(2)}) collective-permute-start(bf16[128,2048]{1,0:T(8,128)(2,1)S(1)} %copy-done), channel_id=1, source_target_pairs={{0,1},{1,0},{2,3},{3,2},{4,5},{5,4},{6,7},{7,6},{8,9},{9,8},{10,11... | collective-permute-start | bytes 1572872 | tf_op jit(solution)/shard_map/ppermute | solution.py:34
  82.3 34.7 %collective-permute-start.33 = (bf16[128,2048]{1,0:T(8,128)(2,1)S(1)}, bf16[128,2048]{1,0:T(8,128)(2,1)S(1)}, u32[]{:S(2)}, u32[]{:S(2)}) collective-permute-start(bf16[128,2048]{1,0:T(8,128)(2,1)S(1)} %copy-done.3), channel_id=1, source_target_pairs={{0,1},{1,0},{2,3},{3,2},{4,5},{5,4},{6,7},{7,6},{8,9},{9,8},{10,11... | collective-permute-start | bytes 1572872 | tf_op jit(solution)/shard_map/ppermute | solution.py:34
  85.0 24.2 %collective-permute-start.1 = (bf16[4,128,256]{2,1,0:T(8,128)(2,1)S(1)}, bf16[4,128,256]{2,1,0:T(8,128)(2,1)S(1)}, u32[]{:S(2)}, u32[]{:S(2)}) collective-permute-start(bf16[4,128,256]{2,1,0:T(8,128)(2,1)S(1)} %copy-done.5), channel_id=1, source_target_pairs={{0,2},{1,3},{2,0},{3,1},{4,6},{5,7},{6,4},{7,5},{8,10},{9,11},{10,... | collective-permute-start | bytes 786440 | tf_op jit(solution)/shard_map/ppermute | solution.py:34
  85.4 31.6 %collective-permute-start.2 = (bf16[4,128,256]{2,1,0:T(8,128)(2,1)S(1)}, bf16[4,128,256]{2,1,0:T(8,128)(2,1)S(1)}, u32[]{:S(2)}, u32[]{:S(2)}) collective-permute-start(bf16[4,128,256]{2,1,0:T(8,128)(2,1)S(1)} %get-tuple-element.74), channel_id=1, source_target_pairs={{0,3},{1,2},{2,1},{3,0},{4,7},{5,6},{6,5},{7,4},{8,11},{9,10},{10,... | collective-permute-start | bytes 786440 | tf_op jit(solution)/shard_map/ppermute | solution.py:34
  117.0 17.0 %collective-permute-start.44 = (bf16[2,2,128,256]{3,2,1,0:T(8,128)(2,1)S(1)}, bf16[2,2,128,256]{3,2,1,0:T(8,128)(2,1)S(1)}, u32[]{:S(2)}, u32[]{:S(2)}) collective-permute-start(bf16[2,2,128,256]{3,2,1,0:T(8,128)(2,1)S(1)} %get-tuple-element.123), channel_id=1, source_target_pairs={{0,4},{4,0},{8,12},{12,8},{16,20},{20,16},{24,28},{28,24},{1,5},{5... | collective-permute-start | bytes 786440 | tf_op jit(solution)/shard_map/ppermute | solution.py:34
  117.0 18.0 %collective-permute-start.45 = (bf16[2,2,128,256]{3,2,1,0:T(8,128)(2,1)S(1)}, bf16[2,2,128,256]{3,2,1,0:T(8,128)(2,1)S(1)}, u32[]{:S(2)}, u32[]{:S(2)}) collective-permute-start(bf16[2,2,128,256]{3,2,1,0:T(8,128)(2,1)S(1)} %get-tuple-element.124), channel_id=1, source_target_pairs={{0,8},{4,12},{8,0},{12,4},{16,24},{20,28},{24,16},{28,20},{1,9},{5... | collective-permute-start | bytes 786440 | tf_op jit(solution)/shard_map/ppermute | solution.py:34
  117.9 18.8 %collective-permute-start.46 = (bf16[2,2,128,256]{3,2,1,0:T(8,128)(2,1)S(1)}, bf16[2,2,128,256]{3,2,1,0:T(8,128)(2,1)S(1)}, u32[]{:S(2)}, u32[]{:S(2)}) collective-permute-start(bf16[2,2,128,256]{3,2,1,0:T(8,128)(2,1)S(1)} %get-tuple-element.125), channel_id=1, source_target_pairs={{0,12},{4,8},{8,4},{12,0},{16,28},{20,24},{24,20},{28,16},{1,13},{... | collective-permute-start | bytes 786440 | tf_op jit(solution)/shard_map/ppermute | solution.py:34
  123.6 13.5 %collective-permute-start.47 = (bf16[2,2,128,256]{3,2,1,0:T(8,128)(2,1)S(1)}, bf16[2,2,128,256]{3,2,1,0:T(8,128)(2,1)S(1)}, u32[]{:S(2)}, u32[]{:S(2)}) collective-permute-start(bf16[2,2,128,256]{3,2,1,0:T(8,128)(2,1)S(1)} %get-tuple-element.126), channel_id=1, source_target_pairs={{0,16},{4,20},{8,24},{12,28},{16,0},{20,4},{24,8},{28,12},{1,17},{... | collective-permute-start | bytes 786440 | tf_op jit(solution)/shard_map/ppermute | solution.py:34
  136.6 14.0 %collective-permute-start.34 = (bf16[2,2,128,256]{3,2,1,0:T(8,128)(2,1)S(1)}, bf16[2,2,128,256]{3,2,1,0:T(8,128)(2,1)S(1)}, u32[]{:S(2)}, u32[]{:S(2)}) collective-permute-start(bf16[2,2,128,256]{3,2,1,0:T(8,128)(2,1)S(1)} %get-tuple-element.111), channel_id=1, source_target_pairs={{0,4},{4,0},{8,12},{12,8},{16,20},{20,16},{24,28},{28,24},{1,5},{5... | collective-permute-start | bytes 786440 | tf_op jit(solution)/shard_map/ppermute | solution.py:34
  137.2 18.2 %collective-permute-start.35 = (bf16[2,2,128,256]{3,2,1,0:T(8,128)(2,1)S(1)}, bf16[2,2,128,256]{3,2,1,0:T(8,128)(2,1)S(1)}, u32[]{:S(2)}, u32[]{:S(2)}) collective-permute-start(bf16[2,2,128,256]{3,2,1,0:T(8,128)(2,1)S(1)} %get-tuple-element.112), channel_id=1, source_target_pairs={{0,8},{4,12},{8,0},{12,4},{16,24},{20,28},{24,16},{28,20},{1,9},{5... | collective-permute-start | bytes 786440 | tf_op jit(solution)/shard_map/ppermute | solution.py:34
  137.8 22.8 %collective-permute-start.36 = (bf16[2,2,128,256]{3,2,1,0:T(8,128)(2,1)S(1)}, bf16[2,2,128,256]{3,2,1,0:T(8,128)(2,1)S(1)}, u32[]{:S(2)}, u32[]{:S(2)}) collective-permute-start(bf16[2,2,128,256]{3,2,1,0:T(8,128)(2,1)S(1)} %get-tuple-element.113), channel_id=1, source_target_pairs={{0,12},{4,8},{8,4},{12,0},{16,28},{20,24},{24,20},{28,16},{1,13},{... | collective-permute-start | bytes 786440 | tf_op jit(solution)/shard_map/ppermute | solution.py:34
  144.2 17.9 %collective-permute-start.37 = (bf16[2,2,128,256]{3,2,1,0:T(8,128)(2,1)S(1)}, bf16[2,2,128,256]{3,2,1,0:T(8,128)(2,1)S(1)}, u32[]{:S(2)}, u32[]{:S(2)}) collective-permute-start(bf16[2,2,128,256]{3,2,1,0:T(8,128)(2,1)S(1)} %get-tuple-element.114), channel_id=1, source_target_pairs={{0,16},{4,20},{8,24},{12,28},{16,0},{20,4},{24,8},{28,12},{1,17},{... | collective-permute-start | bytes 786440 | tf_op jit(solution)/shard_map/ppermute | solution.py:34
  148.5 13.6 %collective-permute-start.38 = (bf16[2,2,128,256]{3,2,1,0:T(8,128)(2,1)S(1)}, bf16[2,2,128,256]{3,2,1,0:T(8,128)(2,1)S(1)}, u32[]{:S(2)}, u32[]{:S(2)}) collective-permute-start(bf16[2,2,128,256]{3,2,1,0:T(8,128)(2,1)S(1)} %get-tuple-element.115), channel_id=1, source_target_pairs={{0,20},{4,16},{8,28},{12,24},{16,4},{20,0},{24,12},{28,8},{1,21},{... | collective-permute-start | bytes 786440 | tf_op jit(solution)/shard_map/ppermute | solution.py:34
  150.7 16.1 %collective-permute-start.39 = (bf16[2,2,128,256]{3,2,1,0:T(8,128)(2,1)S(1)}, bf16[2,2,128,256]{3,2,1,0:T(8,128)(2,1)S(1)}, u32[]{:S(2)}, u32[]{:S(2)}) collective-permute-start(bf16[2,2,128,256]{3,2,1,0:T(8,128)(2,1)S(1)} %get-tuple-element.116), channel_id=1, source_target_pairs={{0,24},{4,28},{8,16},{12,20},{16,8},{20,12},{24,0},{28,4},{1,25},{... | collective-permute-start | bytes 786440 | tf_op jit(solution)/shard_map/ppermute | solution.py:34
  155.4 15.5 %collective-permute-start.40 = (bf16[2,2,128,256]{3,2,1,0:T(8,128)(2,1)S(1)}, bf16[2,2,128,256]{3,2,1,0:T(8,128)(2,1)S(1)}, u32[]{:S(2)}, u32[]{:S(2)}) collective-permute-start(bf16[2,2,128,256]{3,2,1,0:T(8,128)(2,1)S(1)} %get-tuple-element.117), channel_id=1, source_target_pairs={{0,28},{4,24},{8,20},{12,16},{16,12},{20,8},{24,4},{28,0},{1,29},{... | collective-permute-start | bytes 786440 | tf_op jit(solution)/shard_map/ppermute | solution.py:34
  162.1 19.4 %collective-permute-start.13 = (bf16[272,256]{1,0:T(8,128)(2,1)S(1)}, bf16[272,256]{1,0:T(8,128)(2,1)S(1)}, u32[]{:S(2)}, u32[]{:S(2)}) collective-permute-start(bf16[272,256]{1,0:T(8,128)(2,1)S(1)} %get-tuple-element.83), channel_id=1, source_target_pairs={{0,1},{1,0},{2,3},{3,2},{4,5},{5,4},{6,7},{7,6},{8,9},{9,8},{10,11... | collective-permute-start | bytes 417800 | tf_op jit(solution)/shard_map/ppermute | solution.py:34
  162.1 19.9 %collective-permute-start.14 = (bf16[272,256]{1,0:T(8,128)(2,1)S(1)}, bf16[272,256]{1,0:T(8,128)(2,1)S(1)}, u32[]{:S(2)}, u32[]{:S(2)}) collective-permute-start(bf16[272,256]{1,0:T(8,128)(2,1)S(1)} %get-tuple-element.84), channel_id=1, source_target_pairs={{0,2},{1,3},{2,0},{3,1},{4,6},{5,7},{6,4},{7,5},{8,10},{9,11},{10,... | collective-permute-start | bytes 417800 | tf_op jit(solution)/shard_map/ppermute | solution.py:34
  166.7 17.6 %collective-permute-start.15 = (bf16[272,256]{1,0:T(8,128)(2,1)S(1)}, bf16[272,256]{1,0:T(8,128)(2,1)S(1)}, u32[]{:S(2)}, u32[]{:S(2)}) collective-permute-start(bf16[272,256]{1,0:T(8,128)(2,1)S(1)} %get-tuple-element.85), channel_id=1, source_target_pairs={{0,3},{1,2},{2,1},{3,0},{4,7},{5,6},{6,5},{7,4},{8,11},{9,10},{10,... | collective-permute-start | bytes 417800 | tf_op jit(solution)/shard_map/ppermute | solution.py:34
  172.8 17.5 %collective-permute-start.52 = (bf16[2,128,256]{2,1,0:T(8,128)(2,1)S(1)}, bf16[2,128,256]{2,1,0:T(8,128)(2,1)S(1)}, u32[]{:S(2)}, u32[]{:S(2)}) collective-permute-start(bf16[2,128,256]{2,1,0:T(8,128)(2,1)S(1)} %get-tuple-element.132), channel_id=1, source_target_pairs={{0,2},{1,3},{2,0},{3,1},{4,6},{5,7},{6,4},{7,5},{8,10},{9,11},{10,... | collective-permute-start | bytes 393224 | tf_op jit(solution)/shard_map/ppermute | solution.py:34
  182.0 18.1 %collective-permute-start.42 = (bf16[2,128,256]{2,1,0:T(8,128)(2,1)S(1)}, bf16[2,128,256]{2,1,0:T(8,128)(2,1)S(1)}, u32[]{:S(2)}, u32[]{:S(2)}) collective-permute-start(bf16[2,128,256]{2,1,0:T(8,128)(2,1)S(1)} %get-tuple-element.120), channel_id=1, source_target_pairs={{0,2},{1,3},{2,0},{3,1},{4,6},{5,7},{6,4},{7,5},{8,10},{9,11},{10,... | collective-permute-start | bytes 393224 | tf_op jit(solution)/shard_map/ppermute | solution.py:34
  184.3 15.8 %collective-permute-start.43 = (bf16[2,128,256]{2,1,0:T(8,128)(2,1)S(1)}, bf16[2,128,256]{2,1,0:T(8,128)(2,1)S(1)}, u32[]{:S(2)}, u32[]{:S(2)}) collective-permute-start(bf16[2,128,256]{2,1,0:T(8,128)(2,1)S(1)} %get-tuple-element.121), channel_id=1, source_target_pairs={{0,3},{1,2},{2,1},{3,0},{4,7},{5,6},{6,5},{7,4},{8,11},{9,10},{10,... | collective-permute-start | bytes 393224 | tf_op jit(solution)/shard_map/ppermute | solution.py:34
  (31 other events, 376.6 us)
